TPU v7x, 256 devices: a whole 4x4x8 slice. The times are simulated.
256 devices in a mesh: dp: 16 (over y_lo, x, core), chan: 16 (over y_hi, z).
Axes of the slice: x: 4, y: 4 (y_hi: 2, y_lo: 2; y = y_hi * 2 + y_lo), z: 8, core: 2. Of those that a mesh axis runs over, the one named last changes fastest.
Arguments:
- anchors: bfloat16 [256, 128, 4096], P('dp', 'chan'), may hold values from -15 to 15
- views: bfloat16 [256, 128, 4096], P('dp', 'chan'), may hold values from -15 to 15
- dw_weight: float32 [128, 4], replicated, may hold values from -3 to 3
- pw_weight: bfloat16 [256, 128], replicated, may hold values from -0.5 to 0.5
- proj_weight: bfloat16 [256, 1024], replicated, may hold values from -0.375 to 0.375
- partner: int32 [256], P('dp'), may hold values from 0 to 255, each once
Outputs:
- loss: float32 [256], P('dp')
- grad_dw: float32 [128, 4], P('chan')
- grad_pw: float32 [256, 128], replicated
- grad_proj: float32 [256, 1024], P('chan', 'dp')
Inputs may be any that keep to these rules, and one draw needn't show every extreme that they name: `partner`: each view index appears exactly once.
All inputs are finite; a program needn't handle non-finite values.
Results may differ from a plain program's by a relative error of at most 0.0044.
Values may be sent and summed in bfloat16 or wider, within the bound.
No kernel may reach another device: no remote copies, remote signals or barrier semaphores. Data moves between devices by JAX's collectives and lax.ppermute only.
A program may use at most 192 MiB of HBM per device.

v0:
```python
import jax
import jax.numpy as jnp
from jax import lax
from jax.sharding import PartitionSpec as P

TAPS = 4
TAP_SPACING = 16


logit_scale = 16.0


def passed_along(value, axis, steps):
    count = lax.axis_size(axis)
    pairs = [(source, (source + steps) % count) for source in range(count)]
    return lax.ppermute(value, axis, pairs)


def depthwise(trace_block, dw_weight):
    widened = trace_block.astype(jnp.float32)
    length = trace_block.shape[2]
    running = jnp.zeros(widened.shape, jnp.float32)
    for tap_index in range(TAPS):
        offset_steps = tap_index * TAP_SPACING
        shifted = jnp.pad(
            widened[:, :, : length - offset_steps], ((0, 0), (0, 0), (offset_steps, 0))
        )
        running = running + dw_weight[None, :, tap_index, None] * shifted
    return running.astype(jnp.bfloat16)


def silu_slope(mixed):
    sigma = jax.nn.sigmoid(mixed)
    return sigma * (1.0 + mixed * (1.0 - sigma))


def kernel_terms(grad_conv, extended):
    rim_width = (TAPS - 1) * TAP_SPACING
    span_width = grad_conv.shape[2]
    columns = []
    for tap_index in range(TAPS):
        begin = rim_width - tap_index * TAP_SPACING
        window = extended[:, :, begin : begin + span_width]
        columns.append(
            jnp.einsum("nct,nct->c", grad_conv, window, preferred_element_type=jnp.float32)
        )
    return jnp.stack(columns, 1)


def block_scores(queries, key_rows, owner_index, partner, factor):
    logits = factor * lax.dot_general(
        queries, key_rows, (((1,), (1,)), ((), ())), preferred_element_type=jnp.float32
    )
    columns = owner_index * key_rows.shape[0] + jnp.arange(key_rows.shape[0], dtype=jnp.int32)
    matches = columns[None, :] == partner[:, None]
    return (logits, matches)


def body(anchors, views, dw_weight, pw_weight, proj_weight, partner):
    stacked = jnp.concatenate([anchors, views], 0)
    pair_count = anchors.shape[0]
    length = anchors.shape[2]
    chan_index = lax.axis_index("chan")
    chan_count = lax.axis_size("chan")
    cycle_index = lax.axis_index("dp")
    cycle_size = lax.axis_size("dp")
    rim_width = (TAPS - 1) * TAP_SPACING
    local_metrics = anchors.shape[1]
    local_kernel = lax.dynamic_slice_in_dim(dw_weight, chan_index * local_metrics, local_metrics, 0)
    conv_local = depthwise(stacked, local_kernel)
    conv_rows = lax.all_to_all(conv_local, "chan", split_axis=2, concat_axis=1, tiled=True)
    mixed = jnp.einsum("fc,nct->nft", pw_weight, conv_rows, preferred_element_type=jnp.float32)
    partial_pool = jnp.sum(jax.nn.silu(mixed), 2) / length
    conv_time, mixed, partial_pool = (conv_rows, mixed, partial_pool)
    pooled = lax.psum(partial_pool, "chan")
    pooled_bf = pooled.astype(jnp.bfloat16)
    embedding = jnp.dot(pooled_bf, proj_weight, preferred_element_type=jnp.float32)
    inverse = lax.rsqrt(jnp.mean(embedding * embedding, 1, keepdims=True) + 1e-06)
    unit_rows = embedding * inverse
    unit_bf = unit_rows.astype(jnp.bfloat16)
    queries = unit_bf[:pair_count]
    own_keys = unit_bf[pair_count:]
    factor = logit_scale / proj_weight.shape[1]

    def total_terms(key_rows, owner_index, totals, positive):
        logits, matches = block_scores(queries, key_rows, owner_index, partner, factor)
        totals = totals + jnp.sum(jnp.exp(logits - logit_scale), 1)
        positive = positive + jnp.sum(jnp.where(matches, logits, 0.0), 1)
        return (totals, positive)

    def first_turn(turn_index, loop_state):
        key_rows, totals, positive = loop_state
        owner_index = (cycle_index - turn_index) % cycle_size
        totals, positive = total_terms(key_rows, owner_index, totals, positive)
        key_rows = passed_along(key_rows, "dp", 1)
        return (key_rows, totals, positive)

    start_zero = jnp.zeros((pair_count,), jnp.float32)
    key_rows, totals, positive = lax.fori_loop(
        0, cycle_size - 1, first_turn, (own_keys, start_zero, start_zero)
    )
    totals, positive = total_terms(
        key_rows, (cycle_index - (cycle_size - 1)) % cycle_size, totals, positive
    )

    def grad_terms(key_rows, owner_index, carried, grad_query):
        logits, matches = block_scores(queries, key_rows, owner_index, partner, factor)
        coeffs = (
            jnp.exp(logits - logit_scale) / totals[:, None] - matches.astype(jnp.float32)
        ).astype(jnp.bfloat16)
        grad_query = grad_query + factor * jnp.dot(
            coeffs, key_rows, preferred_element_type=jnp.float32
        )
        carried = carried + factor * lax.dot_general(
            coeffs, queries, (((0,), (0,)), ((), ())), preferred_element_type=jnp.float32
        )
        return (carried, grad_query)

    def second_turn(turn_index, loop_state):
        key_rows, carried, grad_query = loop_state
        owner_index = (cycle_index - turn_index) % cycle_size
        carried, grad_query = grad_terms(key_rows, owner_index, carried, grad_query)
        key_rows = passed_along(key_rows, "dp", 1)
        carried = passed_along(carried, "dp", 1)
        return (key_rows, carried, grad_query)

    start_grads = jnp.zeros(own_keys.shape, jnp.float32)
    key_rows, carried, grad_query = lax.fori_loop(
        0, cycle_size - 1, second_turn, (own_keys, start_grads, start_grads)
    )
    carried, grad_query = grad_terms(
        key_rows, (cycle_index - (cycle_size - 1)) % cycle_size, carried, grad_query
    )
    grad_key = passed_along(carried, "dp", 1)
    losses = logit_scale + jnp.log(totals) - positive
    grad_unit = jnp.concatenate([grad_query, grad_key], 0)
    grad_embed = inverse * (
        grad_unit - unit_rows * jnp.mean(unit_rows * grad_unit, 1, keepdims=True)
    )
    grad_embed_bf = grad_embed.astype(jnp.bfloat16)
    filter_rows = proj_weight.shape[0] // chan_count
    pooled_rows = lax.dynamic_slice_in_dim(pooled_bf, chan_index * filter_rows, filter_rows, 1)
    proj_terms = lax.dot_general(
        pooled_rows, grad_embed_bf, (((0,), (0,)), ((), ())), preferred_element_type=jnp.float32
    )
    grad_proj = lax.psum_scatter(proj_terms, "dp", scatter_dimension=1, tiled=True)
    grad_pool = lax.dot_general(
        grad_embed_bf, proj_weight, (((1,), (1,)), ((), ())), preferred_element_type=jnp.float32
    )
    grad_mixed = (grad_pool[:, :, None] / length * silu_slope(mixed)).astype(jnp.bfloat16)
    mix_terms = jnp.einsum("nft,nct->fc", grad_mixed, conv_time, preferred_element_type=jnp.float32)
    grad_conv = jnp.einsum(
        "fc,nft->nct", pw_weight, grad_mixed, preferred_element_type=jnp.float32
    ).astype(jnp.bfloat16)
    grad_pw = lax.psum(mix_terms, ("dp", "chan"))
    grad_local = lax.all_to_all(grad_conv, "chan", split_axis=1, concat_axis=2, tiled=True)
    extended = jnp.pad(stacked, ((0, 0), (0, 0), (rim_width, 0)))
    kernel_part = kernel_terms(grad_local, extended)
    grad_dw = lax.psum(kernel_part, "dp")
    return (losses, grad_dw, grad_pw, grad_proj)


def solution(mesh):
    placed = (P("dp", "chan", None), P("dp", "chan", None), P(), P(), P(), P("dp"))
    return jax.shard_map(
        body,
        mesh=mesh,
        in_specs=placed,
        out_specs=(P("dp"), P("chan", None), P(), P("chan", "dp")),
        check_vma=False,
    )
```

profile of v0, /device:TPU:1, one launch (start us, length us, event | category | flops | bytes accessed | tf_op | source)
XLA Modules:
  0.0 708.3 jit_solution(9025586352325555345)
XLA Ops:
  8.0 1.4 constant_dynamic-update-slice_fusion.1
  9.4 1.3 constant_dynamic-update-slice_fusion
  10.7 7.9 %copy.34 = bf16[32,8,4096]{0,1,2:T(8,128)(2,1)} copy(bf16[32,8,4096]{2,1,0:T(8,128)(2,1)S(1)} %constant_dynamic-update-slice_fusion) | data formatting | bytes 4194304 | tf_op jit(solution)/shard_map/concatenate | solution.py:60
  18.6 10.5 %slice.49 = f32[32,8,4080]{0,1,2:T(8,128)} slice(bf16[32,8,4096]{0,1,2:T(8,128)(2,1)} %copy.34), slice={[0:32], [0:8], [0:4080]} | slice | bytes 8355840 | tf_op jit(solution)/shard_map/slice | solution.py:26
  29.1 1.5 copy-done.1
  30.5 6.0 slice.50
  36.5 6.0 slice.51
  42.5 23.1 %fusion.44 = bf16[4096,8,32]{2,1,0:T(8,128)(2,1)} fusion(f32[32,8,4048]{0,1,2:T(8,128)} %slice.51, f32[8]{0:T(128)S(1)} %get-tuple-element.488, f32[32,8,4064]{0,1,2:T(8,128)} %slice.50, f32[8]{0:T(128)S(1)} %get-tuple-element.489, f32[32,8,4080]{0,1,2:T(8,128)} %slice.49, f32[8]{0:T(128)S(1)} %get-tuple-element.490, bf16[32,8,4096]{0,1,2:T(8,128)(2,1)} %copy.34, ...), kind=kLoop, calls=%fused_computation.88 | loop fusion | flops 9437184 | bytes 16679040
  65.6 14.5 %reshape.59 = bf16[16,2,32768]{2,1,0:T(2,128)(2,1)} reshape(bf16[4096,8,32]{2,1,0:T(8,128)(2,1)} %fusion.44) | data formatting | bytes 4194304
  80.1 11.8 %all-to-all-start = ((bf16[16,2,32768]{2,1,0:T(2,128)(2,1)}), bf16[16,2,32768]{2,1,0:T(2,128)(2,1)}, u32[]{:S(2)}, u32[]{:S(2)}) async-start(bf16[16,2,32768]{2,1,0:T(2,128)(2,1)} %reshape.59), calls=%async_computation | async-start | bytes 4194304 | tf_op jit(solution)/shard_map/all_to_all | solution.py:71
  92.0 49.1 %all-to-all-done = bf16[16,2,32768]{2,1,0:T(2,128)(2,1)} async-done(((bf16[16,2,32768]{2,1,0:T(2,128)(2,1)}), bf16[16,2,32768]{2,1,0:T(2,128)(2,1)}, u32[]{:S(2)}, u32[]{:S(2)}) %all-to-all-start) | async-done | bytes 2097184 | tf_op jit(solution)/shard_map/all_to_all | solution.py:71
  141.1 12.9 %reshape.60 = bf16[4096,8,32]{2,1,0:T(8,128)(2,1)} reshape(bf16[16,2,32768]{2,1,0:T(2,128)(2,1)} %all-to-all-done) | data formatting | bytes 4194304
  154.0 10.5 %copy.36 = bf16[32,16,8,256]{3,2,1,0:T(8,128)(2,1)} copy(bf16[32,16,8,256]{0,2,3,1:T(8,128)(2,1)} %bitcast.123) | data formatting | bytes 4194304 | tf_op jit(solution)/shard_map/all_to_all | solution.py:71
  164.5 6.2 fusion.12
  170.7 60.5 %psum.21 = bf16[32,256]{1,0:T(8,128)(2,1)S(1)} all-reduce(f32[32,256]{1,0:T(8,128)S(1)} %broadcast_multiply_fusion), channel_id=1, replica_groups=mesh['dp'=16,'chan'=16] {'chan'}, use_global_device_ids=true, to_apply=%region_1.2 | all-reduce | flops 8192 | bytes 49152 | tf_op jit(solution)/shard_map/psum | solution.py:75
  231.6 93.3 %while.40 = (s32[]{:T(128)}, bf16[16,1024]{1,0:T(8,128)(2,1)S(1)}, f32[16]{0:T(128)S(1)}, f32[16]{0:T(128)S(1)}, bf16[16,1024]{1,0:T(8,128)(2,1)S(1)}, /*index=5...) while((s32[]{:T(128)}, bf16[16,1024]{1,0:T(8,128)(2,1)S(1)}, ...), condition=%wide.region_6.7_spmd.clone, body=%wide.region_3.6_spmd.clone.sunk | while | flops 525888 | bytes 263144 | solution.py:99
  231.6 17.3 %collective-permute-start = (bf16[16,1024]{1,0:T(8,128)(2,1)S(1)}, bf16[16,1024]{1,0:T(8,128)(2,1)S(1)}, u32[]{:S(2)}, u32[]{:S(2)}) collective-permute-start(bf16[16,1024]{1,0:T(8,128)(2,1)S(1)} %copy.83), channel_id=1, source_target_pairs={{0,16},{16,32},{32,48},{48,64},{64,80},{80,96},{96,112},{112,128},... | collective-permute-start | bytes 98312 | tf_op jit(solution)/shard_map/while/body/eval_jaxpr/ppermute | solution.py:16
  250.0 2.3 collective-permute-start
  252.5 1.5 collective-permute-done
  254.1 1.6 collective-permute-start
  255.8 3.7 collective-permute-done
  259.7 5.3 collective-permute-done
  265.1 5.3 collective-permute-done
  270.6 5.3 collective-permute-done
  276.0 5.3 collective-permute-done
  281.5 5.3 collective-permute-done
  287.0 5.3 collective-permute-done
  292.4 5.3 collective-permute-done
  297.9 5.3 collective-permute-done
  303.3 5.3 collective-permute-done
  308.8 5.3 collective-permute-done
  314.2 5.3 collective-permute-done
  319.7 5.3 collective-permute-done
  325.6 92.6 %while.41 = (s32[]{:T(128)}, bf16[16,1024]{1,0:T(8,128)(2,1)S(1)}, f32[16,1024]{1,0:T(8,128)S(1)}, f32[16,1024]{1,0:T(8,128)S(1)}, bf16[16,1024]{1,0:T(8,128)(2,...) while((s32[]{:T(128)}, bf16[16,1024]{1,0:T(8,128)(2,1)S(1)}, ...), condition=%wide.region_10.11_spmd.clone, body=%wide.region_9.10_spmd.clone.sunk | while | flops 1656608 | bytes 854104 | solution.py:128
  326.3 4.9 collective-permute-done.1
  332.2 5.2 collective-permute-done.1
  338.4 5.2 collective-permute-done.1
  344.5 5.2 collective-permute-done.1
  350.7 5.2 collective-permute-done.1
  356.9 5.2 collective-permute-done.1
  363.1 5.2 collective-permute-done.1
  369.3 5.2 collective-permute-done.1
  375.5 5.2 collective-permute-done.1
  381.7 5.2 collective-permute-done.1
  387.8 5.2 collective-permute-done.1
  394.0 5.2 collective-permute-done.1
  400.2 5.2 collective-permute-done.1
  406.4 5.2 collective-permute-done.1
  412.6 5.2 collective-permute-done.1
  418.9 5.6 collective-permute-done.3
  425.1 5.0 fusion.16
  430.2 1.9 copy-done.2
  432.1 2.6 convert_bitcast_fusion
  434.7 4.6 copy.39
  439.3 4.4 all-to-all-start.1
  443.8 1.1 convolution_bitcast_fusion
  445.0 4.8 fusion.25
  449.8 62.0 %reduce-scatter.4.cloned.1.call-done = f32[64,16]{1,0:T(8,128)} async-done(((f32[1024,16]{1,0:T(8,128)}), f32[64,16]{1,0:T(8,128)}) %reduce-scatter.4.cloned.1.call-update) | async-done | bytes 4112
  511.8 1.4 copy.76
  513.2 2.8 copy.40
  516.0 2.8 fusion.17
  518.8 30.5 %psum.22 = f32[8,4]{0,1:T(4,128)} all-reduce(f32[8,4]{0,1:T(4,128)S(1)} %pad_maximum_fusion.1), channel_id=1, replica_groups=mesh['dp'=16,'chan'=16] {'dp'}, use_global_device_ids=true, to_apply=%region_12.13 | all-reduce | flops 32 | bytes 256 | tf_op jit(solution)/shard_map/psum | solution.py:159
  549.3 150.0 %all-reduce.6.cloned.1.call-done = f32[256,128]{1,0:T(8,128)} async-done(((f32[256,128]{1,0:T(8,128)}), f32[256,128]{1,0:T(8,128)}) %all-reduce.6.cloned.1.call-update) | async-done | bytes 131088 | tf_op jit(solution)/shard_map/psum | solution.py:155
  699.3 1.6 copy.103
  (232 shorter events, 20.3 us)
Async XLA Ops:
  8.0 223.2 %copy-start = (bf16[256,1024]{1,0:T(8,128)(2,1)S(1)}, bf16[256,1024]{1,0:T(8,128)(2,1)}, u32[]{:S(2)}) copy-start(bf16[256,1024]{1,0:T(8,128)(2,1)} %param.14) | copy-start | bytes 1572868
  18.6 11.9 %copy-start.1 = (bf16[32,8,4096]{0,1,2:T(8,128)(2,1)S(1)}, bf16[32,8,4096]{0,1,2:T(8,128)(2,1)}, u32[]{:S(2)}) copy-start(bf16[32,8,4096]{0,1,2:T(8,128)(2,1)} %copy.34) | copy-start | bytes 6291460
  36.5 6.0 copy-start.4
  80.1 61.0 %all-to-all-start = ((bf16[16,2,32768]{2,1,0:T(2,128)(2,1)}), bf16[16,2,32768]{2,1,0:T(2,128)(2,1)}, u32[]{:S(2)}, u32[]{:S(2)}) async-start(bf16[16,2,32768]{2,1,0:T(2,128)(2,1)} %reshape.59), calls=%async_computation | async-start | bytes 4194304 | tf_op jit(solution)/shard_map/all_to_all | solution.py:71
  92.0 72.5 %copy-start.3 = (bf16[256,128]{1,0:T(8,128)(2,1)S(1)}, bf16[256,128]{1,0:T(8,128)(2,1)}, u32[]{:S(2)}) copy-start(bf16[256,128]{1,0:T(8,128)(2,1)} %param.13) | copy-start | bytes 196612
  164.5 67.1 %copy-start.5 = (s32[16]{0:T(128)S(1)}, s32[16]{0:T(128)}, u32[]{:S(2)}) copy-start(s32[16]{0:T(128)} %param.15) | copy-start | bytes 196
  231.6 18.4 %collective-permute-start = (bf16[16,1024]{1,0:T(8,128)(2,1)S(1)}, bf16[16,1024]{1,0:T(8,128)(2,1)S(1)}, u32[]{:S(2)}, u32[]{:S(2)}) collective-permute-start(bf16[16,1024]{1,0:T(8,128)(2,1)S(1)} %copy.83), channel_id=1, source_target_pairs={{0,16},{16,32},{32,48},{48,64},{64,80},{80,96},{96,112},{112,128},... | collective-permute-start | bytes 98312 | tf_op jit(solution)/shard_map/while/body/eval_jaxpr/ppermute | solution.py:16
  250.0 4.0 collective-permute-start
  254.1 5.4 collective-permute-start
  259.5 5.4 collective-permute-start
  265.0 5.4 collective-permute-start
  270.4 5.4 collective-permute-start
  275.9 5.4 collective-permute-start
  281.3 5.4 collective-permute-start
  286.8 5.4 collective-permute-start
  292.2 5.4 collective-permute-start
  297.7 5.4 collective-permute-start
  303.1 5.4 collective-permute-start
  308.6 5.4 collective-permute-start
  314.0 5.4 collective-permute-start
  319.5 5.4 collective-permute-start
  325.6 5.5 collective-permute-start.1
  326.1 5.6 collective-permute-start.2
  331.6 5.8 collective-permute-start.1
  332.0 5.9 collective-permute-start.2
  337.8 5.8 collective-permute-start.1
  338.1 5.9 collective-permute-start.2
  344.0 5.8 collective-permute-start.1
  344.3 5.9 collective-permute-start.2
  350.2 5.8 collective-permute-start.1
  350.5 5.9 collective-permute-start.2
  356.4 5.8 collective-permute-start.1
  356.7 5.9 collective-permute-start.2
  362.6 5.8 collective-permute-start.1
  362.9 5.9 collective-permute-start.2
  368.7 5.8 collective-permute-start.1
  369.1 5.9 collective-permute-start.2
  374.9 5.8 collective-permute-start.1
  375.2 5.9 collective-permute-start.2
  381.1 5.8 collective-permute-start.1
  381.4 5.9 collective-permute-start.2
  387.3 5.8 collective-permute-start.1
  387.6 5.9 collective-permute-start.2
  393.5 5.8 collective-permute-start.1
  393.8 5.9 collective-permute-start.2
  399.7 5.8 collective-permute-start.1
  400.0 5.9 collective-permute-start.2
  405.9 5.8 collective-permute-start.1
  406.2 5.9 collective-permute-start.2
  412.0 5.8 collective-permute-start.1
  412.4 5.9 collective-permute-start.2
  418.5 6.1 collective-permute-start.3
  430.2 1.9 copy-start.2
  439.3 73.9 %all-to-all-start.1 = ((bf16[32,128,256]{2,0,1:T(8,128)(2,1)}), bf16[32,128,256]{2,0,1:T(8,128)(2,1)}, u32[]{:S(2)}, u32[]{:S(2)}) async-start(bf16[32,128,256]{2,0,1:T(8,128)(2,1)} %copy.39), calls=%async_computation.1 | async-start | bytes 4194304 | tf_op jit(solution)/shard_map/all_to_all | solution.py:156
  443.7 68.1 %reduce-scatter.4.cloned.1.call-start = ((), (), s32[]{:S(2)}) async-start(), calls=%async_computation.4 | async-start | bytes 557056
  444.9 254.4 %all-reduce.6.cloned.1.call-start = ((), (), s32[]{:S(2)}) async-start(), calls=%async_computation.3 | async-start | bytes 262144 | tf_op jit(solution)/shard_map/psum | solution.py:155
Sparse Core Ops, SparseCore 0:
  447.1 64.6 reduce-scatter.3
Sparse Core Ops, SparseCore 1:
  451.5 247.8 all-reduce.5
where the time goes:
time: 710 us; the launch traced here: 708 us
  waiting for transfers between devices  420 us (59%)
  blocking collectives  90.9 us (13%)
  local copies, waits for them, and re-layouts  84.8 us (12%)
  starting transfers between devices  38.9 us (5%)
  other arithmetic  32.1 us (5%)
  matrix products  24.8 us (3%)
  between operations  15.7 us (2%)
    ppermute x46, waiting for transfers between devices, passed_along(): return lax.ppermute(value, axis, pairs)  159 us
    psum x1, waiting for transfers between devices, body(): grad_pw = lax.psum(mix_terms, ('dp', 'chan'))  150 us
    unnamed x3, waiting for transfers between devices  62 us
    psum x1, blocking collectives, body(): pooled = lax.psum(partial_pool, 'chan')  60.5 us
    all_to_all x1, waiting for transfers between devices, body(): lax.all_to_all(conv_local, 'chan', split_axis=2, concat_axis=1, tiled=True)  49.1 us
    unnamed x18, local copies, waits for them, and re-layouts  35.1 us
    psum x1, blocking collectives, body(): grad_dw = lax.psum(kernel_part, 'dp')  30.5 us
    unnamed x4, other arithmetic  23.1 us
  transfers between devices with their start and end apart: 50, of which 49 were waited for; matrix products, arithmetic and copies ran while one was open for 3% of the time, Pallas kernels for 0%

commit v1 on v0

v1 whole, which is shorter than its diff:
```python
import functools

import jax
import jax.numpy as jnp
from jax import lax
from jax.experimental import pallas as pl
from jax.experimental.pallas import tpu as pltpu
from jax.sharding import PartitionSpec as P

TAPS = 4
TAP_SPACING = 16
LANES = 128
LOGIT_SCALE = 16.0
CHUNK = 1024
ROWS = 32
F32 = jnp.float32
BF16 = jnp.bfloat16


def trace_kernel(length, x_ref, halo_ref, dw_ref, pw_ref, pool_ref, terms_ref, mixed, slope, taps, acc):
    step = pl.program_id(0)
    metrics, chunk = x_ref.shape
    filters = pw_ref.shape[0]

    @pl.when(step == 0)
    def _():
        acc[...] = jnp.zeros_like(acc)
        terms_ref[...] = jnp.zeros_like(terms_ref)

    for begin in range(0, metrics, ROWS):
        rows = pl.ds(begin, ROWS)
        block = x_ref[rows, :].astype(F32)
        halo = halo_ref[rows, :].astype(F32)
        halo = jnp.where(step > 0, halo, jnp.zeros_like(halo))
        extended = jnp.concatenate([halo, block], axis=1)
        kernel = dw_ref[rows, :]
        running = kernel[:, 0:1] * block
        taps[pl.ds(metrics + begin, ROWS), :] = x_ref[rows, :]
        for tap in range(1, TAPS):
            shifted = pltpu.roll(extended, tap * TAP_SPACING, 1)[:, LANES:]
            running = running + kernel[:, tap : tap + 1] * shifted
            taps[pl.ds(metrics * (tap + 1) + begin, ROWS), :] = shifted.astype(BF16)
        taps[rows, :] = running.astype(BF16)

    mixed[...] = jnp.dot(pw_ref[...], taps[pl.ds(0, metrics), :], preferred_element_type=F32)

    def activate(index, carry):
        rows = pl.ds(pl.multiple_of(index * ROWS, ROWS), ROWS)
        value = mixed[rows, :]
        sigma = jax.nn.sigmoid(value)
        silu = value * sigma
        slope[rows, :] = (sigma + silu * (1.0 - sigma)).astype(BF16)
        total = silu[:, 0:LANES]
        for lane in range(LANES, chunk, LANES):
            total = total + silu[:, lane : lane + LANES]
        acc[rows, :] = acc[rows, :] + total
        return carry

    lax.fori_loop(0, filters // ROWS, activate, 0)
    terms_ref[...] += lax.dot_general(
        taps[...], slope[...], (((1,), (1,)), ((), ())), preferred_element_type=F32
    )

    @pl.when(step == pl.num_programs(0) - 1)
    def _():
        turned = acc[...].T
        pool_ref[...] = jnp.sum(turned, 0, keepdims=True) / length


def trace_pass(trace, dw_weight, pw_weight):
    metrics, length = trace.shape
    filters = pw_weight.shape[0]
    chunk = CHUNK
    per_halo = chunk // LANES
    return pl.pallas_call(
        functools.partial(trace_kernel, length),
        grid=(length // chunk,),
        in_specs=[
            pl.BlockSpec((metrics, chunk), lambda i: (0, i)),
            pl.BlockSpec((metrics, LANES), lambda i: (0, jnp.maximum(i * per_halo - 1, 0))),
            pl.BlockSpec((metrics, TAPS), lambda i: (0, 0)),
            pl.BlockSpec((filters, metrics), lambda i: (0, 0)),
        ],
        out_specs=[
            pl.BlockSpec((1, filters), lambda i: (0, 0)),
            pl.BlockSpec((metrics * (TAPS + 1), filters), lambda i: (0, 0)),
        ],
        out_shape=[
            jax.ShapeDtypeStruct((1, filters), F32),
            jax.ShapeDtypeStruct((metrics * (TAPS + 1), filters), F32),
        ],
        scratch_shapes=[
            pltpu.VMEM((filters, chunk), F32),
            pltpu.VMEM((filters, chunk), BF16),
            pltpu.VMEM((metrics * (TAPS + 1), chunk), BF16),
            pltpu.VMEM((filters, LANES), F32),
        ],
        compiler_params=pltpu.CompilerParams(
            dimension_semantics=("arbitrary",), vmem_limit_bytes=40 << 20
        ),
    )(trace, trace, dw_weight, pw_weight)


def middle_kernel(
    length, own_ref, pooled_ref, proj_ref, pw_turned_ref, terms_a_ref, terms_v_ref,
    loss_ref, grad_a_ref, grad_v_ref, sums_ref, held_a, held_v,
):
    filters, width = proj_ref.shape
    count = pooled_ref.shape[0]
    metrics = pw_turned_ref.shape[0]
    factor = LOGIT_SCALE / width
    proj = proj_ref[...]

    def normed(pooled):
        embedding = jnp.dot(pooled, proj, preferred_element_type=F32)
        inverse = lax.rsqrt(jnp.mean(embedding * embedding, 1, keepdims=True) + 1e-06)
        return embedding * inverse, inverse

    unit_a, inverse_a = normed(pooled_ref[:, 0:filters])
    unit_v, inverse_v = normed(pooled_ref[:, filters : 2 * filters])
    queries = unit_a.astype(BF16)
    keys = unit_v.astype(BF16)
    logits = factor * lax.dot_general(
        queries, keys, (((1,), (1,)), ((), ())), preferred_element_type=F32
    )
    partner = pooled_ref[:, 2 * filters : 2 * filters + 1].astype(F32).astype(jnp.int32)
    columns = lax.broadcasted_iota(jnp.int32, (count, count), 1)
    matches = columns == partner
    weights = jnp.exp(logits - LOGIT_SCALE)
    totals = jnp.sum(weights, 1, keepdims=True)
    positive = jnp.sum(jnp.where(matches, logits, 0.0), 1, keepdims=True)
    loss_ref[...] = LOGIT_SCALE + jnp.log(totals) - positive
    coeffs = (weights / totals - jnp.where(matches, 1.0, 0.0)).astype(BF16)
    unit_grad_a = factor * jnp.dot(coeffs, keys, preferred_element_type=F32)
    unit_grad_v = factor * lax.dot_general(
        coeffs, queries, (((0,), (0,)), ((), ())), preferred_element_type=F32
    )

    def embed_grad(unit, inverse, unit_grad):
        return inverse * (unit_grad - unit * jnp.mean(unit * unit_grad, 1, keepdims=True))

    own = own_ref[0]

    def pool_grad(unit, inverse, unit_grad, out_ref, held):
        grad = embed_grad(unit, inverse, unit_grad).astype(BF16)
        out_ref[...] = grad
        held[...] = grad.astype(F32)
        row = jnp.broadcast_to(held[pl.ds(own, 1), :], (16, width)).astype(BF16)
        pool = lax.dot_general(row, proj, (((1,), (1,)), ((), ())), preferred_element_type=F32)
        return pool[0:1, :] / length

    pool_a = pool_grad(unit_a, inverse_a, unit_grad_a, grad_a_ref, held_a)
    pool_v = pool_grad(unit_v, inverse_v, unit_grad_v, grad_v_ref, held_v)

    def weighted(index):
        rows = pl.ds(index * metrics, metrics)
        return terms_a_ref[rows, :] * pool_a + terms_v_ref[rows, :] * pool_v

    mixing = weighted(0).T
    pw_turned = pw_turned_ref[...].astype(F32)
    lanes = lax.broadcasted_iota(jnp.int32, (metrics, LANES), 1)
    kernel = jnp.zeros((metrics, LANES), F32)
    for tap in range(TAPS):
        column = jnp.sum(pw_turned * weighted(tap + 1), 1, keepdims=True)
        kernel = kernel + jnp.where(lanes == tap, column, 0.0)
    parts = sums_ref.shape[0]
    mix_rows, tap_rows = filters // parts, metrics // parts
    for part in range(parts):
        sums_ref[part, 0:mix_rows, :] = mixing[part * mix_rows : (part + 1) * mix_rows, :]
        sums_ref[part, mix_rows : mix_rows + tap_rows, :] = kernel[
            part * tap_rows : (part + 1) * tap_rows, :
        ]


def middle(own, pooled, proj_weight, pw_turned, terms_a, terms_v, parts, length):
    filters, width = proj_weight.shape
    metrics = pw_turned.shape[0]
    count = pooled.shape[0]
    whole = pl.BlockSpec(memory_space=pltpu.VMEM)
    rows = filters // parts + metrics // parts
    return pl.pallas_call(
        functools.partial(middle_kernel, length),
        in_specs=[pl.BlockSpec(memory_space=pltpu.SMEM)] + [whole] * 5,
        out_specs=[whole] * 4,
        out_shape=[
            jax.ShapeDtypeStruct((count, 1), F32),
            jax.ShapeDtypeStruct((count, width), BF16),
            jax.ShapeDtypeStruct((count, width), BF16),
            jax.ShapeDtypeStruct((parts, rows, metrics), F32),
        ],
        scratch_shapes=[pltpu.VMEM((count, width), F32), pltpu.VMEM((count, width), F32)],
        compiler_params=pltpu.CompilerParams(vmem_limit_bytes=48 << 20),
    )(own, pooled, proj_weight, pw_turned, terms_a, terms_v)


def swap(value, axis):
    return lax.all_to_all(value, axis, 0, 0, tiled=True)


def spread(value, axis):
    count = lax.axis_size(axis)
    return swap(jnp.broadcast_to(value[None], (count,) + value.shape), axis)


def body(anchors, views, dw_weight, pw_weight, proj_weight, partner):
    chan_index = lax.axis_index("chan")
    dp_index = lax.axis_index("dp")
    chan_count = lax.axis_size("chan")
    dp_count = lax.axis_size("dp")
    pairs, local_metrics, length = anchors.shape
    filters, metrics = pw_weight.shape
    width = proj_weight.shape[1]

    trace_a = swap(anchors, "chan").reshape(metrics, length)
    trace_v = swap(views, "chan").reshape(metrics, length)
    pool_a, terms_a = trace_pass(trace_a, dw_weight, pw_weight)
    pool_v, terms_v = trace_pass(trace_v, dw_weight, pw_weight)
    own_partner = lax.dynamic_slice_in_dim(partner, chan_index, 1, 0).astype(BF16)
    message = jnp.concatenate(
        [pool_a.astype(BF16), pool_v.astype(BF16), jnp.broadcast_to(own_partner[None], (1, LANES))], 1
    )
    pooled = spread(message, ("dp", "chan")).reshape(dp_count * chan_count, message.shape[1])

    own = (dp_index * chan_count + chan_index).astype(jnp.int32).reshape(1)
    losses, grad_a, grad_v, sums = middle(
        own, pooled, proj_weight, pw_weight.T, terms_a, terms_v, chan_count, length
    )

    summed = jnp.sum(swap(sums, "chan"), 0)
    summed = jnp.sum(spread(summed, "dp"), 0)
    mix_rows = filters // chan_count
    grad_dw = summed[mix_rows:, :TAPS]
    grad_pw = spread(summed[:mix_rows], "chan").reshape(filters, metrics)

    cols = width // dp_count
    rows = filters // chan_count

    def proj_part(offset, grad):
        features = lax.dynamic_slice_in_dim(pooled, offset + chan_index * rows, rows, 1)
        part = lax.dynamic_slice_in_dim(grad, dp_index * cols, cols, 1)
        return lax.dot_general(
            features, part, (((0,), (0,)), ((), ())), preferred_element_type=F32
        )

    grad_proj = proj_part(0, grad_a) + proj_part(filters, grad_v)
    loss = lax.dynamic_slice_in_dim(losses, dp_index * pairs, pairs, 0).reshape(pairs)
    return (loss, grad_dw, grad_pw, grad_proj)


def solution(mesh):
    placed = (P("dp", "chan", None), P("dp", "chan", None), P(), P(), P(), P("dp"))
    return jax.shard_map(
        body,
        mesh=mesh,
        in_specs=placed,
        out_specs=(P("dp"), P("chan", None), P(), P("chan", "dp")),
        check_vma=False,
    )
```

time: 710 us -> 156 us (0.22)
  waiting for transfers between devices: 420 us -> 48.5 us
  local copies, waits for them, and re-layouts: 84.8 us -> 8.17 us
  blocking collectives: 90.9 us -> 50 us
  other arithmetic: 32.1 us -> 2.68 us
  matrix products: 24.8 us -> 1.02 us
  Pallas kernels: 0 us -> 16.3 us
  between operations: 15.7 us -> 1.48 us
  starting transfers between devices: 38.9 us -> 27 us
    ppermute x46 -> x0, waiting for transfers between devices: 159 us -> none  [passed_along(): return lax.ppermute(value, axis, pairs)]
    psum x1 -> x0, waiting for transfers between devices: 150 us -> none  [body(): grad_pw = lax.psum(mix_terms, ('dp', 'chan'))]
    psum x2 -> x0, blocking collectives: 90.9 us -> none  [the longest x1 60.5 us: body(): pooled = lax.psum(partial_pool, 'chan')]
    unnamed x3 -> x0, waiting for transfers between devices: 62 us -> none
    all_to_all x0 -> x2, blocking collectives: none -> 50 us  [swap(): return lax.all_to_all(value, axis, 0, 0, tiled=True)]
    unnamed x18 -> x17, local copies, waits for them, and re-layouts: 35.1 us -> 4.37 us
    unnamed x4 -> x0, other arithmetic: 23.1 us -> none
    dot_general x69 -> x2, matrix products: 23.7 us -> 1.02 us  [proj_part(): lax.dot_general(features, part, (((0,), (0,)), ((), ())), preferred_eleme...]
  transfers between devices with their start and end apart: 50 -> 4, of which waited for: 49 -> 4; matrix products, arithmetic and copies ran while one was open for 3% -> 2% of each run, Pallas kernels for 0% -> 4%
where the time goes in v1:
time: 156 us; the launch traced here: 155 us
  blocking collectives  50 us (32%)
  waiting for transfers between devices  48.5 us (31%)
  starting transfers between devices  27 us (17%)
  Pallas kernels  16.3 us (10%)
  local copies, waits for them, and re-layouts  8.17 us (5%)
  other arithmetic  2.68 us (2%)
    all_to_all x2, blocking collectives, swap(): return lax.all_to_all(value, axis, 0, 0, tiled=True)  50 us
    all_to_all x4, waiting for transfers between devices, swap(): return lax.all_to_all(value, axis, 0, 0, tiled=True)  48.5 us
    all_to_all x4, starting transfers between devices, swap(): return lax.all_to_all(value, axis, 0, 0, tiled=True)  27 us
    pallas_call x2, Pallas kernels, trace_pass(): pl.pallas_call(functools.partial(trace_kernel, length), grid=(length // c...  13.8 us
    unnamed x17, local copies, waits for them, and re-layouts  4.37 us
  transfers between devices with their start and end apart: 4, of which 4 were waited for; matrix products, arithmetic and copies ran while one was open for 2% of the time, Pallas kernels for 4%

profile of v1, /device:TPU:1, one launch (start us, length us, event | category | flops | bytes accessed | tf_op | source)
XLA Modules:
  0.0 155.2 jit_solution(6427965529602063002)
XLA Ops:
  0.6 38.2 %all_to_all.30 = bf16[16,8,4096]{2,1,0:T(8,128)(2,1)S(1)} all-to-all(bf16[16,8,4096]{2,1,0:T(8,128)(2,1)} %param.7), channel_id=1, replica_groups=mesh['dp'=16,'chan'=16] {'chan'}, dimensions={0} | all-to-all | bytes 2097152 | tf_op jit(solution)/shard_map/all_to_all | solution.py:197
  38.9 0.0 copy-start.3
  38.9 0.0 copy-start.2
  38.9 6.1 %all-to-all-start = ((bf16[16,8,4096]{2,1,0:T(8,128)(2,1)}), bf16[16,8,4096]{2,1,0:T(8,128)(2,1)S(1)}, u32[]{:S(2)}, u32[]{:S(2)}) async-start(bf16[16,8,4096]{2,1,0:T(8,128)(2,1)} %param.6), calls=%async_computation | async-start | bytes 2097152 | tf_op jit(solution)/shard_map/all_to_all | solution.py:197
  45.0 0.0 copy-start
  45.0 0.0 copy-done.3
  45.0 0.6 dynamic_slice.22
  46.3 0.0 copy-done.2
  46.3 0.1 copy.28.dw_ref
  46.4 0.0 copy-done
  46.4 6.9 %shard_map.94 = (f32[1,256]{1,0:T(1,128)S(1)}, f32[640,256]{1,0:T(8,128)S(1)}) custom-call(bf16[128,4096]{1,0:T(8,128)(2,1)S(1)} %bitcast.17, bf16[128,4096]{1,0:T(8,128)(2,1)S(1)} %bitcast.18, f32[128,4]{1,0:T(8,128)S(1)} %copy.28.dw_ref, bf16[256,128]{1,0:T(8,128)(2,1)S(1)} %copy-done), custom_call_target="tpu_custom_call" | custom-call | tf_op jit(solution)/shard_map/pallas_call | solution.py:75
  53.3 17.4 %all-to-all-done = bf16[16,8,4096]{2,1,0:T(8,128)(2,1)S(1)} async-done(((bf16[16,8,4096]{2,1,0:T(8,128)(2,1)}), bf16[16,8,4096]{2,1,0:T(8,128)(2,1)S(1)}, u32[]{:S(2)}, u32[]{:S(2)}) %all-to-all-start) | async-done | bytes 1048608 | tf_op jit(solution)/shard_map/all_to_all | solution.py:197
  70.8 6.9 %shard_map.93 = (f32[1,256]{1,0:T(1,128)S(1)}, f32[640,256]{1,0:T(8,128)S(1)}) custom-call(bf16[128,4096]{1,0:T(8,128)(2,1)S(1)} %bitcast.15, bf16[128,4096]{1,0:T(8,128)(2,1)S(1)} %bitcast.16, f32[128,4]{1,0:T(8,128)S(1)} %copy.28.dw_ref, bf16[256,128]{1,0:T(8,128)(2,1)S(1)} %copy-done), custom_call_target="tpu_custom_call" | custom-call | tf_op jit(solution)/shard_map/pallas_call | solution.py:75
  77.7 0.3 broadcast_in_dim.15
  78.0 0.5 broadcast.7
  78.5 2.6 %reduce.4 = bf16[256,640]{1,0:T(8,128)(2,1)S(1)} reduce(bf16[256,1,640]{2,1,0:T(2,128)(2,1)S(1)} %broadcast_in_dim.15, bf16[]{:T(256)} %broadcast.7), dimensions={1}, to_apply=%broadcast_in_dim.15.reduce_sub_computation | reduce | bytes 655362 | tf_op jit(solution)/shard_map/broadcast_in_dim | solution.py:202
  81.2 1.1 reshape.48
  82.2 11.1 %all-to-all-start.2 = ((bf16[256,2,320]{2,1,0:T(2,128)(2,1)}), bf16[256,2,320]{2,1,0:T(2,128)(2,1)S(1)}, u32[]{:S(2)}, u32[]{:S(2)}) async-start(bf16[256,2,320]{2,1,0:T(2,128)(2,1)} %reshape.48), calls=%async_computation.2 | async-start | bytes 786432 | tf_op jit(solution)/shard_map/all_to_all | solution.py:197
  93.4 0.1 copy.30
  93.5 18.3 %all-to-all-done.2 = bf16[256,2,320]{2,1,0:T(2,128)(2,1)S(1)} async-done(((bf16[256,2,320]{2,1,0:T(2,128)(2,1)}), bf16[256,2,320]{2,1,0:T(2,128)(2,1)S(1)}, u32[]{:S(2)}, u32[]{:S(2)}) %all-to-all-start.2) | async-done | bytes 327712 | tf_op jit(solution)/shard_map/all_to_all | solution.py:197
  111.8 0.6 reshape.49
  112.4 0.0 copy-start.1
  112.4 1.0 copy-done.1
  113.4 2.5 %shard_map.95 = (f32[256,1]{1,0:T(8,128)S(1)}, bf16[256,1024]{1,0:T(8,128)(2,1)S(1)}, bf16[256,1024]{1,0:T(8,128)(2,1)S(1)}, f32[16,24,128]{2,1,0:T(8,128)S(1)}) custom-call(s32[1]{0:T(128)} %bitcast.own_ref, bf16[256,640]{1,0:T(8,128)(2,1)S(1)} %bitcast.19, bf16[256,1024]{1,0:T(8,128)(2,1)S(1)} %copy-done.1, bf16[128,256]{1,0:T(8,128)(2,1)S(1)} %bitcast.20, ...), custom_call_target="tpu_custom_call" | custom-call | tf_op jit(solution)/shard_map/pallas_call | solution.py:181
  115.9 11.8 %all_to_all.31 = f32[16,24,128]{2,1,0:T(8,128)S(1)} all-to-all(f32[16,24,128]{2,1,0:T(8,128)S(1)} %get-tuple-element.17), channel_id=1, replica_groups=mesh['dp'=16,'chan'=16] {'chan'}, dimensions={0} | all-to-all | bytes 393216 | tf_op jit(solution)/shard_map/all_to_all | solution.py:197
  127.8 0.7 broadcast_in_dim.32
  128.4 5.6 %all-to-all-start.4 = ((f32[16,24,128]{2,1,0:T(8,128)}), f32[16,24,128]{2,1,0:T(8,128)S(1)}, u32[]{:S(2)}, u32[]{:S(2)}) async-start(f32[16,24,128]{2,1,0:T(8,128)} %broadcast_in_dim.32), calls=%async_computation.4 | async-start | bytes 393216 | tf_op jit(solution)/shard_map/all_to_all | solution.py:197
  134.0 0.4 constant_dynamic-slice_fusion
  134.4 0.1 copy.35
  134.4 6.3 %all-to-all-done.4 = f32[16,24,128]{2,1,0:T(8,128)S(1)} async-done(((f32[16,24,128]{2,1,0:T(8,128)}), f32[16,24,128]{2,1,0:T(8,128)S(1)}, u32[]{:S(2)}, u32[]{:S(2)}) %all-to-all-start.4) | async-done | bytes 196640 | tf_op jit(solution)/shard_map/all_to_all | solution.py:197
  140.8 0.7 broadcast_in_dim.33
  141.4 4.2 %all-to-all-start.5 = ((f32[16,16,128]{2,1,0:T(8,128)}), f32[16,16,128]{2,1,0:T(8,128)S(1)}, u32[]{:S(2)}, u32[]{:S(2)}) async-start(f32[16,16,128]{2,1,0:T(8,128)} %broadcast_in_dim.33), calls=%async_computation.5 | async-start | bytes 262144 | tf_op jit(solution)/shard_map/all_to_all | solution.py:197
  145.6 0.2 fusion.1
  145.8 0.1 copy.36
  145.9 0.6 dynamic-slice_reduce_fusion
  146.5 0.8 convolution_add_fusion
  147.4 0.7 copy.33
  148.0 6.5 %all-to-all-done.5 = f32[16,16,128]{2,1,0:T(8,128)S(1)} async-done(((f32[16,16,128]{2,1,0:T(8,128)}), f32[16,16,128]{2,1,0:T(8,128)S(1)}, u32[]{:S(2)}, u32[]{:S(2)}) %all-to-all-start.5) | async-done | bytes 131104 | tf_op jit(solution)/shard_map/all_to_all | solution.py:197
  154.5 0.7 copy.40
  (10 shorter events, 0.1 us)
Async XLA Ops:
  38.9 6.1 %copy-start.3 = (s32[16]{0:T(128)S(1)}, s32[16]{0:T(128)}, u32[]{:S(2)}) copy-start(s32[16]{0:T(128)} %param.11) | copy-start | bytes 196
  38.9 7.4 %copy-start.2 = (f32[128,4]{0,1:T(4,128)S(1)}, f32[128,4]{0,1:T(4,128)}, u32[]{:S(2)}) copy-start(f32[128,4]{0,1:T(4,128)} %param.8) | copy-start | bytes 6148
  38.9 31.9 %all-to-all-start = ((bf16[16,8,4096]{2,1,0:T(8,128)(2,1)}), bf16[16,8,4096]{2,1,0:T(8,128)(2,1)S(1)}, u32[]{:S(2)}, u32[]{:S(2)}) async-start(bf16[16,8,4096]{2,1,0:T(8,128)(2,1)} %param.6), calls=%async_computation | async-start | bytes 2097152 | tf_op jit(solution)/shard_map/all_to_all | solution.py:197
  45.0 1.4 copy-start
  82.2 29.5 %all-to-all-start.2 = ((bf16[256,2,320]{2,1,0:T(2,128)(2,1)}), bf16[256,2,320]{2,1,0:T(2,128)(2,1)S(1)}, u32[]{:S(2)}, u32[]{:S(2)}) async-start(bf16[256,2,320]{2,1,0:T(2,128)(2,1)} %reshape.48), calls=%async_computation.2 | async-start | bytes 786432 | tf_op jit(solution)/shard_map/all_to_all | solution.py:197
  112.4 1.0 copy-start.1
  128.4 12.3 %all-to-all-start.4 = ((f32[16,24,128]{2,1,0:T(8,128)}), f32[16,24,128]{2,1,0:T(8,128)S(1)}, u32[]{:S(2)}, u32[]{:S(2)}) async-start(f32[16,24,128]{2,1,0:T(8,128)} %broadcast_in_dim.32), calls=%async_computation.4 | async-start | bytes 393216 | tf_op jit(solution)/shard_map/all_to_all | solution.py:197
  141.4 13.1 %all-to-all-start.5 = ((f32[16,16,128]{2,1,0:T(8,128)}), f32[16,16,128]{2,1,0:T(8,128)S(1)}, u32[]{:S(2)}, u32[]{:S(2)}) async-start(f32[16,16,128]{2,1,0:T(8,128)} %broadcast_in_dim.33), calls=%async_computation.5 | async-start | bytes 262144 | tf_op jit(solution)/shard_map/all_to_all | solution.py:197

commit v2 on v1

v2 whole, which is shorter than its diff:
```python
import functools

import jax
import jax.numpy as jnp
from jax import lax
from jax.experimental import pallas as pl
from jax.experimental.pallas import tpu as pltpu
from jax.sharding import PartitionSpec as P

TAPS = 4
TAP_SPACING = 16
LANES = 128
LOGIT_SCALE = 16.0
POOL_CHUNK = 1024
TERM_CHUNK = 1024
ROWS = 32
F32 = jnp.float32
BF16 = jnp.bfloat16


def convolved(x_ref, halo_ref, dw_ref, begin, step, keep=None):
    sources = ROWS // x_ref.shape[2]
    first = begin // x_ref.shape[2]
    block = x_ref[first : first + sources, 0].astype(F32).reshape(ROWS, x_ref.shape[3])
    halo = halo_ref[first : first + sources, 0].astype(F32).reshape(ROWS, LANES)
    halo = jnp.where(step > 0, halo, jnp.zeros_like(halo))
    extended = jnp.concatenate([halo, block], axis=1)
    kernel = dw_ref[begin : begin + ROWS, :]
    running = kernel[:, 0:1] * block
    if keep is not None:
        keep(0, block)
    for tap in range(1, TAPS):
        shifted = pltpu.roll(extended, tap * TAP_SPACING, 1)[:, LANES:]
        running = running + kernel[:, tap : tap + 1] * shifted
        if keep is not None:
            keep(tap, shifted)
    return running.astype(BF16)


def pool_kernel(length, own_ref, x_ref, halo_ref, dw_ref, pw_ref, message_ref, conv, half, acc, rows_held):
    trace, step = pl.program_id(0), pl.program_id(1)
    metrics = dw_ref.shape[0]
    filters, chunk = half.shape

    @pl.when(step == 0)
    def _():
        acc[...] = jnp.zeros_like(acc)

    for begin in range(0, metrics, ROWS):
        conv[pl.ds(begin, ROWS), :] = convolved(x_ref, halo_ref, dw_ref, begin, step)
    half[...] = jnp.dot(pw_ref[...] * 0.5, conv[...], preferred_element_type=F32)

    def activate(index, carry):
        rows = pl.ds(pl.multiple_of(index * ROWS, ROWS), ROWS)
        value = half[rows, :]
        silu = value + value * jnp.tanh(value)
        total = silu[:, 0:LANES]
        for lane in range(LANES, chunk, LANES):
            total = total + silu[:, lane : lane + LANES]
        acc[rows, :] = acc[rows, :] + total
        return carry

    lax.fori_loop(0, filters // ROWS, activate, 0)

    @pl.when(step == pl.num_programs(1) - 1)
    def _():
        pooled = jnp.sum(acc[...].T, 0, keepdims=True) / length
        rows_held[pl.ds(trace, 1), :] = pooled

    @pl.when((step == pl.num_programs(1) - 1) & (trace == pl.num_programs(0) - 1))
    def _():
        mark = jnp.full((2, LANES), own_ref[1], jnp.int32).astype(F32)
        row = jnp.concatenate([rows_held[0:2, :], mark], 1).astype(BF16)
        message_ref[...] = jnp.broadcast_to(row[None], message_ref.shape)


def terms_kernel(x_ref, halo_ref, dw_ref, pw_ref, proj_ref, terms_ref, proj_out_ref, half, slope, taps):
    trace, step = pl.program_id(0), pl.program_id(1)
    metrics = dw_ref.shape[0]
    filters, chunk = half.shape

    @pl.when(step == 0)
    def _():
        terms_ref[...] = jnp.zeros_like(terms_ref)

    @pl.when((step == 0) & (trace == 0))
    def _():
        proj_out_ref[...] = proj_ref[...]

    for begin in range(0, metrics, ROWS):

        def keep(tap, shifted):
            taps[pl.ds(metrics * (tap + 1) + begin, ROWS), :] = shifted.astype(BF16)

        taps[pl.ds(begin, ROWS), :] = convolved(x_ref, halo_ref, dw_ref, begin, step, keep)
    half[...] = jnp.dot(pw_ref[...] * 0.5, taps[0:metrics, :], preferred_element_type=F32)

    def activate(index, carry):
        rows = pl.ds(pl.multiple_of(index * ROWS, ROWS), ROWS)
        value = half[rows, :]
        turn = jnp.tanh(value)
        slope[rows, :] = ((1.0 + turn) * (1.0 + value * (1.0 - turn))).astype(BF16)
        return carry

    lax.fori_loop(0, filters // ROWS, activate, 0)
    terms_ref[0] += lax.dot_general(
        taps[...], slope[...], (((1,), (1,)), ((), ())), preferred_element_type=F32
    )


def trace_specs(traces, filters, chunk):
    sources, pair, local, length = traces.shape
    per_halo = chunk // LANES
    return [
        pl.BlockSpec((sources, 1, local, chunk), lambda n, i: (0, n, 0, i)),
        pl.BlockSpec(
            (sources, 1, local, LANES), lambda n, i: (0, n, 0, jnp.maximum(i * per_halo - 1, 0))
        ),
        pl.BlockSpec((sources * local, TAPS), lambda n, i: (0, 0)),
        pl.BlockSpec((filters, sources * local), lambda n, i: (0, 0)),
    ]


def pool_pass(own, traces, dw_weight, pw_weight, devices):
    sources, pair, local, length = traces.shape
    filters, metrics = pw_weight.shape
    chunk = POOL_CHUNK
    width = filters + LANES
    return pl.pallas_call(
        functools.partial(pool_kernel, length),
        grid=(pair, length // chunk),
        in_specs=[pl.BlockSpec(memory_space=pltpu.SMEM)] + trace_specs(traces, filters, chunk),
        out_specs=pl.BlockSpec((devices, pair, width), lambda n, i: (0, 0, 0)),
        out_shape=jax.ShapeDtypeStruct((devices, pair, width), BF16),
        scratch_shapes=[
            pltpu.VMEM((metrics, chunk), BF16),
            pltpu.VMEM((filters, chunk), F32),
            pltpu.VMEM((filters, LANES), F32),
            pltpu.VMEM((8, filters), F32),
        ],
        compiler_params=pltpu.CompilerParams(
            dimension_semantics=("arbitrary", "arbitrary"), vmem_limit_bytes=32 << 20
        ),
    )(own, traces, traces, dw_weight, pw_weight)


def terms_pass(traces, dw_weight, pw_weight, proj_weight):
    sources, pair, local, length = traces.shape
    filters, metrics = pw_weight.shape
    chunk = TERM_CHUNK
    deep = metrics * (TAPS + 1)
    return pl.pallas_call(
        terms_kernel,
        grid=(pair, length // chunk),
        in_specs=trace_specs(traces, filters, chunk)
        + [pl.BlockSpec(proj_weight.shape, lambda n, i: (0, 0))],
        out_specs=[
            pl.BlockSpec((1, deep, filters), lambda n, i: (n, 0, 0)),
            pl.BlockSpec(proj_weight.shape, lambda n, i: (0, 0)),
        ],
        out_shape=[
            jax.ShapeDtypeStruct((pair, deep, filters), F32),
            jax.ShapeDtypeStruct(proj_weight.shape, proj_weight.dtype),
        ],
        scratch_shapes=[
            pltpu.VMEM((filters, chunk), F32),
            pltpu.VMEM((filters, chunk), BF16),
            pltpu.VMEM((deep, chunk), BF16),
        ],
        compiler_params=pltpu.CompilerParams(
            dimension_semantics=("arbitrary", "arbitrary"), vmem_limit_bytes=32 << 20
        ),
    )(traces, traces, dw_weight, pw_weight, proj_weight)


def middle_kernel(
    length, own_ref, pooled_ref, proj_ref, pw_turned_ref, terms_ref,
    loss_ref, grad_a_ref, grad_v_ref, sums_ref, held_a, held_v,
):
    filters, width = proj_ref.shape
    count = pooled_ref.shape[0]
    metrics = pw_turned_ref.shape[0]
    factor = LOGIT_SCALE / width
    proj = proj_ref[...]

    def normed(pooled):
        embedding = jnp.dot(pooled, proj, preferred_element_type=F32)
        inverse = lax.rsqrt(jnp.mean(embedding * embedding, 1, keepdims=True) + 1e-06)
        return embedding * inverse, inverse

    unit_a, inverse_a = normed(pooled_ref[:, 0:filters])
    unit_v, inverse_v = normed(pooled_ref[:, filters + LANES : 2 * filters + LANES])
    queries = unit_a.astype(BF16)
    keys = unit_v.astype(BF16)
    logits = factor * lax.dot_general(
        queries, keys, (((1,), (1,)), ((), ())), preferred_element_type=F32
    )
    partner = pooled_ref[:, filters : filters + 1].astype(F32).astype(jnp.int32)
    columns = lax.broadcasted_iota(jnp.int32, (count, count), 1)
    matches = columns == partner
    weights = jnp.exp(logits - LOGIT_SCALE)
    totals = jnp.sum(weights, 1, keepdims=True)
    positive = jnp.sum(jnp.where(matches, logits, 0.0), 1, keepdims=True)
    loss_ref[...] = LOGIT_SCALE + jnp.log(totals) - positive
    coeffs = (weights / totals - jnp.where(matches, 1.0, 0.0)).astype(BF16)
    unit_grad_a = factor * jnp.dot(coeffs, keys, preferred_element_type=F32)
    unit_grad_v = factor * lax.dot_general(
        coeffs, queries, (((0,), (0,)), ((), ())), preferred_element_type=F32
    )

    def embed_grad(unit, inverse, unit_grad):
        return inverse * (unit_grad - unit * jnp.mean(unit * unit_grad, 1, keepdims=True))

    own = own_ref[0]

    def pool_grad(unit, inverse, unit_grad, out_ref, held):
        grad = embed_grad(unit, inverse, unit_grad).astype(BF16)
        out_ref[...] = grad
        held[...] = grad.astype(F32)
        row = jnp.broadcast_to(held[pl.ds(own, 1), :], (16, width)).astype(BF16)
        pool = lax.dot_general(row, proj, (((1,), (1,)), ((), ())), preferred_element_type=F32)
        return pool[0:1, :] * (0.5 / length)

    pool_a = pool_grad(unit_a, inverse_a, unit_grad_a, grad_a_ref, held_a)
    pool_v = pool_grad(unit_v, inverse_v, unit_grad_v, grad_v_ref, held_v)

    def weighted(index):
        rows = pl.ds(index * metrics, metrics)
        return terms_ref[0, rows, :] * pool_a + terms_ref[1, rows, :] * pool_v

    mixing = weighted(0).T
    pw_turned = pw_turned_ref[...].astype(F32)
    lanes = lax.broadcasted_iota(jnp.int32, (metrics, LANES), 1)
    kernel = jnp.zeros((metrics, LANES), F32)
    for tap in range(TAPS):
        column = jnp.sum(pw_turned * weighted(tap + 1), 1, keepdims=True)
        kernel = kernel + jnp.where(lanes == tap, column, 0.0)
    parts = sums_ref.shape[0]
    mix_rows, tap_rows = filters // parts, metrics // parts
    for part in range(parts):
        sums_ref[part, 0:mix_rows, :] = mixing[part * mix_rows : (part + 1) * mix_rows, :]
        sums_ref[part, mix_rows : mix_rows + tap_rows, :] = kernel[
            part * tap_rows : (part + 1) * tap_rows, :
        ]


def middle(own, pooled, proj_weight, pw_turned, terms, parts, length):
    filters, width = proj_weight.shape
    metrics = pw_turned.shape[0]
    count = pooled.shape[0]
    whole = pl.BlockSpec(memory_space=pltpu.VMEM)
    rows = filters // parts + metrics // parts
    return pl.pallas_call(
        functools.partial(middle_kernel, length),
        in_specs=[pl.BlockSpec(memory_space=pltpu.SMEM)] + [whole] * 4,
        out_specs=[whole] * 4,
        out_shape=[
            jax.ShapeDtypeStruct((count, 1), F32),
            jax.ShapeDtypeStruct((count, width), BF16),
            jax.ShapeDtypeStruct((count, width), BF16),
            jax.ShapeDtypeStruct((parts, rows, metrics), F32),
        ],
        scratch_shapes=[pltpu.VMEM((count, width), F32), pltpu.VMEM((count, width), F32)],
        compiler_params=pltpu.CompilerParams(vmem_limit_bytes=48 << 20),
    )(own, pooled, proj_weight, pw_turned, terms)


def swap(value, axis):
    return lax.all_to_all(value, axis, 0, 0, tiled=True)


def fold_kernel(mix_rows, parts_ref, out_ref, tap_ref=None):
    total = jnp.sum(parts_ref[...], 0)
    if tap_ref is not None:
        tap_ref[...] = total[mix_rows:, 0:TAPS]
        total = total[0:mix_rows, :]
    out_ref[...] = jnp.broadcast_to(total[None], out_ref.shape)


def fold(parts, mix_rows, last):
    count, rows, width = parts.shape
    whole = pl.BlockSpec(memory_space=pltpu.VMEM)
    out = jax.ShapeDtypeStruct((count, mix_rows if last else rows, width), F32)
    if last:
        out = [out, jax.ShapeDtypeStruct((rows - mix_rows, TAPS), F32)]
    return pl.pallas_call(
        functools.partial(fold_kernel, mix_rows),
        in_specs=[whole],
        out_specs=[whole] * 2 if last else whole,
        out_shape=out,
    )(parts)


def body(anchors, views, dw_weight, pw_weight, proj_weight, partner):
    chan_index = lax.axis_index("chan")
    dp_index = lax.axis_index("dp")
    chan_count = lax.axis_size("chan")
    dp_count = lax.axis_size("dp")
    pairs, local_metrics, length = anchors.shape
    filters, metrics = pw_weight.shape
    width = proj_weight.shape[1]

    position = (dp_index * chan_count + chan_index).astype(jnp.int32)
    own = jnp.stack([position, lax.dynamic_slice_in_dim(partner, chan_index, 1, 0)[0]])
    traces = swap(jnp.stack([anchors, views], 1), "chan")
    message = pool_pass(own, traces, dw_weight, pw_weight, dp_count * chan_count)
    pooled = swap(message, ("dp", "chan")).reshape(message.shape[0], -1)
    terms, proj_held = terms_pass(traces, dw_weight, pw_weight, proj_weight)
    losses, grad_a, grad_v, sums = middle(
        own, pooled, proj_held, pw_weight.T, terms, chan_count, length
    )

    folded = fold(swap(sums, "chan"), filters // chan_count, False)
    shares, grad_dw = fold(swap(folded, "dp"), filters // chan_count, True)
    grad_pw = swap(shares, "chan").reshape(filters, metrics)

    cols = width // dp_count
    rows = filters // chan_count

    def proj_part(offset, grad):
        features = lax.dynamic_slice_in_dim(pooled, offset + chan_index * rows, rows, 1)
        part = lax.dynamic_slice_in_dim(grad, dp_index * cols, cols, 1)
        return lax.dot_general(
            features, part, (((0,), (0,)), ((), ())), preferred_element_type=F32
        )

    grad_proj = proj_part(0, grad_a) + proj_part(filters + LANES, grad_v)
    loss = lax.dynamic_slice_in_dim(losses, dp_index * pairs, pairs, 0).reshape(pairs)
    return (loss, grad_dw, grad_pw, grad_proj)


def solution(mesh):
    placed = (P("dp", "chan", None), P("dp", "chan", None), P(), P(), P(), P("dp"))
    return jax.shard_map(
        body,
        mesh=mesh,
        in_specs=placed,
        out_specs=(P("dp"), P("chan", None), P(), P("chan", "dp")),
        check_vma=False,
    )
```

time: 156 us -> 160 us (1.026)
  blocking collectives: 50 us -> 17.4 us
  Pallas kernels: 16.3 us -> 29.4 us
  waiting for transfers between devices: 48.5 us -> 61 us
  starting transfers between devices: 27 us -> 35.1 us
  local copies, waits for them, and re-layouts: 8.17 us -> 10.3 us
    all_to_all x2 -> x1, blocking collectives: 50 us -> 17.4 us  [swap(): return lax.all_to_all(value, axis, 0, 0, tiled=True)]
    pallas_call x2 -> x4, Pallas kernels: 13.8 us -> 26.3 us  [the longest x1 13.4 us: terms_pass(): pl.pallas_call(terms_kernel, grid=(pair, length // chunk), in_specs=trace...]
    all_to_all x4, waiting for transfers between devices: 48.5 us -> 61 us  [swap(): return lax.all_to_all(value, axis, 0, 0, tiled=True)]
    all_to_all x4, starting transfers between devices: 27 us -> 35.1 us  [swap(): return lax.all_to_all(value, axis, 0, 0, tiled=True)]
    unnamed x17 -> x23, local copies, waits for them, and re-layouts: 4.37 us -> 9.07 us
    another operation x0 -> x2, other arithmetic: none -> 3.8 us  [the longest x1 3.08 us: body(): traces = swap(jnp.stack([anchors, views], 1), 'chan')]
    broadcast_in_dim x1 -> x0, other arithmetic: 2.61 us -> none  [spread(): return swap(jnp.broadcast_to(value[None], (count,) + value.shape), axis)]
    broadcast_in_dim x5 -> x0, local copies, waits for them, and re-layouts: 2.2 us -> none  [the longest x4 2.2 us: spread(): return swap(jnp.broadcast_to(value[None], (count,) + value.shape), axis)]
  transfers between devices with their start and end apart: 4 -> 4, of which waited for: 4 -> 4; matrix products, arithmetic and copies ran while one was open for 2% -> 4% of each run, Pallas kernels for 4% -> 8%
where the time goes in v2:
time: 160 us
  waiting for transfers between devices  61 us (38%)
  starting transfers between devices  35.1 us (22%)
  Pallas kernels  29.4 us (18%)
  blocking collectives  17.4 us (11%)
  local copies, waits for them, and re-layouts  10.3 us (6%)
  other arithmetic  3.8 us (2%)
  matrix products  1.94 us (1%)
    all_to_all x4, waiting for transfers between devices, swap(): return lax.all_to_all(value, axis, 0, 0, tiled=True)  61 us
    all_to_all x4, starting transfers between devices, swap(): return lax.all_to_all(value, axis, 0, 0, tiled=True)  35.1 us
    all_to_all x1, blocking collectives, swap(): return lax.all_to_all(value, axis, 0, 0, tiled=True)  17.4 us
    pallas_call x1, Pallas kernels, terms_pass(): pl.pallas_call(terms_kernel, grid=(pair, length // chunk), in_specs=trace...  13.4 us
    pallas_call x1, Pallas kernels, pool_pass(): pl.pallas_call(functools.partial(pool_kernel, length), grid=(pair, length...  9.67 us
    unnamed x23, local copies, waits for them, and re-layouts  9.07 us
    pallas_call x2, Pallas kernels, fold(): pl.pallas_call(functools.partial(fold_kernel, mix_rows), in_specs=[whole]...  3.24 us
  transfers between devices with their start and end apart: 4, of which 4 were waited for; matrix products, arithmetic and copies ran while one was open for 4% of the time, Pallas kernels for 8%

profile of v2, /device:TPU:1, one launch (start us, length us, event | category | flops | bytes accessed | tf_op | source)
XLA Modules:
  0.0 159.6 jit_solution(14136531849672009483)
XLA Ops:
  0.6 3.1 %pad_maximum_fusion = bf16[16,2,8,4096]{3,2,1,0:T(8,128)(2,1)} fusion(bf16[16,1,8,4096]{3,2,1,0:T(8,128)(2,1)} %bitcast.11, bf16[16,1,8,4096]{3,2,1,0:T(8,128)(2,1)} %bitcast.12), kind=kLoop, calls=%fused_computation | loop fusion | flops 1048576 | bytes 4194304 | tf_op jit(solution)/shard_map/stack | solution.py:305
  3.7 0.0 copy-start.7
  3.7 0.0 copy-start.8
  3.7 0.0 copy-start
  3.7 11.9 %all-to-all-start = ((bf16[16,2,8,4096]{3,2,1,0:T(8,128)(2,1)}), bf16[16,2,8,4096]{3,2,1,0:T(8,128)(2,1)S(1)}, u32[]{:S(2)}, u32[]{:S(2)}) async-start(bf16[16,2,8,4096]{3,2,1,0:T(8,128)(2,1)} %pad_maximum_fusion), calls=%async_computation | async-start | bytes 4194304 | tf_op jit(solution)/shard_map/all_to_all | solution.py:269
  15.6 0.0 copy-done.7
  15.6 0.1 copy.14.dw_ref
  15.7 0.0 copy-done.8
  15.7 0.6 dynamic_slice.18
  16.3 0.7 pad_add_fusion.own_ref
  17.0 47.7 %all-to-all-done.x_ref.halo_ref = bf16[16,2,8,4096]{3,2,1,0:T(8,128)(2,1)S(1)} async-done(((bf16[16,2,8,4096]{3,2,1,0:T(8,128)(2,1)}), bf16[16,2,8,4096]{3,2,1,0:T(8,128)(2,1)S(1)}, u32[]{:S(2)}, u32[]{:S(2)}) %all-to-all-start) | async-done | bytes 2097184 | tf_op jit(solution)/shard_map/all_to_all | solution.py:269
  64.7 0.0 copy-done
  64.7 9.7 %shard_map.93 = bf16[256,2,384]{2,1,0:T(2,128)(2,1)} custom-call(s32[2]{0:T(128)S(1)} %pad_add_fusion.own_ref, bf16[16,2,8,4096]{3,2,1,0:T(8,128)(2,1)S(1)} %all-to-all-done.x_ref.halo_ref, bf16[16,2,8,4096]{3,2,1,0:T(8,128)(2,1)S(1)} %all-to-all-done.x_ref.halo_ref, f32[128,4]{1,0:T(8,128)S(1)} %copy.14.dw_ref, bf16[256,128]{1,0:T(8,128)(2,1)S(1)} %copy-done), custom_call_target="tpu_custom_call" | custom-call | tf_op jit(solution)/shard_map/pallas_call | solution.py:129
  74.4 11.8 %all-to-all-start.1 = ((bf16[256,2,384]{2,1,0:T(2,128)(2,1)}), bf16[256,2,384]{2,1,0:T(2,128)(2,1)}, u32[]{:S(2)}, u32[]{:S(2)}) async-start(bf16[256,2,384]{2,1,0:T(2,128)(2,1)} %shard_map.93), calls=%async_computation.1 | async-start | bytes 786432 | tf_op jit(solution)/shard_map/all_to_all | solution.py:269
  86.2 0.7 copy.16
  87.0 0.0 copy-start.1
  87.0 1.0 copy-done.1
  88.0 13.4 %shard_map.94 = (f32[2,640,256]{2,1,0:T(8,128)S(1)}, bf16[256,1024]{1,0:T(8,128)(2,1)S(1)}) custom-call(bf16[16,2,8,4096]{3,2,1,0:T(8,128)(2,1)S(1)} %all-to-all-done.x_ref.halo_ref, bf16[16,2,8,4096]{3,2,1,0:T(8,128)(2,1)S(1)} %all-to-all-done.x_ref.halo_ref, f32[128,4]{1,0:T(8,128)S(1)} %copy.14.dw_ref, bf16[256,128]{1,0:T(8,128)(2,1)S(1)} %copy-done, ...), custom_call_target="tpu_custom_call" | custom-call | tf_op jit(solution)/shard_map/pallas_call | solution.py:152
  101.4 0.0 copy-start.2
  101.4 0.8 copy-done.2
  102.2 1.6 %all-to-all-done.1 = bf16[256,2,384]{2,1,0:T(2,128)(2,1)} async-done(((bf16[256,2,384]{2,1,0:T(2,128)(2,1)}), bf16[256,2,384]{2,1,0:T(2,128)(2,1)}, u32[]{:S(2)}, u32[]{:S(2)}) %all-to-all-start.1) | async-done | bytes 393248 | tf_op jit(solution)/shard_map/all_to_all | solution.py:269
  103.8 1.0 copy.18
  104.9 0.0 copy-start.3
  104.9 1.0 copy-done.3
  105.9 0.0 copy-start.4
  105.9 0.8 copy-done.4
  106.8 3.1 %shard_map.95 = (f32[256,1]{1,0:T(8,128)S(1)}, bf16[256,1024]{1,0:T(8,128)(2,1)S(1)}, bf16[256,1024]{1,0:T(8,128)(2,1)S(1)}, f32[16,24,128]{2,1,0:T(8,128)S(1)}) custom-call(s32[2]{0:T(128)S(1)} %pad_add_fusion.own_ref, bf16[256,768]{1,0:T(8,128)(2,1)S(1)} %bitcast.7, bf16[256,1024]{1,0:T(8,128)(2,1)S(1)} %copy-done.3, bf16[128,256]{1,0:T(8,128)(2,1)S(1)} %bitcast.10, ...), custom_call_target="tpu_custom_call" | custom-call | tf_op jit(solution)/shard_map/pallas_call | solution.py:253
  109.8 0.0 copy-start.5
  109.9 0.8 copy-done.5
  110.6 17.4 %all_to_all.25.parts_ref = f32[16,24,128]{2,1,0:T(8,128)} all-to-all(f32[16,24,128]{2,1,0:T(8,128)S(1)} %get-tuple-element.15), channel_id=1, replica_groups=mesh['dp'=16,'chan'=16] {'chan'}, dimensions={0} | all-to-all | bytes 393216 | tf_op jit(solution)/shard_map/all_to_all | solution.py:269
  128.0 1.6 %shard_map.96 = f32[16,24,128]{2,1,0:T(8,128)} custom-call(f32[16,24,128]{2,1,0:T(8,128)} %all_to_all.25.parts_ref), custom_call_target="tpu_custom_call" | custom-call | tf_op jit(solution)/shard_map/pallas_call | solution.py:286
  129.7 6.5 %all-to-all-start.3 = ((f32[16,24,128]{2,1,0:T(8,128)}), f32[16,24,128]{2,1,0:T(8,128)S(1)}, u32[]{:S(2)}, u32[]{:S(2)}) async-start(f32[16,24,128]{2,1,0:T(8,128)} %shard_map.96), calls=%async_computation.3 | async-start | bytes 393216 | tf_op jit(solution)/shard_map/all_to_all | solution.py:269
  136.2 6.7 %all-to-all-done.3.parts_ref = f32[16,24,128]{2,1,0:T(8,128)S(1)} async-done(((f32[16,24,128]{2,1,0:T(8,128)}), f32[16,24,128]{2,1,0:T(8,128)S(1)}, u32[]{:S(2)}, u32[]{:S(2)}) %all-to-all-start.3) | async-done | bytes 196640 | tf_op jit(solution)/shard_map/all_to_all | solution.py:269
  142.8 0.0 copy-start.6
  142.8 0.7 copy-done.6
  143.5 1.6 %shard_map.97 = (f32[16,16,128]{2,1,0:T(8,128)}, f32[8,4]{1,0:T(8,128)}) custom-call(f32[16,24,128]{2,1,0:T(8,128)} %copy-done.6), custom_call_target="tpu_custom_call" | custom-call | tf_op jit(solution)/shard_map/pallas_call | solution.py:286
  145.1 4.9 %all-to-all-start.4 = ((f32[16,16,128]{2,1,0:T(8,128)}), f32[16,16,128]{2,1,0:T(8,128)S(1)}, u32[]{:S(2)}, u32[]{:S(2)}) async-start(f32[16,16,128]{2,1,0:T(8,128)} %get-tuple-element.17), calls=%async_computation.4 | async-start | bytes 262144 | tf_op jit(solution)/shard_map/all_to_all | solution.py:269
  150.0 1.1 fusion.2
  151.1 0.6 dynamic-slice_reduce_fusion
  151.7 0.8 convolution_add_fusion
  152.6 1.3 copy.17
  153.9 5.0 %all-to-all-done.4 = f32[16,16,128]{2,1,0:T(8,128)S(1)} async-done(((f32[16,16,128]{2,1,0:T(8,128)}), f32[16,16,128]{2,1,0:T(8,128)S(1)}, u32[]{:S(2)}, u32[]{:S(2)}) %all-to-all-start.4) | async-done | bytes 131104 | tf_op jit(solution)/shard_map/all_to_all | solution.py:269
  158.9 0.7 copy.20
Async XLA Ops:
  3.7 11.9 %copy-start.7 = (f32[128,4]{0,1:T(4,128)S(1)}, f32[128,4]{0,1:T(4,128)}, u32[]{:S(2)}) copy-start(f32[128,4]{0,1:T(4,128)} %param.8) | copy-start | bytes 6148
  3.7 12.0 %copy-start.8 = (s32[16]{0:T(128)S(1)}, s32[16]{0:T(128)}, u32[]{:S(2)}) copy-start(s32[16]{0:T(128)} %param.11) | copy-start | bytes 196
  3.7 61.0 %copy-start = (bf16[256,128]{1,0:T(8,128)(2,1)S(1)}, bf16[256,128]{1,0:T(8,128)(2,1)}, u32[]{:S(2)}) copy-start(bf16[256,128]{1,0:T(8,128)(2,1)} %pw_ref.3) | copy-start | bytes 196612
  3.7 61.0 %all-to-all-start = ((bf16[16,2,8,4096]{3,2,1,0:T(8,128)(2,1)}), bf16[16,2,8,4096]{3,2,1,0:T(8,128)(2,1)S(1)}, u32[]{:S(2)}, u32[]{:S(2)}) async-start(bf16[16,2,8,4096]{3,2,1,0:T(8,128)(2,1)} %pad_maximum_fusion), calls=%async_computation | async-start | bytes 4194304 | tf_op jit(solution)/shard_map/all_to_all | solution.py:269
  74.4 29.4 %all-to-all-start.1 = ((bf16[256,2,384]{2,1,0:T(2,128)(2,1)}), bf16[256,2,384]{2,1,0:T(2,128)(2,1)}, u32[]{:S(2)}, u32[]{:S(2)}) async-start(bf16[256,2,384]{2,1,0:T(2,128)(2,1)} %shard_map.93), calls=%async_computation.1 | async-start | bytes 786432 | tf_op jit(solution)/shard_map/all_to_all | solution.py:269
  87.0 1.0 copy-start.1
  101.4 0.8 copy-start.2
  104.9 1.0 copy-start.3
  105.9 0.8 copy-start.4
  109.8 0.8 copy-start.5
  129.7 13.2 %all-to-all-start.3 = ((f32[16,24,128]{2,1,0:T(8,128)}), f32[16,24,128]{2,1,0:T(8,128)S(1)}, u32[]{:S(2)}, u32[]{:S(2)}) async-start(f32[16,24,128]{2,1,0:T(8,128)} %shard_map.96), calls=%async_computation.3 | async-start | bytes 393216 | tf_op jit(solution)/shard_map/all_to_all | solution.py:269
  142.8 0.7 copy-start.6
  145.1 13.8 %all-to-all-start.4 = ((f32[16,16,128]{2,1,0:T(8,128)}), f32[16,16,128]{2,1,0:T(8,128)S(1)}, u32[]{:S(2)}, u32[]{:S(2)}) async-start(f32[16,16,128]{2,1,0:T(8,128)} %get-tuple-element.17), calls=%async_computation.4 | async-start | bytes 262144 | tf_op jit(solution)/shard_map/all_to_all | solution.py:269

commit v3 on v1

v3 whole, which is shorter than its diff:
```python
import functools

import jax
import jax.numpy as jnp
from jax import lax
from jax.experimental import pallas as pl
from jax.experimental.pallas import tpu as pltpu
from jax.sharding import PartitionSpec as P

TAPS = 4
TAP_SPACING = 16
RIM = (TAPS - 1) * TAP_SPACING
LOGIT_SCALE = 16.0
LANES = 128
SUBLANES = 8
POOL_CHUNK = 2048
BLOCK = 128
F32 = jnp.float32
BF16 = jnp.bfloat16


def mixed_half(block, begin, dw_turned_ref, half_turned, turned):
    steps = block.shape[1]
    flipped = block.T
    turned[RIM + begin : RIM + begin + steps, :] = flipped
    running = dw_turned_ref[0:1, :] * flipped
    for tap in range(1, TAPS):
        first = RIM + begin - tap * TAP_SPACING
        running = running + dw_turned_ref[tap : tap + 1, :] * turned[first : first + steps, :]
    return jnp.dot(running.astype(BF16), half_turned, preferred_element_type=F32)


def pool_kernel(length, x_ref, dw_turned_ref, pw_turned_ref, message_ref, turned, acc, held):
    trace, step = pl.program_id(0), pl.program_id(1)
    sources, _, local, chunk = x_ref.shape
    filters = pw_turned_ref.shape[1]

    @pl.when(step == 0)
    def _():
        acc[...] = jnp.zeros_like(acc)
        turned[0:RIM, :] = jnp.zeros((RIM, sources * local), F32)

    @pl.when(step > 0)
    def _():
        turned[0:RIM, :] = turned[chunk : chunk + RIM, :]

    half_turned = pw_turned_ref[...] * 0.5
    total = acc[...]
    for begin in range(0, chunk, BLOCK):
        block = x_ref[:, 0, :, begin : begin + BLOCK].astype(F32).reshape(sources * local, BLOCK)
        value = mixed_half(block, begin, dw_turned_ref, half_turned, turned)
        silu = value + value * jnp.tanh(value)
        total = total + jnp.sum(silu.reshape(BLOCK // SUBLANES, SUBLANES, filters), 0)
    acc[...] = total

    @pl.when(step == pl.num_programs(1) - 1)
    def _():
        held[pl.ds(trace, 1), :] = jnp.sum(acc[...], 0, keepdims=True) / length

    @pl.when((step == pl.num_programs(1) - 1) & (trace == pl.num_programs(0) - 1))
    def _():
        rows = held[0 : message_ref.shape[1], :].astype(BF16)
        message_ref[...] = jnp.broadcast_to(rows[None], message_ref.shape)


def pool_pass(traces, dw_turned, pw_turned, devices):
    sources, pair, local, length = traces.shape
    metrics, filters = pw_turned.shape
    return pl.pallas_call(
        functools.partial(pool_kernel, length),
        grid=(pair, length // POOL_CHUNK),
        in_specs=[
            pl.BlockSpec((sources, 1, local, POOL_CHUNK), lambda n, i: (0, n, 0, i)),
            pl.BlockSpec(dw_turned.shape, lambda n, i: (0, 0)),
            pl.BlockSpec(pw_turned.shape, lambda n, i: (0, 0)),
        ],
        out_specs=pl.BlockSpec((devices, pair, filters), lambda n, i: (0, 0, 0)),
        out_shape=jax.ShapeDtypeStruct((devices, pair, filters), BF16),
        scratch_shapes=[
            pltpu.VMEM((POOL_CHUNK + RIM, metrics), F32),
            pltpu.VMEM((SUBLANES, filters), F32),
            pltpu.VMEM((SUBLANES, filters), F32),
        ],
        compiler_params=pltpu.CompilerParams(
            dimension_semantics=("arbitrary", "arbitrary"), vmem_limit_bytes=12 << 20
        ),
    )(traces, dw_turned, pw_turned)


def terms_kernel(
    x_ref, dw_turned_ref, pw_turned_ref, terms_ref, turned, slope, plain
):
    sources, _, local, length = x_ref.shape
    metrics = sources * local
    half_turned = pw_turned_ref[...] * 0.5
    turned[0:RIM, :] = jnp.zeros((RIM, metrics), F32)
    slope[length : length + RIM, :] = jnp.zeros((RIM, slope.shape[1]), BF16)
    for begin in range(0, length, BLOCK):
        block = x_ref[:, 0, :, begin : begin + BLOCK].astype(F32).reshape(metrics, BLOCK)
        plain[:, begin : begin + BLOCK] = block.astype(BF16)
        value = mixed_half(block, begin, dw_turned_ref, half_turned, turned)
        bent = jnp.tanh(value)
        slope[begin : begin + BLOCK, :] = (
            (1.0 + bent) * (1.0 + value * (1.0 - bent))
        ).astype(BF16)
    for tap in range(TAPS):
        first = tap * TAP_SPACING
        terms_ref[0, tap * metrics : (tap + 1) * metrics, :] = jnp.dot(
            plain[...], slope[first : first + length, :], preferred_element_type=F32
        )


def terms_pass(traces, dw_turned, pw_turned):
    sources, pair, local, length = traces.shape
    metrics, filters = pw_turned.shape
    return pl.pallas_call(
        terms_kernel,
        grid=(pair,),
        in_specs=[
            pl.BlockSpec((sources, 1, local, length), lambda n: (0, n, 0, 0)),
            pl.BlockSpec(dw_turned.shape, lambda n: (0, 0)),
            pl.BlockSpec(pw_turned.shape, lambda n: (0, 0)),
        ],
        out_specs=pl.BlockSpec((1, metrics * TAPS, filters), lambda n: (n, 0, 0)),
        out_shape=jax.ShapeDtypeStruct((pair, metrics * TAPS, filters), F32),
        scratch_shapes=[
            pltpu.VMEM((length + RIM, metrics), F32),
            pltpu.VMEM((length + RIM, filters), BF16),
            pltpu.VMEM((metrics, length), BF16),
        ],
        compiler_params=pltpu.CompilerParams(
            dimension_semantics=("arbitrary",), vmem_limit_bytes=20 << 20
        ),
    )(traces, dw_turned, pw_turned)


def middle_kernel(
    length, own_ref, pooled_ref, partner_ref, proj_ref, dw_ref, pw_turned_ref, terms_ref,
    loss_ref, grad_a_ref, grad_v_ref, sums_ref, held_a, held_v,
):
    filters, width = proj_ref.shape
    count = pooled_ref.shape[0]
    metrics = pw_turned_ref.shape[0]
    factor = LOGIT_SCALE / width
    proj = proj_ref[...]

    def normed(pooled):
        embedding = jnp.dot(pooled, proj, preferred_element_type=F32)
        inverse = lax.rsqrt(jnp.mean(embedding * embedding, 1, keepdims=True) + 1e-06)
        return embedding * inverse, inverse

    unit_a, inverse_a = normed(pooled_ref[:, 0:filters])
    unit_v, inverse_v = normed(pooled_ref[:, filters : 2 * filters])
    queries = unit_a.astype(BF16)
    keys = unit_v.astype(BF16)
    logits = factor * lax.dot_general(
        queries, keys, (((1,), (1,)), ((), ())), preferred_element_type=F32
    )
    columns = lax.broadcasted_iota(jnp.int32, (count, count), 1)
    matches = columns == partner_ref[...]
    weights = jnp.exp(logits - LOGIT_SCALE)
    totals = jnp.sum(weights, 1, keepdims=True)
    positive = jnp.sum(jnp.where(matches, logits, 0.0), 1, keepdims=True)
    loss_ref[...] = LOGIT_SCALE + jnp.log(totals) - positive
    coeffs = (weights / totals - jnp.where(matches, 1.0, 0.0)).astype(BF16)
    unit_grad_a = factor * jnp.dot(coeffs, keys, preferred_element_type=F32)
    unit_grad_v = factor * lax.dot_general(
        coeffs, queries, (((0,), (0,)), ((), ())), preferred_element_type=F32
    )
    own = own_ref[0]

    def pool_grad(unit, inverse, unit_grad, out_ref, held):
        grad = inverse * (unit_grad - unit * jnp.mean(unit * unit_grad, 1, keepdims=True))
        grad = grad.astype(BF16)
        out_ref[...] = grad
        held[...] = grad.astype(F32)
        row = jnp.broadcast_to(held[pl.ds(own, 1), :], (16, width)).astype(BF16)
        pool = lax.dot_general(row, proj, (((1,), (1,)), ((), ())), preferred_element_type=F32)
        return pool[0:1, :] * (0.5 / length)

    pool_a = pool_grad(unit_a, inverse_a, unit_grad_a, grad_a_ref, held_a)
    pool_v = pool_grad(unit_v, inverse_v, unit_grad_v, grad_v_ref, held_v)

    pw_turned = pw_turned_ref[...].astype(F32)
    lanes = lax.broadcasted_iota(jnp.int32, (metrics, LANES), 1)
    mixing = jnp.zeros((metrics, filters), F32)
    kernel = jnp.zeros((metrics, LANES), F32)
    for tap in range(TAPS):
        rows = pl.ds(tap * metrics, metrics)
        weighted = terms_ref[0, rows, :] * pool_a + terms_ref[1, rows, :] * pool_v
        mixing = mixing + dw_ref[:, tap : tap + 1] * weighted
        column = jnp.sum(pw_turned * weighted, 1, keepdims=True)
        kernel = kernel + jnp.where(lanes == tap, column, 0.0)
    mixing = mixing.T
    parts = sums_ref.shape[0]
    mix_rows, tap_rows = filters // parts, metrics // parts
    for part in range(parts):
        sums_ref[part, 0:mix_rows, :] = mixing[part * mix_rows : (part + 1) * mix_rows, :]
        sums_ref[part, mix_rows : mix_rows + tap_rows, :] = kernel[
            part * tap_rows : (part + 1) * tap_rows, :
        ]


def middle(own, pooled, partners, proj_weight, dw_weight, pw_turned, terms, parts, length):
    filters, width = proj_weight.shape
    metrics = pw_turned.shape[0]
    count = pooled.shape[0]
    whole = pl.BlockSpec(memory_space=pltpu.VMEM)
    rows = filters // parts + metrics // parts
    return pl.pallas_call(
        functools.partial(middle_kernel, length),
        in_specs=[pl.BlockSpec(memory_space=pltpu.SMEM)] + [whole] * 6,
        out_specs=[whole] * 4,
        out_shape=[
            jax.ShapeDtypeStruct((count, 1), F32),
            jax.ShapeDtypeStruct((count, width), BF16),
            jax.ShapeDtypeStruct((count, width), BF16),
            jax.ShapeDtypeStruct((parts, rows, metrics), F32),
        ],
        scratch_shapes=[pltpu.VMEM((count, width), F32), pltpu.VMEM((count, width), F32)],
        compiler_params=pltpu.CompilerParams(vmem_limit_bytes=24 << 20),
    )(own, pooled, partners, proj_weight, dw_weight, pw_turned, terms)


def swap(value, axis):
    return lax.all_to_all(value, axis, 0, 0, tiled=True)


def fold_kernel(parts_ref, out_ref):
    out_ref[...] = jnp.broadcast_to(jnp.sum(parts_ref[...], 0)[None], out_ref.shape)


def fold(parts, copies):
    whole = pl.BlockSpec(memory_space=pltpu.VMEM)
    return pl.pallas_call(
        fold_kernel,
        in_specs=[whole],
        out_specs=whole,
        out_shape=jax.ShapeDtypeStruct((copies,) + parts.shape[1:], F32),
        compiler_params=pltpu.CompilerParams(vmem_limit_bytes=4 << 20),
    )(parts)


def unpack_kernel(index_ref, shares_ref, mix_ref, tap_ref):
    parts, rows, width = shares_ref.shape
    mix_rows = mix_ref.shape[0] // parts
    for part in range(parts):
        mix_ref[part * mix_rows : (part + 1) * mix_rows, :] = shares_ref[part, 0:mix_rows, :]
    taps = shares_ref[index_ref[0], mix_rows:rows, :]
    tap_ref[...] = taps.T[0 : tap_ref.shape[0], :]


def unpack(chan_index, shares, mix_rows):
    parts, rows, width = shares.shape
    whole = pl.BlockSpec(memory_space=pltpu.VMEM)
    return pl.pallas_call(
        unpack_kernel,
        in_specs=[pl.BlockSpec(memory_space=pltpu.SMEM), whole],
        out_specs=[whole, whole],
        out_shape=[
            jax.ShapeDtypeStruct((parts * mix_rows, width), F32),
            jax.ShapeDtypeStruct((TAPS, rows - mix_rows), F32),
        ],
        compiler_params=pltpu.CompilerParams(vmem_limit_bytes=4 << 20),
    )(chan_index.astype(jnp.int32).reshape(1), shares)


def body(anchors, views, dw_weight, pw_weight, proj_weight, partner):
    chan_index = lax.axis_index("chan")
    dp_index = lax.axis_index("dp")
    chan_count = lax.axis_size("chan")
    dp_count = lax.axis_size("dp")
    pairs, local_metrics, length = anchors.shape
    filters, metrics = pw_weight.shape
    width = proj_weight.shape[1]
    dw_turned, pw_turned = dw_weight.T, pw_weight.T

    partners = lax.dynamic_update_slice_in_dim(
        jnp.zeros((dp_count, pairs), jnp.int32), partner[None], dp_index, 0
    )
    bit = 1
    while bit < dp_count:
        partners += lax.ppermute(partners, "dp", [(i, i ^ bit) for i in range(dp_count)])
        bit *= 2
    partners = partners.reshape(pairs * dp_count, 1)
    traces = swap(jnp.stack([anchors, views], 1), "chan")
    traces, partners = lax.optimization_barrier((traces, partners))
    message = pool_pass(traces, dw_turned, pw_turned, dp_count * chan_count)
    pooled = swap(message, ("dp", "chan")).reshape(message.shape[0], -1)
    terms = terms_pass(traces, dw_turned, pw_turned)
    own = (dp_index * chan_count + chan_index).astype(jnp.int32).reshape(1)
    losses, grad_a, grad_v, sums = middle(
        own, pooled, partners, proj_weight, dw_weight, pw_turned, terms, dp_count, length
    )

    shares = fold(swap(sums, "dp"), chan_count)
    shares = fold(swap(shares, "chan"), dp_count)
    grad_pw, grad_dw = unpack(chan_index, swap(shares, "dp"), filters // dp_count)

    cols = width // dp_count
    rows = filters // chan_count

    def proj_part(offset, grad):
        features = lax.dynamic_slice_in_dim(pooled, offset + chan_index * rows, rows, 1)
        part = lax.dynamic_slice_in_dim(grad, dp_index * cols, cols, 1)
        return lax.dot_general(
            features, part, (((0,), (0,)), ((), ())), preferred_element_type=F32
        )

    grad_proj = proj_part(0, grad_a) + proj_part(filters, grad_v)
    loss = lax.dynamic_slice_in_dim(losses, dp_index * pairs, pairs, 0).reshape(pairs)
    return (loss, grad_dw.T, grad_pw, grad_proj)


def solution(mesh):
    placed = (P("dp", "chan", None), P("dp", "chan", None), P(), P(), P(), P("dp"))
    return jax.shard_map(
        body,
        mesh=mesh,
        in_specs=placed,
        out_specs=(P("dp"), P("chan", None), P(), P("chan", "dp")),
        check_vma=False,
    )
```

time: 156 us -> 136 us (0.87)
  blocking collectives: 50 us -> 9.87 us
  waiting for transfers between devices: 48.5 us -> 67 us
  starting transfers between devices: 27 us -> 37.3 us
  local copies, waits for them, and re-layouts: 8.17 us -> 2.21 us
  Pallas kernels: 16.3 us -> 14.2 us
    all_to_all x2 -> x1, blocking collectives: 50 us -> 9.87 us  [swap(): return lax.all_to_all(value, axis, 0, 0, tiled=True)]
    all_to_all x4, waiting for transfers between devices: 48.5 us -> 61.3 us  [swap(): return lax.all_to_all(value, axis, 0, 0, tiled=True)]
    ppermute x0 -> x4, waiting for transfers between devices: none -> 5.68 us  [body(): lax.ppermute(partners, 'dp', [(i, i ^ bit) for i in range(dp_count)])]
    ppermute x0 -> x4, starting transfers between devices: none -> 5.47 us  [body(): lax.ppermute(partners, 'dp', [(i, i ^ bit) for i in range(dp_count)])]
    all_to_all x4, starting transfers between devices: 27 us -> 31.8 us  [swap(): return lax.all_to_all(value, axis, 0, 0, tiled=True)]
    unnamed x17 -> x11, local copies, waits for them, and re-layouts: 4.37 us -> 1.3 us
    another operation x0 -> x1, other arithmetic: none -> 3.07 us  [body(): traces = swap(jnp.stack([anchors, views], 1), 'chan')]
    broadcast_in_dim x1 -> x0, other arithmetic: 2.61 us -> none  [spread(): return swap(jnp.broadcast_to(value[None], (count,) + value.shape), axis)]
  transfers between devices with their start and end apart: 4 -> 8, of which waited for: 4 -> 8; matrix products, arithmetic and copies ran while one was open for 2% -> 2% of each run, Pallas kernels for 4% -> 4%
where the time goes in v3:
time: 136 us; the launch traced here: 135 us
  waiting for transfers between devices  67 us (49%)
  starting transfers between devices  37.3 us (27%)
  Pallas kernels  14.2 us (10%)
  blocking collectives  9.87 us (7%)
  other arithmetic  3.09 us (2%)
  local copies, waits for them, and re-layouts  2.21 us (2%)
    all_to_all x4, waiting for transfers between devices, swap(): return lax.all_to_all(value, axis, 0, 0, tiled=True)  61.3 us
    all_to_all x4, starting transfers between devices, swap(): return lax.all_to_all(value, axis, 0, 0, tiled=True)  31.8 us
    all_to_all x1, blocking collectives, swap(): return lax.all_to_all(value, axis, 0, 0, tiled=True)  9.87 us
    ppermute x4, waiting for transfers between devices, body(): lax.ppermute(partners, 'dp', [(i, i ^ bit) for i in range(dp_count)])  5.68 us
    pallas_call x1, Pallas kernels, terms_pass(): pl.pallas_call(terms_kernel, grid=(pair,), in_specs=[pl.BlockSpec((source...  5.61 us
    ppermute x4, starting transfers between devices, body(): lax.ppermute(partners, 'dp', [(i, i ^ bit) for i in range(dp_count)])  5.47 us
    pallas_call x1, Pallas kernels, pool_pass(): pl.pallas_call(functools.partial(pool_kernel, length), grid=(pair, length...  3.89 us
    another operation x1, other arithmetic, body(): traces = swap(jnp.stack([anchors, views], 1), 'chan')  3.07 us
  transfers between devices with their start and end apart: 8, of which 8 were waited for; matrix products, arithmetic and copies ran while one was open for 2% of the time, Pallas kernels for 4%

profile of v3, /device:TPU:1, one launch (start us, length us, event | category | flops | bytes accessed | tf_op | source)
XLA Modules:
  0.0 135.5 jit_solution(9153548534046065366)
XLA Ops:
  0.6 3.1 %pad_maximum_fusion = bf16[16,2,8,4096]{3,2,1,0:T(8,128)(2,1)} fusion(bf16[16,1,8,4096]{3,2,1,0:T(8,128)(2,1)} %bitcast.20, bf16[16,1,8,4096]{3,2,1,0:T(8,128)(2,1)} %bitcast.21), kind=kLoop, calls=%fused_computation | loop fusion | flops 1048576 | bytes 4194304 | tf_op jit(solution)/shard_map/stack | solution.py:286
  3.7 0.0 copy-start.3
  3.7 0.0 copy-start.2
  3.7 0.0 copy-start.1
  3.7 11.9 %all-to-all-start = ((bf16[16,2,8,4096]{3,2,1,0:T(8,128)(2,1)}), bf16[16,2,8,4096]{3,2,1,0:T(8,128)(2,1)S(1)}, u32[]{:S(2)}, u32[]{:S(2)}) async-start(bf16[16,2,8,4096]{3,2,1,0:T(8,128)(2,1)} %pad_maximum_fusion), calls=%async_computation | async-start | bytes 4194304 | tf_op jit(solution)/shard_map/all_to_all | solution.py:226
  15.6 0.0 copy-done.3
  15.7 1.0 collective-permute-start
  16.7 0.8 collective-permute-done
  17.6 1.3 collective-permute-start.1
  18.9 1.3 collective-permute-done.1
  20.1 2.7 %collective-permute-start.2 = (s32[16,16]{1,0:T(8,128)S(1)}, s32[16,16]{1,0:T(8,128)S(1)}, u32[]{:S(2)}, u32[]{:S(2)}) collective-permute-start(s32[16,16]{1,0:T(8,128)S(1)} %add.43), channel_id=1, source_target_pairs={{0,64},{16,80},{32,96},{48,112},{64,0},{80,16},{96,32},{112,48},{1... | collective-permute-start | bytes 3080 | tf_op jit(solution)/shard_map/ppermute | solution.py:283
  22.9 1.3 collective-permute-done.2
  24.2 0.4 collective-permute-start.3
  24.6 0.0 copy-done.2
  24.6 0.1 copy.12
  24.7 2.3 %collective-permute-done.3 = s32[16,16]{1,0:T(8,128)S(1)} collective-permute-done((s32[16,16]{1,0:T(8,128)S(1)}, s32[16,16]{1,0:T(8,128)S(1)}, u32[]{:S(2)}, u32[]{:S(2)}) %collective-permute-start.3) | collective-permute-done | bytes 1056 | tf_op jit(solution)/shard_map/ppermute | solution.py:283
  27.0 0.1 reshape.24
  27.1 37.7 %all-to-all-done.x_ref = bf16[16,2,8,4096]{3,2,1,0:T(8,128)(2,1)S(1)} async-done(((bf16[16,2,8,4096]{3,2,1,0:T(8,128)(2,1)}), bf16[16,2,8,4096]{3,2,1,0:T(8,128)(2,1)S(1)}, u32[]{:S(2)}, u32[]{:S(2)}) %all-to-all-start) | async-done | bytes 2097184 | tf_op jit(solution)/shard_map/all_to_all | solution.py:226
  64.7 0.0 copy-done.1
  64.7 3.9 %shard_map.93 = bf16[256,2,256]{2,1,0:T(2,128)(2,1)} custom-call(bf16[16,2,8,4096]{3,2,1,0:T(8,128)(2,1)S(1)} %all-to-all-done.x_ref, f32[4,128]{1,0:T(4,128)S(1)} %bitcast.17, bf16[128,256]{1,0:T(8,128)(2,1)S(1)} %bitcast.14), custom_call_target="tpu_custom_call" | custom-call | tf_op jit(solution)/shard_map/pallas_call | solution.py:69
  68.6 10.9 %all-to-all-start.1 = ((bf16[256,2,256]{2,1,0:T(2,128)(2,1)}), bf16[256,2,256]{2,1,0:T(2,128)(2,1)S(1)}, u32[]{:S(2)}, u32[]{:S(2)}) async-start(bf16[256,2,256]{2,1,0:T(2,128)(2,1)} %shard_map.93), calls=%async_computation.1 | async-start | bytes 524288 | tf_op jit(solution)/shard_map/all_to_all | solution.py:226
  79.5 0.1 copy.14.dw_ref
  79.7 5.6 %shard_map.94.terms_ref = f32[2,512,256]{2,1,0:T(8,128)S(1)} custom-call(bf16[16,2,8,4096]{3,2,1,0:T(8,128)(2,1)S(1)} %all-to-all-done.x_ref, f32[4,128]{1,0:T(4,128)S(1)} %bitcast.18, bf16[128,256]{1,0:T(8,128)(2,1)S(1)} %bitcast.15), custom_call_target="tpu_custom_call" | custom-call | tf_op jit(solution)/shard_map/pallas_call | solution.py:116
  85.3 0.1 copy.13.partner_ref
  85.4 9.7 %all-to-all-done.1 = bf16[256,2,256]{2,1,0:T(2,128)(2,1)S(1)} async-done(((bf16[256,2,256]{2,1,0:T(2,128)(2,1)}), bf16[256,2,256]{2,1,0:T(2,128)(2,1)S(1)}, u32[]{:S(2)}, u32[]{:S(2)}) %all-to-all-start.1) | async-done | bytes 262176 | tf_op jit(solution)/shard_map/all_to_all | solution.py:226
  95.2 0.0 copy-start
  95.2 1.0 copy-done
  96.2 2.6 %shard_map.95 = (f32[256,1]{1,0:T(8,128)S(1)}, bf16[256,1024]{1,0:T(8,128)(2,1)S(1)}, bf16[256,1024]{1,0:T(8,128)(2,1)S(1)}, f32[16,24,128]{2,1,0:T(8,128)S(1)}) custom-call(s32[1]{0:T(128)} %bitcast.own_ref, bf16[256,512]{1,0:T(8,128)(2,1)S(1)} %bitcast.11, s32[256,1]{1,0:T(8,128)S(1)} %copy.13.partner_ref, bf16[256,1024]{1,0:T(8,128)(2,1)S(1)} %copy-done, ...), custom_call_target="tpu_custom_call" | custom-call | tf_op jit(solution)/shard_map/pallas_call | solution.py:210
  98.9 9.9 %all_to_all.25.parts_ref = f32[16,24,128]{2,1,0:T(8,128)S(1)} all-to-all(f32[16,24,128]{2,1,0:T(8,128)S(1)} %get-tuple-element.15), channel_id=1, replica_groups=mesh['dp'=16,'chan'=16] {'dp'}, dimensions={0} | all-to-all | bytes 393216 | tf_op jit(solution)/shard_map/all_to_all | solution.py:226
  108.7 0.7 shard_map.96
  109.4 3.5 %all-to-all-start.3 = ((f32[16,24,128]{2,1,0:T(8,128)}), f32[16,24,128]{2,1,0:T(8,128)S(1)}, u32[]{:S(2)}, u32[]{:S(2)}) async-start(f32[16,24,128]{2,1,0:T(8,128)} %shard_map.96), calls=%async_computation.3 | async-start | bytes 393216 | tf_op jit(solution)/shard_map/all_to_all | solution.py:226
  113.0 0.6 dynamic-slice_reduce_fusion
  113.6 0.2 fusion.2
  113.8 8.1 %all-to-all-done.3.parts_ref = f32[16,24,128]{2,1,0:T(8,128)S(1)} async-done(((f32[16,24,128]{2,1,0:T(8,128)}), f32[16,24,128]{2,1,0:T(8,128)S(1)}, u32[]{:S(2)}, u32[]{:S(2)}) %all-to-all-start.3) | async-done | bytes 196640 | tf_op jit(solution)/shard_map/all_to_all | solution.py:226
  121.9 0.7 shard_map.97
  122.6 5.5 %all-to-all-start.4 = ((f32[16,24,128]{2,1,0:T(8,128)}), f32[16,24,128]{2,1,0:T(8,128)S(1)}, u32[]{:S(2)}, u32[]{:S(2)}) async-start(f32[16,24,128]{2,1,0:T(8,128)} %shard_map.97), calls=%async_computation.4 | async-start | bytes 393216 | tf_op jit(solution)/shard_map/all_to_all | solution.py:226
  128.1 0.8 convolution_add_fusion
  128.9 5.9 %all-to-all-done.4.shares_ref = f32[16,24,128]{2,1,0:T(8,128)S(1)} async-done(((f32[16,24,128]{2,1,0:T(8,128)}), f32[16,24,128]{2,1,0:T(8,128)S(1)}, u32[]{:S(2)}, u32[]{:S(2)}) %all-to-all-start.4) | async-done | bytes 196640 | tf_op jit(solution)/shard_map/all_to_all | solution.py:226
  134.8 0.7 shard_map.98
  (8 shorter events, 0.1 us)
Async XLA Ops:
  3.7 11.9 %copy-start.3 = (s32[16]{0:T(128)S(1)}, s32[16]{0:T(128)}, u32[]{:S(2)}) copy-start(s32[16]{0:T(128)} %param.11) | copy-start | bytes 196
  3.7 20.9 %copy-start.2 = (bf16[256,128]{1,0:T(8,128)(2,1)S(1)}, bf16[256,128]{1,0:T(8,128)(2,1)}, u32[]{:S(2)}) copy-start(bf16[256,128]{1,0:T(8,128)(2,1)} %param.9) | copy-start | bytes 196612
  3.7 61.0 %copy-start.1 = (f32[128,4]{0,1:T(4,128)S(1)}, f32[128,4]{0,1:T(4,128)}, u32[]{:S(2)}) copy-start(f32[128,4]{0,1:T(4,128)} %param.8) | copy-start | bytes 6148
  3.7 61.0 %all-to-all-start = ((bf16[16,2,8,4096]{3,2,1,0:T(8,128)(2,1)}), bf16[16,2,8,4096]{3,2,1,0:T(8,128)(2,1)S(1)}, u32[]{:S(2)}, u32[]{:S(2)}) async-start(bf16[16,2,8,4096]{3,2,1,0:T(8,128)(2,1)} %pad_maximum_fusion), calls=%async_computation | async-start | bytes 4194304 | tf_op jit(solution)/shard_map/all_to_all | solution.py:226
  15.7 1.9 %collective-permute-start = (s32[16,16]{1,0:T(8,128)S(1)}, s32[16,16]{1,0:T(8,128)S(1)}, u32[]{:S(2)}, u32[]{:S(2)}) collective-permute-start(s32[16,16]{1,0:T(8,128)S(1)} %dynamic_update_slice.5), channel_id=1, source_target_pairs={{0,16},{16,0},{32,48},{48,32},{64,80},{80,64},{96,112},{112,96},{1... | collective-permute-start | bytes 3080 | tf_op jit(solution)/shard_map/ppermute | solution.py:283
  17.6 2.6 %collective-permute-start.1 = (s32[16,16]{1,0:T(8,128)S(1)}, s32[16,16]{1,0:T(8,128)S(1)}, u32[]{:S(2)}, u32[]{:S(2)}) collective-permute-start(s32[16,16]{1,0:T(8,128)S(1)} %add.42), channel_id=1, source_target_pairs={{0,32},{16,48},{32,0},{48,16},{64,96},{80,112},{96,64},{112,80},{1... | collective-permute-start | bytes 3080 | tf_op jit(solution)/shard_map/ppermute | solution.py:283
  20.1 4.0 %collective-permute-start.2 = (s32[16,16]{1,0:T(8,128)S(1)}, s32[16,16]{1,0:T(8,128)S(1)}, u32[]{:S(2)}, u32[]{:S(2)}) collective-permute-start(s32[16,16]{1,0:T(8,128)S(1)} %add.43), channel_id=1, source_target_pairs={{0,64},{16,80},{32,96},{48,112},{64,0},{80,16},{96,32},{112,48},{1... | collective-permute-start | bytes 3080 | tf_op jit(solution)/shard_map/ppermute | solution.py:283
  24.2 2.8 %collective-permute-start.3 = (s32[16,16]{1,0:T(8,128)S(1)}, s32[16,16]{1,0:T(8,128)S(1)}, u32[]{:S(2)}, u32[]{:S(2)}) collective-permute-start(s32[16,16]{1,0:T(8,128)S(1)} %add.44), channel_id=1, source_target_pairs={{0,128},{16,144},{32,160},{48,176},{64,192},{80,208},{96,224},{112... | collective-permute-start | bytes 3080 | tf_op jit(solution)/shard_map/ppermute | solution.py:283
  68.6 26.5 %all-to-all-start.1 = ((bf16[256,2,256]{2,1,0:T(2,128)(2,1)}), bf16[256,2,256]{2,1,0:T(2,128)(2,1)S(1)}, u32[]{:S(2)}, u32[]{:S(2)}) async-start(bf16[256,2,256]{2,1,0:T(2,128)(2,1)} %shard_map.93), calls=%async_computation.1 | async-start | bytes 524288 | tf_op jit(solution)/shard_map/all_to_all | solution.py:226
  95.2 1.0 copy-start
  109.4 12.5 %all-to-all-start.3 = ((f32[16,24,128]{2,1,0:T(8,128)}), f32[16,24,128]{2,1,0:T(8,128)S(1)}, u32[]{:S(2)}, u32[]{:S(2)}) async-start(f32[16,24,128]{2,1,0:T(8,128)} %shard_map.96), calls=%async_computation.3 | async-start | bytes 393216 | tf_op jit(solution)/shard_map/all_to_all | solution.py:226
  122.6 12.2 %all-to-all-start.4 = ((f32[16,24,128]{2,1,0:T(8,128)}), f32[16,24,128]{2,1,0:T(8,128)S(1)}, u32[]{:S(2)}, u32[]{:S(2)}) async-start(f32[16,24,128]{2,1,0:T(8,128)} %shard_map.97), calls=%async_computation.4 | async-start | bytes 393216 | tf_op jit(solution)/shard_map/all_to_all | solution.py:226

commit v4 on v3

v4 whole, which is shorter than its diff:
```python
import functools

import jax
import jax.numpy as jnp
from jax import lax
from jax.experimental import pallas as pl
from jax.experimental.pallas import tpu as pltpu
from jax.sharding import PartitionSpec as P

TAPS = 4
TAP_SPACING = 16
RIM = (TAPS - 1) * TAP_SPACING
LOGIT_SCALE = 16.0
LANES = 128
SUBLANES = 8
BLOCK = 256
F32 = jnp.float32
BF16 = jnp.bfloat16


def mixed_half(flipped, begin, dw_turned_ref, half, turned):
    steps = flipped.shape[0]
    turned[RIM + begin : RIM + begin + steps, :] = flipped
    running = dw_turned_ref[0:1, :] * flipped
    for tap in range(1, TAPS):
        first = RIM + begin - tap * TAP_SPACING
        running = running + dw_turned_ref[tap : tap + 1, :] * turned[first : first + steps, :]
    return lax.dot_general(
        running.astype(BF16), half, (((1,), (1,)), ((), ())), preferred_element_type=F32
    )


def pool_kernel(x_ref, dw_turned_ref, pw_ref, message_ref, turned):
    sources, pair, local, length = x_ref.shape
    filters = pw_ref.shape[0]
    half = pw_ref[...] * 0.5
    rows = []
    for trace in range(pair):
        held = turned.at[trace]
        held[0:RIM, :] = jnp.zeros((RIM, sources * local), F32)
        total = jnp.zeros((SUBLANES, filters), F32)
        for begin in range(0, length, BLOCK):
            block = x_ref[:, trace, :, begin : begin + BLOCK]
            flipped = block.reshape(sources * local, BLOCK).T.astype(F32)
            value = mixed_half(flipped, begin, dw_turned_ref, half, held)
            silu = value + value * jnp.tanh(value)
            total = total + jnp.sum(silu.reshape(BLOCK // SUBLANES, SUBLANES, filters), 0)
        rows.append(jnp.sum(total, 0, keepdims=True) / length)
    rows = jnp.concatenate(rows, 0).astype(BF16)
    message_ref[...] = jnp.broadcast_to(rows[None], message_ref.shape)


def pool_pass(traces, dw_turned, pw_weight, devices):
    sources, pair, local, length = traces.shape
    filters, metrics = pw_weight.shape
    whole = pl.BlockSpec(memory_space=pltpu.VMEM)
    return pl.pallas_call(
        pool_kernel,
        in_specs=[whole] * 3,
        out_specs=whole,
        out_shape=jax.ShapeDtypeStruct((devices, pair, filters), BF16),
        scratch_shapes=[pltpu.VMEM((pair, length + RIM, metrics), F32)],
        compiler_params=pltpu.CompilerParams(vmem_limit_bytes=12 << 20),
    )(traces, dw_turned, pw_weight)


def terms_kernel(x_ref, dw_turned_ref, pw_ref, terms_ref, turned, slope, plain):
    sources, pair, local, length = x_ref.shape
    metrics = sources * local
    half = pw_ref[...] * 0.5
    for trace in range(pair):
        held = turned.at[trace]
        bends = slope.at[trace]
        flat = plain.at[trace]
        held[0:RIM, :] = jnp.zeros((RIM, metrics), F32)
        bends[length : length + RIM, :] = jnp.zeros((RIM, bends.shape[1]), BF16)
        for begin in range(0, length, BLOCK):
            block = x_ref[:, trace, :, begin : begin + BLOCK].reshape(metrics, BLOCK)
            flat[:, begin : begin + BLOCK] = block
            value = mixed_half(block.T.astype(F32), begin, dw_turned_ref, half, held)
            bent = jnp.tanh(value)
            bends[begin : begin + BLOCK, :] = (
                (1.0 + bent) * (1.0 + value * (1.0 - bent))
            ).astype(BF16)
        for tap in range(TAPS):
            first = tap * TAP_SPACING
            terms_ref[trace, tap * metrics : (tap + 1) * metrics, :] = jnp.dot(
                flat[...], bends[first : first + length, :], preferred_element_type=F32
            )


def terms_pass(traces, dw_turned, pw_weight):
    sources, pair, local, length = traces.shape
    filters, metrics = pw_weight.shape
    whole = pl.BlockSpec(memory_space=pltpu.VMEM)
    return pl.pallas_call(
        terms_kernel,
        in_specs=[whole] * 3,
        out_specs=whole,
        out_shape=jax.ShapeDtypeStruct((pair, metrics * TAPS, filters), F32),
        scratch_shapes=[
            pltpu.VMEM((pair, length + RIM, metrics), F32),
            pltpu.VMEM((pair, length + RIM, filters), BF16),
            pltpu.VMEM((pair, metrics, length), BF16),
        ],
        compiler_params=pltpu.CompilerParams(vmem_limit_bytes=24 << 20),
    )(traces, dw_turned, pw_weight)


def middle_kernel(
    length, own_ref, pooled_ref, partner_ref, proj_ref, dw_ref, pw_turned_ref, terms_ref,
    loss_ref, grad_a_ref, grad_v_ref, sums_ref, held_a, held_v,
):
    filters, width = proj_ref.shape
    count = pooled_ref.shape[0]
    metrics = pw_turned_ref.shape[0]
    factor = LOGIT_SCALE / width
    proj = proj_ref[...]

    def normed(pooled):
        embedding = jnp.dot(pooled, proj, preferred_element_type=F32)
        inverse = lax.rsqrt(jnp.mean(embedding * embedding, 1, keepdims=True) + 1e-06)
        return embedding * inverse, inverse

    unit_a, inverse_a = normed(pooled_ref[:, 0:filters])
    unit_v, inverse_v = normed(pooled_ref[:, filters : 2 * filters])
    queries = unit_a.astype(BF16)
    keys = unit_v.astype(BF16)
    logits = factor * lax.dot_general(
        queries, keys, (((1,), (1,)), ((), ())), preferred_element_type=F32
    )
    columns = lax.broadcasted_iota(jnp.int32, (count, count), 1)
    matches = columns == partner_ref[...]
    weights = jnp.exp(logits - LOGIT_SCALE)
    totals = jnp.sum(weights, 1, keepdims=True)
    positive = jnp.sum(jnp.where(matches, logits, 0.0), 1, keepdims=True)
    loss_ref[...] = LOGIT_SCALE + jnp.log(totals) - positive
    coeffs = (weights / totals - jnp.where(matches, 1.0, 0.0)).astype(BF16)
    unit_grad_a = factor * jnp.dot(coeffs, keys, preferred_element_type=F32)
    unit_grad_v = factor * lax.dot_general(
        coeffs, queries, (((0,), (0,)), ((), ())), preferred_element_type=F32
    )
    own = own_ref[0]

    def pool_grad(unit, inverse, unit_grad, out_ref, held):
        grad = inverse * (unit_grad - unit * jnp.mean(unit * unit_grad, 1, keepdims=True))
        grad = grad.astype(BF16)
        out_ref[...] = grad
        held[...] = grad.astype(F32)
        row = jnp.broadcast_to(held[pl.ds(own, 1), :], (16, width)).astype(BF16)
        pool = lax.dot_general(row, proj, (((1,), (1,)), ((), ())), preferred_element_type=F32)
        return pool[0:1, :] * (0.5 / length)

    pool_a = pool_grad(unit_a, inverse_a, unit_grad_a, grad_a_ref, held_a)
    pool_v = pool_grad(unit_v, inverse_v, unit_grad_v, grad_v_ref, held_v)

    pw_turned = pw_turned_ref[...].astype(F32)
    lanes = lax.broadcasted_iota(jnp.int32, (metrics, LANES), 1)
    mixing = jnp.zeros((metrics, filters), F32)
    kernel = jnp.zeros((metrics, LANES), F32)
    for tap in range(TAPS):
        rows = pl.ds(tap * metrics, metrics)
        weighted = terms_ref[0, rows, :] * pool_a + terms_ref[1, rows, :] * pool_v
        mixing = mixing + dw_ref[:, tap : tap + 1] * weighted
        column = jnp.sum(pw_turned * weighted, 1, keepdims=True)
        kernel = kernel + jnp.where(lanes == tap, column, 0.0)
    mixing = mixing.T
    kernel = kernel.T
    parts = sums_ref.shape[0]
    mix_rows = filters // parts
    for part in range(parts):
        for row in range(mix_rows):
            sums_ref[part, 0:1, row * LANES : (row + 1) * LANES] = mixing[
                part * mix_rows + row : part * mix_rows + row + 1, :
            ]
        sums_ref[part, 0:1, mix_rows * LANES :] = kernel[part : part + 1, :]


def middle(own, pooled, partners, proj_weight, dw_weight, pw_turned, terms, parts, length):
    filters, width = proj_weight.shape
    metrics = pw_turned.shape[0]
    count = pooled.shape[0]
    whole = pl.BlockSpec(memory_space=pltpu.VMEM)
    packed = (filters // parts + 1) * metrics
    return pl.pallas_call(
        functools.partial(middle_kernel, length),
        in_specs=[pl.BlockSpec(memory_space=pltpu.SMEM)] + [whole] * 6,
        out_specs=[whole] * 4,
        out_shape=[
            jax.ShapeDtypeStruct((count, 1), F32),
            jax.ShapeDtypeStruct((count, width), BF16),
            jax.ShapeDtypeStruct((count, width), BF16),
            jax.ShapeDtypeStruct((parts, 1, packed), F32),
        ],
        scratch_shapes=[pltpu.VMEM((count, width), F32), pltpu.VMEM((count, width), F32)],
        compiler_params=pltpu.CompilerParams(vmem_limit_bytes=24 << 20),
    )(own, pooled, partners, proj_weight, dw_weight, pw_turned, terms)


def swap(value, axis):
    return lax.all_to_all(value, axis, 0, 0, tiled=True)


def fold_kernel(parts_ref, out_ref):
    out_ref[...] = jnp.broadcast_to(jnp.sum(parts_ref[...], 0)[None], out_ref.shape)


def fold(parts, copies):
    whole = pl.BlockSpec(memory_space=pltpu.VMEM)
    return pl.pallas_call(
        fold_kernel,
        in_specs=[whole],
        out_specs=whole,
        out_shape=jax.ShapeDtypeStruct((copies,) + parts.shape[1:], F32),
        compiler_params=pltpu.CompilerParams(vmem_limit_bytes=4 << 20),
    )(parts)


def unpack_kernel(index_ref, shares_ref, mix_ref, tap_ref):
    parts = shares_ref.shape[0]
    mix_rows = mix_ref.shape[0] // parts
    taps, local = tap_ref.shape
    for part in range(parts):
        for row in range(mix_rows):
            mix_ref[part * mix_rows + row : part * mix_rows + row + 1, :] = shares_ref[
                part, 0:1, row * LANES : (row + 1) * LANES
            ]
    back = lax.rem(LANES - index_ref[0] * local, LANES)
    rows = jnp.concatenate(
        [shares_ref[tap, 0:1, mix_rows * LANES :] for tap in range(taps)] * (SUBLANES // taps), 0
    )
    tap_ref[...] = pltpu.roll(rows, back, 1)[0:taps, 0:local]


def unpack(chan_index, shares, filters, local_metrics):
    whole = pl.BlockSpec(memory_space=pltpu.VMEM)
    return pl.pallas_call(
        unpack_kernel,
        in_specs=[pl.BlockSpec(memory_space=pltpu.SMEM), whole],
        out_specs=[whole, whole],
        out_shape=[
            jax.ShapeDtypeStruct((filters, LANES), F32),
            jax.ShapeDtypeStruct((TAPS, local_metrics), F32),
        ],
        compiler_params=pltpu.CompilerParams(vmem_limit_bytes=4 << 20),
    )(chan_index.astype(jnp.int32).reshape(1), shares)


def body(anchors, views, dw_weight, pw_weight, proj_weight, partner):
    chan_index = lax.axis_index("chan")
    dp_index = lax.axis_index("dp")
    chan_count = lax.axis_size("chan")
    dp_count = lax.axis_size("dp")
    pairs, local_metrics, length = anchors.shape
    filters, metrics = pw_weight.shape
    width = proj_weight.shape[1]
    dw_turned = dw_weight.T

    traces = swap(jnp.stack([anchors, views], 1), "chan")
    message = pool_pass(traces, dw_turned, pw_weight, dp_count * chan_count)
    message, partner, pw_later = lax.optimization_barrier((message, partner, pw_weight))
    partners = lax.dynamic_update_slice_in_dim(
        jnp.zeros((dp_count, pairs), jnp.int32), partner[None], dp_index, 0
    )
    bit = 1
    while bit < dp_count:
        partners += lax.ppermute(partners, "dp", [(i, i ^ bit) for i in range(dp_count)])
        bit *= 2
    partners = partners.reshape(pairs * dp_count, 1)
    pooled = swap(message, ("dp", "chan")).reshape(message.shape[0], -1)
    terms = terms_pass(traces, dw_turned, pw_weight)
    own = (dp_index * chan_count + chan_index).astype(jnp.int32).reshape(1)
    losses, grad_a, grad_v, sums = middle(
        own, pooled, partners, proj_weight, dw_weight, pw_later.T, terms, dp_count, length
    )

    shares = fold(swap(sums, "dp"), chan_count)
    shares = fold(swap(shares, "chan"), dp_count)
    grad_pw, grad_dw = unpack(chan_index, swap(shares, "dp"), filters, local_metrics)

    cols = width // dp_count
    rows = filters // chan_count

    def proj_part(offset, grad):
        features = lax.dynamic_slice_in_dim(pooled, offset + chan_index * rows, rows, 1)
        part = lax.dynamic_slice_in_dim(grad, dp_index * cols, cols, 1)
        return lax.dot_general(
            features, part, (((0,), (0,)), ((), ())), preferred_element_type=F32
        )

    grad_proj = proj_part(0, grad_a) + proj_part(filters, grad_v)
    loss = lax.dynamic_slice_in_dim(losses, dp_index * pairs, pairs, 0).reshape(pairs)
    return (loss, grad_dw.T, grad_pw, grad_proj)


def solution(mesh):
    placed = (P("dp", "chan", None), P("dp", "chan", None), P(), P(), P(), P("dp"))
    return jax.shard_map(
        body,
        mesh=mesh,
        in_specs=placed,
        out_specs=(P("dp"), P("chan", None), P(), P("chan", "dp")),
        check_vma=False,
    )
```

time: 136 us -> 144 us (1.059)
  blocking collectives: 9.87 us -> 72.4 us
  waiting for transfers between devices: 67 us -> 20.7 us
  starting transfers between devices: 37.3 us -> 30.2 us
    all_to_all x1 -> x2, blocking collectives: 9.87 us -> 72.4 us  [swap(): return lax.all_to_all(value, axis, 0, 0, tiled=True)]
    all_to_all x4 -> x3, waiting for transfers between devices: 61.3 us -> 13.4 us  [swap(): return lax.all_to_all(value, axis, 0, 0, tiled=True)]
    all_to_all x4 -> x3, starting transfers between devices: 31.8 us -> 26.7 us  [swap(): return lax.all_to_all(value, axis, 0, 0, tiled=True)]
    ppermute x4, starting transfers between devices: 5.47 us -> 3.41 us  [body(): lax.ppermute(partners, 'dp', [(i, i ^ bit) for i in range(dp_count)])]
    ppermute x4, waiting for transfers between devices: 5.68 us -> 7.24 us  [body(): lax.ppermute(partners, 'dp', [(i, i ^ bit) for i in range(dp_count)])]
  transfers between devices with their start and end apart: 8 -> 7, of which waited for: 8 -> 5; matrix products, arithmetic and copies ran while one was open for 2% -> 1% of each run, Pallas kernels for 4% -> 3%
where the time goes in v4:
time: 144 us; the launch traced here: 143 us
  blocking collectives  72.4 us (50%)
  starting transfers between devices  30.2 us (21%)
  waiting for transfers between devices  20.7 us (14%)
  Pallas kernels  13.1 us (9%)
  local copies, waits for them, and re-layouts  3.05 us (2%)
  other arithmetic  1.75 us (1%)
    all_to_all x2, blocking collectives, swap(): return lax.all_to_all(value, axis, 0, 0, tiled=True)  72.4 us
    all_to_all x3, starting transfers between devices, swap(): return lax.all_to_all(value, axis, 0, 0, tiled=True)  26.7 us
    all_to_all x3, waiting for transfers between devices, swap(): return lax.all_to_all(value, axis, 0, 0, tiled=True)  13.4 us
    ppermute x4, waiting for transfers between devices, body(): lax.ppermute(partners, 'dp', [(i, i ^ bit) for i in range(dp_count)])  7.24 us
    pallas_call x1, Pallas kernels, terms_pass(): pl.pallas_call(terms_kernel, in_specs=[whole] * 3, out_specs=whole, out_s...  4.98 us
    ppermute x4, starting transfers between devices, body(): lax.ppermute(partners, 'dp', [(i, i ^ bit) for i in range(dp_count)])  3.41 us
    pallas_call x1, Pallas kernels, pool_pass(): pl.pallas_call(pool_kernel, in_specs=[whole] * 3, out_specs=whole, out_sh...  3.37 us
  transfers between devices with their start and end apart: 7, of which 5 were waited for; matrix products, arithmetic and copies ran while one was open for 1% of the time, Pallas kernels for 3%

profile of v4, /device:TPU:1, one launch (start us, length us, event | category | flops | bytes accessed | tf_op | source)
XLA Modules:
  0.0 143.1 jit_solution(3713967146163350977)
XLA Ops:
  0.6 1.7 %pad_maximum_fusion = bf16[16,2,8,4096]{3,2,1,0:T(8,128)(2,1)S(1)} fusion(bf16[16,1,8,4096]{3,2,1,0:T(8,128)(2,1)} %bitcast.17, bf16[16,1,8,4096]{3,2,1,0:T(8,128)(2,1)} %bitcast.18), kind=kLoop, calls=%fused_computation | loop fusion | flops 1048576 | bytes 4194304 | tf_op jit(solution)/shard_map/stack | solution.py:259
  2.4 0.0 copy-start
  2.4 0.0 copy-start.2
  2.4 60.6 %all_to_all.25.x_ref = bf16[16,2,8,4096]{3,2,1,0:T(8,128)(2,1)S(1)} all-to-all(bf16[16,2,8,4096]{3,2,1,0:T(8,128)(2,1)S(1)} %pad_maximum_fusion), channel_id=1, replica_groups=mesh['dp'=16,'chan'=16] {'chan'}, dimensions={0} | all-to-all | bytes 4194304 | tf_op jit(solution)/shard_map/all_to_all | solution.py:201
  63.0 0.0 copy-start.3
  63.0 0.0 copy-done
  63.0 0.0 copy-done.2
  63.0 3.4 %shard_map.93 = bf16[256,2,256]{2,1,0:T(2,128)(2,1)} custom-call(bf16[16,2,8,4096]{3,2,1,0:T(8,128)(2,1)S(1)} %all_to_all.25.x_ref, f32[4,128]{1,0:T(4,128)S(1)} %bitcast.15, bf16[256,128]{1,0:T(8,128)(2,1)S(1)} %copy-done), custom_call_target="tpu_custom_call" | custom-call | tf_op jit(solution)/shard_map/pallas_call | solution.py:57
  66.4 11.4 %all-to-all-start.1 = ((bf16[256,2,256]{2,1,0:T(2,128)(2,1)}), bf16[256,2,256]{2,1,0:T(2,128)(2,1)}, u32[]{:S(2)}, u32[]{:S(2)}) async-start(bf16[256,2,256]{2,1,0:T(2,128)(2,1)} %shard_map.93), calls=%async_computation.1 | async-start | bytes 524288 | tf_op jit(solution)/shard_map/all_to_all | solution.py:201
  77.8 0.0 copy-done.3
  77.9 2.3 %collective-permute-start = (s32[16,16]{1,0:T(8,128)S(1)}, s32[16,16]{1,0:T(8,128)S(1)}, u32[]{:S(2)}, u32[]{:S(2)}) collective-permute-start(s32[16,16]{1,0:T(8,128)S(1)} %dynamic_update_slice.5), channel_id=1, source_target_pairs={{0,16},{16,0},{32,48},{48,32},{64,80},{80,64},{96,112},{112,96},{1... | collective-permute-start | bytes 3080 | tf_op jit(solution)/shard_map/ppermute | solution.py:267
  80.2 0.8 collective-permute-done
  81.1 0.1 collective-permute-start.1
  81.1 3.0 %collective-permute-done.1 = s32[16,16]{1,0:T(8,128)S(1)} collective-permute-done((s32[16,16]{1,0:T(8,128)S(1)}, s32[16,16]{1,0:T(8,128)S(1)}, u32[]{:S(2)}, u32[]{:S(2)}) %collective-permute-start.1) | collective-permute-done | bytes 1056 | tf_op jit(solution)/shard_map/ppermute | solution.py:267
  84.1 1.0 collective-permute-start.2
  85.2 3.4 %collective-permute-done.2 = s32[16,16]{1,0:T(8,128)S(1)} collective-permute-done((s32[16,16]{1,0:T(8,128)S(1)}, s32[16,16]{1,0:T(8,128)S(1)}, u32[]{:S(2)}, u32[]{:S(2)}) %collective-permute-start.2) | collective-permute-done | bytes 1056 | tf_op jit(solution)/shard_map/ppermute | solution.py:267
  88.6 0.0 collective-permute-start.3
  88.6 0.1 copy.14.dw_ref
  88.7 0.1 copy.12
  88.8 5.0 %shard_map.94.terms_ref = f32[2,512,256]{2,1,0:T(8,128)S(1)} custom-call(bf16[16,2,8,4096]{3,2,1,0:T(8,128)(2,1)S(1)} %all_to_all.25.x_ref, f32[4,128]{1,0:T(4,128)S(1)} %bitcast.16, bf16[256,128]{1,0:T(8,128)(2,1)S(1)} %copy-done), custom_call_target="tpu_custom_call" | custom-call | tf_op jit(solution)/shard_map/pallas_call | solution.py:96
  93.8 0.0 collective-permute-done.3
  93.8 0.1 reshape.28.partner_ref
  93.9 0.0 all-to-all-done.1
  93.9 1.0 copy.15
  94.9 0.0 copy-start.1
  94.9 1.0 copy-done.1
  96.0 2.6 %shard_map.95 = (f32[256,1]{1,0:T(8,128)S(1)}, bf16[256,1024]{1,0:T(8,128)(2,1)S(1)}, bf16[256,1024]{1,0:T(8,128)(2,1)S(1)}, f32[16,1,2176]{2,1,0:T(1,128)S(1)}) custom-call(s32[1]{0:T(128)} %bitcast.own_ref, bf16[256,512]{1,0:T(8,128)(2,1)S(1)} %bitcast.11, s32[256,1]{1,0:T(8,128)S(1)} %reshape.28.partner_ref, bf16[256,1024]{1,0:T(8,128)(2,1)S(1)} %copy-done.1, ...), custom_call_target="tpu_custom_call" | custom-call | tf_op jit(solution)/shard_map/pallas_call | solution.py:185
  98.6 11.8 %all_to_all.26.parts_ref = f32[16,1,2176]{2,1,0:T(1,128)S(1)} all-to-all(f32[16,1,2176]{2,1,0:T(1,128)S(1)} %get-tuple-element.17), channel_id=1, replica_groups=mesh['dp'=16,'chan'=16] {'dp'}, dimensions={0} | all-to-all | bytes 278528 | tf_op jit(solution)/shard_map/all_to_all | solution.py:201
  110.4 0.7 shard_map.96
  111.2 9.9 %all-to-all-start.3 = ((f32[16,1,2176]{2,1,0:T(1,128)}), f32[16,1,2176]{2,1,0:T(1,128)S(1)}, u32[]{:S(2)}, u32[]{:S(2)}) async-start(f32[16,1,2176]{2,1,0:T(1,128)} %shard_map.96), calls=%async_computation.3 | async-start | bytes 278528 | tf_op jit(solution)/shard_map/all_to_all | solution.py:201
  121.1 0.6 dynamic-slice_reduce_fusion
  121.7 0.2 fusion.2
  121.9 8.1 %all-to-all-done.3.parts_ref = f32[16,1,2176]{2,1,0:T(1,128)S(1)} async-done(((f32[16,1,2176]{2,1,0:T(1,128)}), f32[16,1,2176]{2,1,0:T(1,128)S(1)}, u32[]{:S(2)}, u32[]{:S(2)}) %all-to-all-start.3) | async-done | bytes 139296 | tf_op jit(solution)/shard_map/all_to_all | solution.py:201
  130.0 0.7 shard_map.97
  130.7 5.4 %all-to-all-start.4 = ((f32[16,1,2176]{2,1,0:T(1,128)}), f32[16,1,2176]{2,1,0:T(1,128)S(1)}, u32[]{:S(2)}, u32[]{:S(2)}) async-start(f32[16,1,2176]{2,1,0:T(1,128)} %shard_map.97), calls=%async_computation.4 | async-start | bytes 278528 | tf_op jit(solution)/shard_map/all_to_all | solution.py:201
  136.2 0.8 convolution_add_fusion
  137.0 5.4 %all-to-all-done.4.shares_ref = f32[16,1,2176]{2,1,0:T(1,128)S(1)} async-done(((f32[16,1,2176]{2,1,0:T(1,128)}), f32[16,1,2176]{2,1,0:T(1,128)S(1)}, u32[]{:S(2)}, u32[]{:S(2)}) %all-to-all-start.4) | async-done | bytes 139296 | tf_op jit(solution)/shard_map/all_to_all | solution.py:201
  142.4 0.7 shard_map.98
  (7 shorter events, 0.1 us)
Async XLA Ops:
  2.4 60.6 %copy-start = (bf16[256,128]{1,0:T(8,128)(2,1)S(1)}, bf16[256,128]{1,0:T(8,128)(2,1)}, u32[]{:S(2)}) copy-start(bf16[256,128]{1,0:T(8,128)(2,1)} %pw_ref.3) | copy-start | bytes 196612
  2.4 60.6 %copy-start.2 = (f32[128,4]{0,1:T(4,128)S(1)}, f32[128,4]{0,1:T(4,128)}, u32[]{:S(2)}) copy-start(f32[128,4]{0,1:T(4,128)} %param.8) | copy-start | bytes 6148
  63.0 14.8 %copy-start.3 = (s32[16]{0:T(128)S(1)}, s32[16]{0:T(128)}, u32[]{:S(2)}) copy-start(s32[16]{0:T(128)} %param.11) | copy-start | bytes 196
  66.4 27.5 %all-to-all-start.1 = ((bf16[256,2,256]{2,1,0:T(2,128)(2,1)}), bf16[256,2,256]{2,1,0:T(2,128)(2,1)}, u32[]{:S(2)}, u32[]{:S(2)}) async-start(bf16[256,2,256]{2,1,0:T(2,128)(2,1)} %shard_map.93), calls=%async_computation.1 | async-start | bytes 524288 | tf_op jit(solution)/shard_map/all_to_all | solution.py:201
  77.9 3.1 %collective-permute-start = (s32[16,16]{1,0:T(8,128)S(1)}, s32[16,16]{1,0:T(8,128)S(1)}, u32[]{:S(2)}, u32[]{:S(2)}) collective-permute-start(s32[16,16]{1,0:T(8,128)S(1)} %dynamic_update_slice.5), channel_id=1, source_target_pairs={{0,16},{16,0},{32,48},{48,32},{64,80},{80,64},{96,112},{112,96},{1... | collective-permute-start | bytes 3080 | tf_op jit(solution)/shard_map/ppermute | solution.py:267
  81.1 3.1 %collective-permute-start.1 = (s32[16,16]{1,0:T(8,128)S(1)}, s32[16,16]{1,0:T(8,128)S(1)}, u32[]{:S(2)}, u32[]{:S(2)}) collective-permute-start(s32[16,16]{1,0:T(8,128)S(1)} %add.42), channel_id=1, source_target_pairs={{0,32},{16,48},{32,0},{48,16},{64,96},{80,112},{96,64},{112,80},{1... | collective-permute-start | bytes 3080 | tf_op jit(solution)/shard_map/ppermute | solution.py:267
  84.1 4.4 %collective-permute-start.2 = (s32[16,16]{1,0:T(8,128)S(1)}, s32[16,16]{1,0:T(8,128)S(1)}, u32[]{:S(2)}, u32[]{:S(2)}) collective-permute-start(s32[16,16]{1,0:T(8,128)S(1)} %add.43), channel_id=1, source_target_pairs={{0,64},{16,80},{32,96},{48,112},{64,0},{80,16},{96,32},{112,48},{1... | collective-permute-start | bytes 3080 | tf_op jit(solution)/shard_map/ppermute | solution.py:267
  88.6 5.2 %collective-permute-start.3 = (s32[16,16]{1,0:T(8,128)S(1)}, s32[16,16]{1,0:T(8,128)S(1)}, u32[]{:S(2)}, u32[]{:S(2)}) collective-permute-start(s32[16,16]{1,0:T(8,128)S(1)} %add.44), channel_id=1, source_target_pairs={{0,128},{16,144},{32,160},{48,176},{64,192},{80,208},{96,224},{112... | collective-permute-start | bytes 3080 | tf_op jit(solution)/shard_map/ppermute | solution.py:267
  94.9 1.0 copy-start.1
  111.2 18.8 %all-to-all-start.3 = ((f32[16,1,2176]{2,1,0:T(1,128)}), f32[16,1,2176]{2,1,0:T(1,128)S(1)}, u32[]{:S(2)}, u32[]{:S(2)}) async-start(f32[16,1,2176]{2,1,0:T(1,128)} %shard_map.96), calls=%async_computation.3 | async-start | bytes 278528 | tf_op jit(solution)/shard_map/all_to_all | solution.py:201
  130.7 11.7 %all-to-all-start.4 = ((f32[16,1,2176]{2,1,0:T(1,128)}), f32[16,1,2176]{2,1,0:T(1,128)S(1)}, u32[]{:S(2)}, u32[]{:S(2)}) async-start(f32[16,1,2176]{2,1,0:T(1,128)} %shard_map.97), calls=%async_computation.4 | async-start | bytes 278528 | tf_op jit(solution)/shard_map/all_to_all | solution.py:201

commit v5 on v4

--- a/solution.py
+++ b/solution.py
@@ -25,18 +25,16 @@
     for tap in range(1, TAPS):
         first = RIM + begin - tap * TAP_SPACING
         running = running + dw_turned_ref[tap : tap + 1, :] * turned[first : first + steps, :]
-    return lax.dot_general(
-        running.astype(BF16), half, (((1,), (1,)), ((), ())), preferred_element_type=F32
-    )
-
-
-def pool_kernel(x_ref, dw_turned_ref, pw_ref, message_ref, turned):
+    return jnp.dot(running.astype(BF16), half, preferred_element_type=F32)
+
+
+def pool_kernel(x_ref, dw_turned_ref, pw_turned_ref, message_ref, turned):
     sources, pair, local, length = x_ref.shape
-    filters = pw_ref.shape[0]
-    half = pw_ref[...] * 0.5
+    filters = pw_turned_ref.shape[1]
+    half = pw_turned_ref[...] * 0.5
     rows = []
     for trace in range(pair):
-        held = turned.at[trace]
+        held = turned
         held[0:RIM, :] = jnp.zeros((RIM, sources * local), F32)
         total = jnp.zeros((SUBLANES, filters), F32)
         for begin in range(0, length, BLOCK):
@@ -50,28 +48,26 @@
     message_ref[...] = jnp.broadcast_to(rows[None], message_ref.shape)
 
 
-def pool_pass(traces, dw_turned, pw_weight, devices):
+def pool_pass(traces, dw_turned, pw_turned, devices):
     sources, pair, local, length = traces.shape
-    filters, metrics = pw_weight.shape
+    metrics, filters = pw_turned.shape
     whole = pl.BlockSpec(memory_space=pltpu.VMEM)
     return pl.pallas_call(
         pool_kernel,
         in_specs=[whole] * 3,
         out_specs=whole,
         out_shape=jax.ShapeDtypeStruct((devices, pair, filters), BF16),
-        scratch_shapes=[pltpu.VMEM((pair, length + RIM, metrics), F32)],
-        compiler_params=pltpu.CompilerParams(vmem_limit_bytes=12 << 20),
-    )(traces, dw_turned, pw_weight)
-
-
-def terms_kernel(x_ref, dw_turned_ref, pw_ref, terms_ref, turned, slope, plain):
+        scratch_shapes=[pltpu.VMEM((length + RIM, metrics), F32)],
+        compiler_params=pltpu.CompilerParams(vmem_limit_bytes=8 << 20),
+    )(traces, dw_turned, pw_turned)
+
+
+def terms_kernel(x_ref, dw_turned_ref, pw_turned_ref, terms_ref, turned, slope, plain):
     sources, pair, local, length = x_ref.shape
     metrics = sources * local
-    half = pw_ref[...] * 0.5
+    half = pw_turned_ref[...] * 0.5
     for trace in range(pair):
-        held = turned.at[trace]
-        bends = slope.at[trace]
-        flat = plain.at[trace]
+        held, bends, flat = turned, slope, plain
         held[0:RIM, :] = jnp.zeros((RIM, metrics), F32)
         bends[length : length + RIM, :] = jnp.zeros((RIM, bends.shape[1]), BF16)
         for begin in range(0, length, BLOCK):
@@ -89,9 +85,9 @@
             )
 
 
-def terms_pass(traces, dw_turned, pw_weight):
+def terms_pass(traces, dw_turned, pw_turned):
     sources, pair, local, length = traces.shape
-    filters, metrics = pw_weight.shape
+    metrics, filters = pw_turned.shape
     whole = pl.BlockSpec(memory_space=pltpu.VMEM)
     return pl.pallas_call(
         terms_kernel,
@@ -99,12 +95,12 @@
         out_specs=whole,
         out_shape=jax.ShapeDtypeStruct((pair, metrics * TAPS, filters), F32),
         scratch_shapes=[
-            pltpu.VMEM((pair, length + RIM, metrics), F32),
-            pltpu.VMEM((pair, length + RIM, filters), BF16),
-            pltpu.VMEM((pair, metrics, length), BF16),
+            pltpu.VMEM((length + RIM, metrics), F32),
+            pltpu.VMEM((length + RIM, filters), BF16),
+            pltpu.VMEM((metrics, length), BF16),
         ],
-        compiler_params=pltpu.CompilerParams(vmem_limit_bytes=24 << 20),
-    )(traces, dw_turned, pw_weight)
+        compiler_params=pltpu.CompilerParams(vmem_limit_bytes=12 << 20),
+    )(traces, dw_turned, pw_turned)
 
 
 def middle_kernel(
@@ -254,11 +250,8 @@
     pairs, local_metrics, length = anchors.shape
     filters, metrics = pw_weight.shape
     width = proj_weight.shape[1]
-    dw_turned = dw_weight.T
-
-    traces = swap(jnp.stack([anchors, views], 1), "chan")
-    message = pool_pass(traces, dw_turned, pw_weight, dp_count * chan_count)
-    message, partner, pw_later = lax.optimization_barrier((message, partner, pw_weight))
+    dw_turned, pw_turned = dw_weight.T, pw_weight.T
+
     partners = lax.dynamic_update_slice_in_dim(
         jnp.zeros((dp_count, pairs), jnp.int32), partner[None], dp_index, 0
     )
@@ -267,11 +260,14 @@
         partners += lax.ppermute(partners, "dp", [(i, i ^ bit) for i in range(dp_count)])
         bit *= 2
     partners = partners.reshape(pairs * dp_count, 1)
+    traces = swap(jnp.stack([anchors, views], 1), "chan")
+    traces, partners = lax.optimization_barrier((traces, partners))
+    message = pool_pass(traces, dw_turned, pw_turned, dp_count * chan_count)
     pooled = swap(message, ("dp", "chan")).reshape(message.shape[0], -1)
-    terms = terms_pass(traces, dw_turned, pw_weight)
+    terms = terms_pass(traces, dw_turned, pw_turned)
     own = (dp_index * chan_count + chan_index).astype(jnp.int32).reshape(1)
     losses, grad_a, grad_v, sums = middle(
-        own, pooled, partners, proj_weight, dw_weight, pw_later.T, terms, dp_count, length
+        own, pooled, partners, proj_weight, dw_weight, pw_turned, terms, dp_count, length
     )
 
     shares = fold(swap(sums, "dp"), chan_count)

time: 144 us -> 134 us (0.931)
  blocking collectives: 72.4 us -> 9.37 us
  waiting for transfers between devices: 20.7 us -> 67.2 us
  starting transfers between devices: 30.2 us -> 36.9 us
    all_to_all x2 -> x1, blocking collectives: 72.4 us -> 9.37 us  [swap(): return lax.all_to_all(value, axis, 0, 0, tiled=True)]
    all_to_all x3 -> x4, waiting for transfers between devices: 13.4 us -> 61.5 us  [swap(): return lax.all_to_all(value, axis, 0, 0, tiled=True)]
    all_to_all x3 -> x4, starting transfers between devices: 26.7 us -> 31.4 us  [swap(): return lax.all_to_all(value, axis, 0, 0, tiled=True)]
    ppermute x4, starting transfers between devices: 3.41 us -> 5.47 us  [body(): lax.ppermute(partners, 'dp', [(i, i ^ bit) for i in range(dp_count)])]
    ppermute x4, waiting for transfers between devices: 7.24 us -> 5.68 us  [body(): lax.ppermute(partners, 'dp', [(i, i ^ bit) for i in range(dp_count)])]
  transfers between devices with their start and end apart: 7 -> 8, of which waited for: 5 -> 8; matrix products, arithmetic and copies ran while one was open for 1% -> 2% of each run, Pallas kernels for 3% -> 4%
where the time goes in v5:
time: 134 us
  waiting for transfers between devices  67.2 us (50%)
  starting transfers between devices  36.9 us (28%)
  Pallas kernels  13.1 us (10%)
  blocking collectives  9.37 us (7%)
  other arithmetic  3.09 us (2%)
  local copies, waits for them, and re-layouts  2.21 us (2%)
    all_to_all x4, waiting for transfers between devices, swap(): return lax.all_to_all(value, axis, 0, 0, tiled=True)  61.5 us
    all_to_all x4, starting transfers between devices, swap(): return lax.all_to_all(value, axis, 0, 0, tiled=True)  31.4 us
    all_to_all x1, blocking collectives, swap(): return lax.all_to_all(value, axis, 0, 0, tiled=True)  9.37 us
    ppermute x4, waiting for transfers between devices, body(): lax.ppermute(partners, 'dp', [(i, i ^ bit) for i in range(dp_count)])  5.68 us
    ppermute x4, starting transfers between devices, body(): lax.ppermute(partners, 'dp', [(i, i ^ bit) for i in range(dp_count)])  5.47 us
    pallas_call x1, Pallas kernels, terms_pass(): pl.pallas_call(terms_kernel, in_specs=[whole] * 3, out_specs=whole, out_s...  4.87 us
    pallas_call x1, Pallas kernels, pool_pass(): pl.pallas_call(pool_kernel, in_specs=[whole] * 3, out_specs=whole, out_sh...  3.4 us
    another operation x1, other arithmetic, body(): traces = swap(jnp.stack([anchors, views], 1), 'chan')  3.07 us
  transfers between devices with their start and end apart: 8, of which 8 were waited for; matrix products, arithmetic and copies ran while one was open for 2% of the time, Pallas kernels for 4%

profile of v5, /device:TPU:1, one launch (start us, length us, event | category | flops | bytes accessed | tf_op | source)
XLA Modules:
  0.0 133.7 jit_solution(5162868109830303504)
XLA Ops:
  0.6 3.1 %pad_maximum_fusion = bf16[16,2,8,4096]{3,2,1,0:T(8,128)(2,1)} fusion(bf16[16,1,8,4096]{3,2,1,0:T(8,128)(2,1)} %bitcast.20, bf16[16,1,8,4096]{3,2,1,0:T(8,128)(2,1)} %bitcast.21), kind=kLoop, calls=%fused_computation | loop fusion | flops 1048576 | bytes 4194304 | tf_op jit(solution)/shard_map/stack | solution.py:263
  3.7 0.0 copy-start.3
  3.7 0.0 copy-start.2
  3.7 0.0 copy-start.1
  3.7 11.9 %all-to-all-start = ((bf16[16,2,8,4096]{3,2,1,0:T(8,128)(2,1)}), bf16[16,2,8,4096]{3,2,1,0:T(8,128)(2,1)S(1)}, u32[]{:S(2)}, u32[]{:S(2)}) async-start(bf16[16,2,8,4096]{3,2,1,0:T(8,128)(2,1)} %pad_maximum_fusion), calls=%async_computation | async-start | bytes 4194304 | tf_op jit(solution)/shard_map/all_to_all | solution.py:197
  15.6 0.0 copy-done.3
  15.7 1.0 collective-permute-start
  16.7 0.8 collective-permute-done
  17.6 1.3 collective-permute-start.1
  18.9 1.3 collective-permute-done.1
  20.1 2.7 %collective-permute-start.2 = (s32[16,16]{1,0:T(8,128)S(1)}, s32[16,16]{1,0:T(8,128)S(1)}, u32[]{:S(2)}, u32[]{:S(2)}) collective-permute-start(s32[16,16]{1,0:T(8,128)S(1)} %add.43), channel_id=1, source_target_pairs={{0,64},{16,80},{32,96},{48,112},{64,0},{80,16},{96,32},{112,48},{1... | collective-permute-start | bytes 3080 | tf_op jit(solution)/shard_map/ppermute | solution.py:260
  22.9 1.3 collective-permute-done.2
  24.2 0.4 collective-permute-start.3
  24.6 0.0 copy-done.2
  24.6 0.1 copy.12
  24.7 2.3 %collective-permute-done.3 = s32[16,16]{1,0:T(8,128)S(1)} collective-permute-done((s32[16,16]{1,0:T(8,128)S(1)}, s32[16,16]{1,0:T(8,128)S(1)}, u32[]{:S(2)}, u32[]{:S(2)}) %collective-permute-start.3) | collective-permute-done | bytes 1056 | tf_op jit(solution)/shard_map/ppermute | solution.py:260
  27.0 0.1 reshape.24
  27.1 37.7 %all-to-all-done.x_ref = bf16[16,2,8,4096]{3,2,1,0:T(8,128)(2,1)S(1)} async-done(((bf16[16,2,8,4096]{3,2,1,0:T(8,128)(2,1)}), bf16[16,2,8,4096]{3,2,1,0:T(8,128)(2,1)S(1)}, u32[]{:S(2)}, u32[]{:S(2)}) %all-to-all-start) | async-done | bytes 2097184 | tf_op jit(solution)/shard_map/all_to_all | solution.py:197
  64.7 0.0 copy-done.1
  64.7 3.4 %shard_map.93 = bf16[256,2,256]{2,1,0:T(2,128)(2,1)} custom-call(bf16[16,2,8,4096]{3,2,1,0:T(8,128)(2,1)S(1)} %all-to-all-done.x_ref, f32[4,128]{1,0:T(4,128)S(1)} %bitcast.17, bf16[128,256]{1,0:T(8,128)(2,1)S(1)} %bitcast.14), custom_call_target="tpu_custom_call" | custom-call | tf_op jit(solution)/shard_map/pallas_call | solution.py:55
  68.1 10.9 %all-to-all-start.1 = ((bf16[256,2,256]{2,1,0:T(2,128)(2,1)}), bf16[256,2,256]{2,1,0:T(2,128)(2,1)S(1)}, u32[]{:S(2)}, u32[]{:S(2)}) async-start(bf16[256,2,256]{2,1,0:T(2,128)(2,1)} %shard_map.93), calls=%async_computation.1 | async-start | bytes 524288 | tf_op jit(solution)/shard_map/all_to_all | solution.py:197
  79.1 0.1 copy.14.dw_ref
  79.2 4.9 %shard_map.94.terms_ref = f32[2,512,256]{2,1,0:T(8,128)S(1)} custom-call(bf16[16,2,8,4096]{3,2,1,0:T(8,128)(2,1)S(1)} %all-to-all-done.x_ref, f32[4,128]{1,0:T(4,128)S(1)} %bitcast.18, bf16[128,256]{1,0:T(8,128)(2,1)S(1)} %bitcast.15), custom_call_target="tpu_custom_call" | custom-call | tf_op jit(solution)/shard_map/pallas_call | solution.py:92
  84.1 0.1 copy.13.partner_ref
  84.2 10.5 %all-to-all-done.1 = bf16[256,2,256]{2,1,0:T(2,128)(2,1)S(1)} async-done(((bf16[256,2,256]{2,1,0:T(2,128)(2,1)}), bf16[256,2,256]{2,1,0:T(2,128)(2,1)S(1)}, u32[]{:S(2)}, u32[]{:S(2)}) %all-to-all-start.1) | async-done | bytes 262176 | tf_op jit(solution)/shard_map/all_to_all | solution.py:197
  94.7 0.0 copy-start
  94.7 1.0 copy-done
  95.8 2.6 %shard_map.95 = (f32[256,1]{1,0:T(8,128)S(1)}, bf16[256,1024]{1,0:T(8,128)(2,1)S(1)}, bf16[256,1024]{1,0:T(8,128)(2,1)S(1)}, f32[16,1,2176]{2,1,0:T(1,128)S(1)}) custom-call(s32[1]{0:T(128)} %bitcast.own_ref, bf16[256,512]{1,0:T(8,128)(2,1)S(1)} %bitcast.11, s32[256,1]{1,0:T(8,128)S(1)} %copy.13.partner_ref, bf16[256,1024]{1,0:T(8,128)(2,1)S(1)} %copy-done, ...), custom_call_target="tpu_custom_call" | custom-call | tf_op jit(solution)/shard_map/pallas_call | solution.py:181
  98.4 9.4 %all_to_all.25.parts_ref = f32[16,1,2176]{2,1,0:T(1,128)S(1)} all-to-all(f32[16,1,2176]{2,1,0:T(1,128)S(1)} %get-tuple-element.15), channel_id=1, replica_groups=mesh['dp'=16,'chan'=16] {'dp'}, dimensions={0} | all-to-all | bytes 278528 | tf_op jit(solution)/shard_map/all_to_all | solution.py:197
  107.8 0.8 shard_map.96
  108.5 3.5 %all-to-all-start.3 = ((f32[16,1,2176]{2,1,0:T(1,128)}), f32[16,1,2176]{2,1,0:T(1,128)S(1)}, u32[]{:S(2)}, u32[]{:S(2)}) async-start(f32[16,1,2176]{2,1,0:T(1,128)} %shard_map.96), calls=%async_computation.3 | async-start | bytes 278528 | tf_op jit(solution)/shard_map/all_to_all | solution.py:197
  112.1 0.6 dynamic-slice_reduce_fusion
  112.7 0.2 fusion.2
  112.9 8.0 %all-to-all-done.3.parts_ref = f32[16,1,2176]{2,1,0:T(1,128)S(1)} async-done(((f32[16,1,2176]{2,1,0:T(1,128)}), f32[16,1,2176]{2,1,0:T(1,128)S(1)}, u32[]{:S(2)}, u32[]{:S(2)}) %all-to-all-start.3) | async-done | bytes 139296 | tf_op jit(solution)/shard_map/all_to_all | solution.py:197
  121.0 0.8 shard_map.97
  121.7 5.1 %all-to-all-start.4 = ((f32[16,1,2176]{2,1,0:T(1,128)}), f32[16,1,2176]{2,1,0:T(1,128)S(1)}, u32[]{:S(2)}, u32[]{:S(2)}) async-start(f32[16,1,2176]{2,1,0:T(1,128)} %shard_map.97), calls=%async_computation.4 | async-start | bytes 278528 | tf_op jit(solution)/shard_map/all_to_all | solution.py:197
  126.8 0.8 convolution_add_fusion
  127.7 5.4 %all-to-all-done.4.shares_ref = f32[16,1,2176]{2,1,0:T(1,128)S(1)} async-done(((f32[16,1,2176]{2,1,0:T(1,128)}), f32[16,1,2176]{2,1,0:T(1,128)S(1)}, u32[]{:S(2)}, u32[]{:S(2)}) %all-to-all-start.4) | async-done | bytes 139296 | tf_op jit(solution)/shard_map/all_to_all | solution.py:197
  133.1 0.7 shard_map.98
  (8 shorter events, 0.1 us)
Async XLA Ops:
  3.7 11.9 %copy-start.3 = (s32[16]{0:T(128)S(1)}, s32[16]{0:T(128)}, u32[]{:S(2)}) copy-start(s32[16]{0:T(128)} %param.11) | copy-start | bytes 196
  3.7 20.9 %copy-start.2 = (bf16[256,128]{1,0:T(8,128)(2,1)S(1)}, bf16[256,128]{1,0:T(8,128)(2,1)}, u32[]{:S(2)}) copy-start(bf16[256,128]{1,0:T(8,128)(2,1)} %param.9) | copy-start | bytes 196612
  3.7 61.0 %copy-start.1 = (f32[128,4]{0,1:T(4,128)S(1)}, f32[128,4]{0,1:T(4,128)}, u32[]{:S(2)}) copy-start(f32[128,4]{0,1:T(4,128)} %param.8) | copy-start | bytes 6148
  3.7 61.0 %all-to-all-start = ((bf16[16,2,8,4096]{3,2,1,0:T(8,128)(2,1)}), bf16[16,2,8,4096]{3,2,1,0:T(8,128)(2,1)S(1)}, u32[]{:S(2)}, u32[]{:S(2)}) async-start(bf16[16,2,8,4096]{3,2,1,0:T(8,128)(2,1)} %pad_maximum_fusion), calls=%async_computation | async-start | bytes 4194304 | tf_op jit(solution)/shard_map/all_to_all | solution.py:197
  15.7 1.9 %collective-permute-start = (s32[16,16]{1,0:T(8,128)S(1)}, s32[16,16]{1,0:T(8,128)S(1)}, u32[]{:S(2)}, u32[]{:S(2)}) collective-permute-start(s32[16,16]{1,0:T(8,128)S(1)} %dynamic_update_slice.5), channel_id=1, source_target_pairs={{0,16},{16,0},{32,48},{48,32},{64,80},{80,64},{96,112},{112,96},{1... | collective-permute-start | bytes 3080 | tf_op jit(solution)/shard_map/ppermute | solution.py:260
  17.6 2.6 %collective-permute-start.1 = (s32[16,16]{1,0:T(8,128)S(1)}, s32[16,16]{1,0:T(8,128)S(1)}, u32[]{:S(2)}, u32[]{:S(2)}) collective-permute-start(s32[16,16]{1,0:T(8,128)S(1)} %add.42), channel_id=1, source_target_pairs={{0,32},{16,48},{32,0},{48,16},{64,96},{80,112},{96,64},{112,80},{1... | collective-permute-start | bytes 3080 | tf_op jit(solution)/shard_map/ppermute | solution.py:260
  20.1 4.0 %collective-permute-start.2 = (s32[16,16]{1,0:T(8,128)S(1)}, s32[16,16]{1,0:T(8,128)S(1)}, u32[]{:S(2)}, u32[]{:S(2)}) collective-permute-start(s32[16,16]{1,0:T(8,128)S(1)} %add.43), channel_id=1, source_target_pairs={{0,64},{16,80},{32,96},{48,112},{64,0},{80,16},{96,32},{112,48},{1... | collective-permute-start | bytes 3080 | tf_op jit(solution)/shard_map/ppermute | solution.py:260
  24.2 2.8 %collective-permute-start.3 = (s32[16,16]{1,0:T(8,128)S(1)}, s32[16,16]{1,0:T(8,128)S(1)}, u32[]{:S(2)}, u32[]{:S(2)}) collective-permute-start(s32[16,16]{1,0:T(8,128)S(1)} %add.44), channel_id=1, source_target_pairs={{0,128},{16,144},{32,160},{48,176},{64,192},{80,208},{96,224},{112... | collective-permute-start | bytes 3080 | tf_op jit(solution)/shard_map/ppermute | solution.py:260
  68.1 26.6 %all-to-all-start.1 = ((bf16[256,2,256]{2,1,0:T(2,128)(2,1)}), bf16[256,2,256]{2,1,0:T(2,128)(2,1)S(1)}, u32[]{:S(2)}, u32[]{:S(2)}) async-start(bf16[256,2,256]{2,1,0:T(2,128)(2,1)} %shard_map.93), calls=%async_computation.1 | async-start | bytes 524288 | tf_op jit(solution)/shard_map/all_to_all | solution.py:197
  94.7 1.0 copy-start
  108.5 12.4 %all-to-all-start.3 = ((f32[16,1,2176]{2,1,0:T(1,128)}), f32[16,1,2176]{2,1,0:T(1,128)S(1)}, u32[]{:S(2)}, u32[]{:S(2)}) async-start(f32[16,1,2176]{2,1,0:T(1,128)} %shard_map.96), calls=%async_computation.3 | async-start | bytes 278528 | tf_op jit(solution)/shard_map/all_to_all | solution.py:197
  121.7 11.3 %all-to-all-start.4 = ((f32[16,1,2176]{2,1,0:T(1,128)}), f32[16,1,2176]{2,1,0:T(1,128)S(1)}, u32[]{:S(2)}, u32[]{:S(2)}) async-start(f32[16,1,2176]{2,1,0:T(1,128)} %shard_map.97), calls=%async_computation.4 | async-start | bytes 278528 | tf_op jit(solution)/shard_map/all_to_all | solution.py:197

commit v6 on v5

--- a/solution.py
+++ b/solution.py
@@ -34,7 +34,7 @@
     half = pw_turned_ref[...] * 0.5
     rows = []
     for trace in range(pair):
-        held = turned
+        held = turned.at[trace]
         held[0:RIM, :] = jnp.zeros((RIM, sources * local), F32)
         total = jnp.zeros((SUBLANES, filters), F32)
         for begin in range(0, length, BLOCK):
@@ -57,7 +57,7 @@
         in_specs=[whole] * 3,
         out_specs=whole,
         out_shape=jax.ShapeDtypeStruct((devices, pair, filters), BF16),
-        scratch_shapes=[pltpu.VMEM((length + RIM, metrics), F32)],
+        scratch_shapes=[pltpu.VMEM((pair, length + RIM, metrics), F32)],
         compiler_params=pltpu.CompilerParams(vmem_limit_bytes=8 << 20),
     )(traces, dw_turned, pw_turned)
 
@@ -103,52 +103,58 @@
     )(traces, dw_turned, pw_turned)
 
 
-def middle_kernel(
+def normed(embedding):
+    inverse = lax.rsqrt(jnp.mean(embedding * embedding, 1, keepdims=True) + 1e-06)
+    return embedding * inverse, inverse
+
+
+def scored(queries, keys, partner, factor):
+    count = queries.shape[0]
+    logits = factor * lax.dot_general(
+        queries, keys, (((1,), (1,)), ((), ())), preferred_element_type=F32
+    )
+    columns = lax.broadcasted_iota(jnp.int32, (count, count), 1)
+    matches = columns == partner
+    weights = jnp.exp(logits - LOGIT_SCALE)
+    totals = jnp.sum(weights, 1, keepdims=True)
+    positive = jnp.sum(jnp.where(matches, logits, 0.0), 1, keepdims=True)
+    loss = LOGIT_SCALE + jnp.log(totals) - positive
+    return loss, (weights / totals - jnp.where(matches, 1.0, 0.0)).astype(BF16)
+
+
+def embed_grad(unit, inverse, unit_grad):
+    grad = inverse * (unit_grad - unit * jnp.mean(unit * unit_grad, 1, keepdims=True))
+    return grad.astype(BF16)
+
+
+def own_kernel(
     length, own_ref, pooled_ref, partner_ref, proj_ref, dw_ref, pw_turned_ref, terms_ref,
-    loss_ref, grad_a_ref, grad_v_ref, sums_ref, held_a, held_v,
+    loss_ref, sums_ref, embed_a, embed_v, coeff_rows, coeff_columns,
 ):
     filters, width = proj_ref.shape
-    count = pooled_ref.shape[0]
     metrics = pw_turned_ref.shape[0]
     factor = LOGIT_SCALE / width
     proj = proj_ref[...]
-
-    def normed(pooled):
-        embedding = jnp.dot(pooled, proj, preferred_element_type=F32)
-        inverse = lax.rsqrt(jnp.mean(embedding * embedding, 1, keepdims=True) + 1e-06)
-        return embedding * inverse, inverse
-
-    unit_a, inverse_a = normed(pooled_ref[:, 0:filters])
-    unit_v, inverse_v = normed(pooled_ref[:, filters : 2 * filters])
-    queries = unit_a.astype(BF16)
-    keys = unit_v.astype(BF16)
-    logits = factor * lax.dot_general(
-        queries, keys, (((1,), (1,)), ((), ())), preferred_element_type=F32
-    )
-    columns = lax.broadcasted_iota(jnp.int32, (count, count), 1)
-    matches = columns == partner_ref[...]
-    weights = jnp.exp(logits - LOGIT_SCALE)
-    totals = jnp.sum(weights, 1, keepdims=True)
-    positive = jnp.sum(jnp.where(matches, logits, 0.0), 1, keepdims=True)
-    loss_ref[...] = LOGIT_SCALE + jnp.log(totals) - positive
-    coeffs = (weights / totals - jnp.where(matches, 1.0, 0.0)).astype(BF16)
-    unit_grad_a = factor * jnp.dot(coeffs, keys, preferred_element_type=F32)
-    unit_grad_v = factor * lax.dot_general(
-        coeffs, queries, (((0,), (0,)), ((), ())), preferred_element_type=F32
-    )
+    embed_a[...] = jnp.dot(pooled_ref[:, 0:filters], proj, preferred_element_type=F32)
+    embed_v[...] = jnp.dot(pooled_ref[:, filters : 2 * filters], proj, preferred_element_type=F32)
+    queries = normed(embed_a[...])[0].astype(BF16)
+    keys = normed(embed_v[...])[0].astype(BF16)
+    loss, coeffs = scored(queries, keys, partner_ref[...], factor)
+    loss_ref[...] = loss
+    coeff_rows[...] = coeffs.astype(F32)
+    coeff_columns[...] = coeffs.astype(F32).T
     own = own_ref[0]
 
-    def pool_grad(unit, inverse, unit_grad, out_ref, held):
-        grad = inverse * (unit_grad - unit * jnp.mean(unit * unit_grad, 1, keepdims=True))
-        grad = grad.astype(BF16)
-        out_ref[...] = grad
-        held[...] = grad.astype(F32)
-        row = jnp.broadcast_to(held[pl.ds(own, 1), :], (16, width)).astype(BF16)
-        pool = lax.dot_general(row, proj, (((1,), (1,)), ((), ())), preferred_element_type=F32)
+    def pool_grad(coeff, others, embed):
+        row = jnp.broadcast_to(coeff[pl.ds(own, 1), :], (16, coeff.shape[1])).astype(BF16)
+        unit_grad = factor * jnp.dot(row, others, preferred_element_type=F32)
+        unit, inverse = normed(embed[pl.ds(own, 1), :])
+        grad = embed_grad(unit, inverse, unit_grad)
+        pool = lax.dot_general(grad, proj, (((1,), (1,)), ((), ())), preferred_element_type=F32)
         return pool[0:1, :] * (0.5 / length)
 
-    pool_a = pool_grad(unit_a, inverse_a, unit_grad_a, grad_a_ref, held_a)
-    pool_v = pool_grad(unit_v, inverse_v, unit_grad_v, grad_v_ref, held_v)
+    pool_a = pool_grad(coeff_rows, keys, embed_a)
+    pool_v = pool_grad(coeff_columns, queries, embed_v)
 
     pw_turned = pw_turned_ref[...].astype(F32)
     lanes = lax.broadcasted_iota(jnp.int32, (metrics, LANES), 1)
@@ -172,25 +178,61 @@
         sums_ref[part, 0:1, mix_rows * LANES :] = kernel[part : part + 1, :]
 
 
-def middle(own, pooled, partners, proj_weight, dw_weight, pw_turned, terms, parts, length):
+def own_pass(own, pooled, partners, proj_weight, dw_weight, pw_turned, terms, parts, length):
     filters, width = proj_weight.shape
     metrics = pw_turned.shape[0]
     count = pooled.shape[0]
     whole = pl.BlockSpec(memory_space=pltpu.VMEM)
     packed = (filters // parts + 1) * metrics
     return pl.pallas_call(
-        functools.partial(middle_kernel, length),
+        functools.partial(own_kernel, length),
         in_specs=[pl.BlockSpec(memory_space=pltpu.SMEM)] + [whole] * 6,
-        out_specs=[whole] * 4,
+        out_specs=[whole] * 2,
         out_shape=[
             jax.ShapeDtypeStruct((count, 1), F32),
-            jax.ShapeDtypeStruct((count, width), BF16),
-            jax.ShapeDtypeStruct((count, width), BF16),
             jax.ShapeDtypeStruct((parts, 1, packed), F32),
         ],
-        scratch_shapes=[pltpu.VMEM((count, width), F32), pltpu.VMEM((count, width), F32)],
-        compiler_params=pltpu.CompilerParams(vmem_limit_bytes=24 << 20),
+        scratch_shapes=[
+            pltpu.VMEM((count, width), F32),
+            pltpu.VMEM((count, width), F32),
+            pltpu.VMEM((count, count), F32),
+            pltpu.VMEM((count, count), F32),
+        ],
+        compiler_params=pltpu.CompilerParams(vmem_limit_bytes=20 << 20),
     )(own, pooled, partners, proj_weight, dw_weight, pw_turned, terms)
+
+
+def embed_kernel(pooled_ref, partner_ref, proj_ref, grad_a_ref, grad_v_ref):
+    filters, width = proj_ref.shape
+    factor = LOGIT_SCALE / width
+    proj = proj_ref[...]
+
+    def embedded(pooled):
+        return normed(jnp.dot(pooled, proj, preferred_element_type=F32))
+
+    unit_a, inverse_a = embedded(pooled_ref[:, 0:filters])
+    unit_v, inverse_v = embedded(pooled_ref[:, filters : 2 * filters])
+    queries = unit_a.astype(BF16)
+    keys = unit_v.astype(BF16)
+    _, coeffs = scored(queries, keys, partner_ref[...], factor)
+    unit_grad_a = factor * jnp.dot(coeffs, keys, preferred_element_type=F32)
+    unit_grad_v = factor * lax.dot_general(
+        coeffs, queries, (((0,), (0,)), ((), ())), preferred_element_type=F32
+    )
+    grad_a_ref[...] = embed_grad(unit_a, inverse_a, unit_grad_a)
+    grad_v_ref[...] = embed_grad(unit_v, inverse_v, unit_grad_v)
+
+
+def embed_pass(pooled, partners, proj_weight):
+    whole = pl.BlockSpec(memory_space=pltpu.VMEM)
+    shape = jax.ShapeDtypeStruct((pooled.shape[0], proj_weight.shape[1]), BF16)
+    return pl.pallas_call(
+        embed_kernel,
+        in_specs=[whole] * 3,
+        out_specs=[whole] * 2,
+        out_shape=[shape, shape],
+        compiler_params=pltpu.CompilerParams(vmem_limit_bytes=20 << 20),
+    )(pooled, partners, proj_weight)
 
 
 def swap(value, axis):
@@ -266,9 +308,10 @@
     pooled = swap(message, ("dp", "chan")).reshape(message.shape[0], -1)
     terms = terms_pass(traces, dw_turned, pw_turned)
     own = (dp_index * chan_count + chan_index).astype(jnp.int32).reshape(1)
-    losses, grad_a, grad_v, sums = middle(
+    losses, sums = own_pass(
         own, pooled, partners, proj_weight, dw_weight, pw_turned, terms, dp_count, length
     )
+    grad_a, grad_v = embed_pass(pooled, partners, proj_weight)
 
     shares = fold(swap(sums, "dp"), chan_count)
     shares = fold(swap(shares, "chan"), dp_count)

time: 134 us -> 134 us (level)
  waiting for transfers between devices: 67.2 us -> 65.4 us
  Pallas kernels: 13.1 us -> 14.5 us
    all_to_all x4, waiting for transfers between devices: 61.5 us -> 59.7 us  [swap(): return lax.all_to_all(value, axis, 0, 0, tiled=True)]
    pallas_call x1 -> x2, Pallas kernels: 2.63 us -> 4.05 us  [the longest x1 2.21 us: own_pass(): pl.pallas_call(functools.partial(own_kernel, length), in_specs=[pl.BlockS...]
  transfers between devices with their start and end apart: 8 -> 8, of which waited for: 8 -> 8; matrix products, arithmetic and copies ran while one was open for 2% -> 2% of each run, Pallas kernels for 4% -> 5%
where the time goes in v6:
time: 134 us; the launch traced here: 133 us
  waiting for transfers between devices  65.4 us (49%)
  starting transfers between devices  36.9 us (28%)
  Pallas kernels  14.5 us (11%)
  blocking collectives  9.37 us (7%)
  other arithmetic  3.1 us (2%)
  local copies, waits for them, and re-layouts  2.22 us (2%)
    all_to_all x4, waiting for transfers between devices, swap(): return lax.all_to_all(value, axis, 0, 0, tiled=True)  59.7 us
    all_to_all x4, starting transfers between devices, swap(): return lax.all_to_all(value, axis, 0, 0, tiled=True)  31.4 us
    all_to_all x1, blocking collectives, swap(): return lax.all_to_all(value, axis, 0, 0, tiled=True)  9.37 us
    ppermute x4, waiting for transfers between devices, body(): lax.ppermute(partners, 'dp', [(i, i ^ bit) for i in range(dp_count)])  5.68 us
    ppermute x4, starting transfers between devices, body(): lax.ppermute(partners, 'dp', [(i, i ^ bit) for i in range(dp_count)])  5.47 us
    pallas_call x1, Pallas kernels, terms_pass(): pl.pallas_call(terms_kernel, in_specs=[whole] * 3, out_specs=whole, out_s...  4.87 us
    pallas_call x1, Pallas kernels, pool_pass(): pl.pallas_call(pool_kernel, in_specs=[whole] * 3, out_specs=whole, out_sh...  3.39 us
    another operation x1, other arithmetic, body(): traces = swap(jnp.stack([anchors, views], 1), 'chan')  3.08 us
  transfers between devices with their start and end apart: 8, of which 8 were waited for; matrix products, arithmetic and copies ran while one was open for 2% of the time, Pallas kernels for 5%

profile of v6, /device:TPU:1, one launch (start us, length us, event | category | flops | bytes accessed | tf_op | source)
XLA Modules:
  0.0 133.3 jit_solution(3466525493073883118)
XLA Ops:
  0.6 3.1 %pad_maximum_fusion = bf16[16,2,8,4096]{3,2,1,0:T(8,128)(2,1)} fusion(bf16[16,1,8,4096]{3,2,1,0:T(8,128)(2,1)} %bitcast.21, bf16[16,1,8,4096]{3,2,1,0:T(8,128)(2,1)} %bitcast.22), kind=kLoop, calls=%fused_computation | loop fusion | flops 1048576 | bytes 4194304 | tf_op jit(solution)/shard_map/stack | solution.py:305
  3.7 0.0 copy-start.4
  3.7 0.0 copy-start.3
  3.7 0.0 copy-start.2
  3.7 11.9 %all-to-all-start = ((bf16[16,2,8,4096]{3,2,1,0:T(8,128)(2,1)}), bf16[16,2,8,4096]{3,2,1,0:T(8,128)(2,1)S(1)}, u32[]{:S(2)}, u32[]{:S(2)}) async-start(bf16[16,2,8,4096]{3,2,1,0:T(8,128)(2,1)} %pad_maximum_fusion), calls=%async_computation | async-start | bytes 4194304 | tf_op jit(solution)/shard_map/all_to_all | solution.py:239
  15.6 0.0 copy-done.4
  15.7 1.0 collective-permute-start
  16.7 0.8 collective-permute-done
  17.6 1.3 collective-permute-start.1
  18.9 1.3 collective-permute-done.1
  20.2 2.7 %collective-permute-start.2 = (s32[16,16]{1,0:T(8,128)S(1)}, s32[16,16]{1,0:T(8,128)S(1)}, u32[]{:S(2)}, u32[]{:S(2)}) collective-permute-start(s32[16,16]{1,0:T(8,128)S(1)} %add.43), channel_id=1, source_target_pairs={{0,64},{16,80},{32,96},{48,112},{64,0},{80,16},{96,32},{112,48},{1... | collective-permute-start | bytes 3080 | tf_op jit(solution)/shard_map/ppermute | solution.py:302
  22.9 1.3 collective-permute-done.2
  24.2 0.4 collective-permute-start.3
  24.6 0.0 copy-done.3
  24.6 0.1 copy.12
  24.7 2.3 %collective-permute-done.3 = s32[16,16]{1,0:T(8,128)S(1)} collective-permute-done((s32[16,16]{1,0:T(8,128)S(1)}, s32[16,16]{1,0:T(8,128)S(1)}, u32[]{:S(2)}, u32[]{:S(2)}) %collective-permute-start.3) | collective-permute-done | bytes 1056 | tf_op jit(solution)/shard_map/ppermute | solution.py:302
  27.0 0.1 reshape.24
  27.1 37.7 %all-to-all-done.x_ref = bf16[16,2,8,4096]{3,2,1,0:T(8,128)(2,1)S(1)} async-done(((bf16[16,2,8,4096]{3,2,1,0:T(8,128)(2,1)}), bf16[16,2,8,4096]{3,2,1,0:T(8,128)(2,1)S(1)}, u32[]{:S(2)}, u32[]{:S(2)}) %all-to-all-start) | async-done | bytes 2097184 | tf_op jit(solution)/shard_map/all_to_all | solution.py:239
  64.7 0.0 copy-done.2
  64.7 3.4 %shard_map.93 = bf16[256,2,256]{2,1,0:T(2,128)(2,1)} custom-call(bf16[16,2,8,4096]{3,2,1,0:T(8,128)(2,1)S(1)} %all-to-all-done.x_ref, f32[4,128]{1,0:T(4,128)S(1)} %bitcast.18, bf16[128,256]{1,0:T(8,128)(2,1)S(1)} %bitcast.15), custom_call_target="tpu_custom_call" | custom-call | tf_op jit(solution)/shard_map/pallas_call | solution.py:55
  68.1 10.9 %all-to-all-start.1 = ((bf16[256,2,256]{2,1,0:T(2,128)(2,1)}), bf16[256,2,256]{2,1,0:T(2,128)(2,1)S(1)}, u32[]{:S(2)}, u32[]{:S(2)}) async-start(bf16[256,2,256]{2,1,0:T(2,128)(2,1)} %shard_map.93), calls=%async_computation.1 | async-start | bytes 524288 | tf_op jit(solution)/shard_map/all_to_all | solution.py:239
  79.1 0.1 copy.14.dw_ref
  79.2 4.9 %shard_map.94.terms_ref = f32[2,512,256]{2,1,0:T(8,128)S(1)} custom-call(bf16[16,2,8,4096]{3,2,1,0:T(8,128)(2,1)S(1)} %all-to-all-done.x_ref, f32[4,128]{1,0:T(4,128)S(1)} %bitcast.19, bf16[128,256]{1,0:T(8,128)(2,1)S(1)} %bitcast.16), custom_call_target="tpu_custom_call" | custom-call | tf_op jit(solution)/shard_map/pallas_call | solution.py:92
  84.1 0.0 copy-start.1
  84.1 0.1 copy.13.partner_ref
  84.2 10.5 %all-to-all-done.1 = bf16[256,2,256]{2,1,0:T(2,128)(2,1)S(1)} async-done(((bf16[256,2,256]{2,1,0:T(2,128)(2,1)}), bf16[256,2,256]{2,1,0:T(2,128)(2,1)S(1)}, u32[]{:S(2)}, u32[]{:S(2)}) %all-to-all-start.1) | async-done | bytes 262176 | tf_op jit(solution)/shard_map/all_to_all | solution.py:239
  94.7 0.0 copy-start
  94.7 1.0 copy-done
  95.8 2.2 %shard_map.95 = (f32[256,1]{1,0:T(8,128)S(1)}, f32[16,1,2176]{2,1,0:T(1,128)S(1)}) custom-call(s32[1]{0:T(128)} %bitcast.own_ref, bf16[256,512]{1,0:T(8,128)(2,1)S(1)} %bitcast.11, s32[256,1]{1,0:T(8,128)S(1)} %copy.13.partner_ref, bf16[256,1024]{1,0:T(8,128)(2,1)S(1)} %copy-done, f32[128,4]{1,0:T(8,128)S(1)} %copy.14.dw_ref, bf16[128,256]{1,0:T(8,128)(2,1)S(1)} %bitcast.17, ...), custom_call_target="tpu_custom_call" | custom-call | tf_op jit(solution)/shard_map/pallas_call | solution.py:187
  98.0 9.4 %all_to_all.25.parts_ref = f32[16,1,2176]{2,1,0:T(1,128)S(1)} all-to-all(f32[16,1,2176]{2,1,0:T(1,128)S(1)} %get-tuple-element.15), channel_id=1, replica_groups=mesh['dp'=16,'chan'=16] {'dp'}, dimensions={0} | all-to-all | bytes 278528 | tf_op jit(solution)/shard_map/all_to_all | solution.py:239
  107.4 0.8 shard_map.96
  108.1 3.5 %all-to-all-start.3 = ((f32[16,1,2176]{2,1,0:T(1,128)}), f32[16,1,2176]{2,1,0:T(1,128)S(1)}, u32[]{:S(2)}, u32[]{:S(2)}) async-start(f32[16,1,2176]{2,1,0:T(1,128)} %shard_map.96), calls=%async_computation.3 | async-start | bytes 278528 | tf_op jit(solution)/shard_map/all_to_all | solution.py:239
  111.6 0.0 copy-done.1
  111.7 1.8 %shard_map.99 = (bf16[256,1024]{1,0:T(8,128)(2,1)S(1)}, bf16[256,1024]{1,0:T(8,128)(2,1)S(1)}) custom-call(bf16[256,512]{1,0:T(8,128)(2,1)S(1)} %bitcast.12, s32[256,1]{1,0:T(8,128)S(1)} %copy.13.partner_ref, bf16[256,1024]{1,0:T(8,128)(2,1)S(1)} %copy-done.1), custom_call_target="tpu_custom_call" | custom-call | tf_op jit(solution)/shard_map/pallas_call | solution.py:229
  113.5 0.6 dynamic-slice_reduce_fusion
  114.1 0.2 fusion.2
  114.4 6.2 %all-to-all-done.3.parts_ref = f32[16,1,2176]{2,1,0:T(1,128)S(1)} async-done(((f32[16,1,2176]{2,1,0:T(1,128)}), f32[16,1,2176]{2,1,0:T(1,128)S(1)}, u32[]{:S(2)}, u32[]{:S(2)}) %all-to-all-start.3) | async-done | bytes 139296 | tf_op jit(solution)/shard_map/all_to_all | solution.py:239
  120.5 0.8 shard_map.97
  121.3 5.1 %all-to-all-start.4 = ((f32[16,1,2176]{2,1,0:T(1,128)}), f32[16,1,2176]{2,1,0:T(1,128)S(1)}, u32[]{:S(2)}, u32[]{:S(2)}) async-start(f32[16,1,2176]{2,1,0:T(1,128)} %shard_map.97), calls=%async_computation.4 | async-start | bytes 278528 | tf_op jit(solution)/shard_map/all_to_all | solution.py:239
  126.4 0.8 convolution_add_fusion
  127.3 5.4 %all-to-all-done.4.shares_ref = f32[16,1,2176]{2,1,0:T(1,128)S(1)} async-done(((f32[16,1,2176]{2,1,0:T(1,128)}), f32[16,1,2176]{2,1,0:T(1,128)S(1)}, u32[]{:S(2)}, u32[]{:S(2)}) %all-to-all-start.4) | async-done | bytes 139296 | tf_op jit(solution)/shard_map/all_to_all | solution.py:239
  132.7 0.7 shard_map.98
  (8 shorter events, 0.1 us)
Async XLA Ops:
  3.7 11.9 %copy-start.4 = (s32[16]{0:T(128)S(1)}, s32[16]{0:T(128)}, u32[]{:S(2)}) copy-start(s32[16]{0:T(128)} %param.11) | copy-start | bytes 196
  3.7 20.9 %copy-start.3 = (bf16[256,128]{1,0:T(8,128)(2,1)S(1)}, bf16[256,128]{1,0:T(8,128)(2,1)}, u32[]{:S(2)}) copy-start(bf16[256,128]{1,0:T(8,128)(2,1)} %param.9) | copy-start | bytes 196612
  3.7 61.0 %copy-start.2 = (f32[128,4]{0,1:T(4,128)S(1)}, f32[128,4]{0,1:T(4,128)}, u32[]{:S(2)}) copy-start(f32[128,4]{0,1:T(4,128)} %param.8) | copy-start | bytes 6148
  3.7 61.0 %all-to-all-start = ((bf16[16,2,8,4096]{3,2,1,0:T(8,128)(2,1)}), bf16[16,2,8,4096]{3,2,1,0:T(8,128)(2,1)S(1)}, u32[]{:S(2)}, u32[]{:S(2)}) async-start(bf16[16,2,8,4096]{3,2,1,0:T(8,128)(2,1)} %pad_maximum_fusion), calls=%async_computation | async-start | bytes 4194304 | tf_op jit(solution)/shard_map/all_to_all | solution.py:239
  15.7 1.9 %collective-permute-start = (s32[16,16]{1,0:T(8,128)S(1)}, s32[16,16]{1,0:T(8,128)S(1)}, u32[]{:S(2)}, u32[]{:S(2)}) collective-permute-start(s32[16,16]{1,0:T(8,128)S(1)} %dynamic_update_slice.5), channel_id=1, source_target_pairs={{0,16},{16,0},{32,48},{48,32},{64,80},{80,64},{96,112},{112,96},{1... | collective-permute-start | bytes 3080 | tf_op jit(solution)/shard_map/ppermute | solution.py:302
  17.6 2.6 %collective-permute-start.1 = (s32[16,16]{1,0:T(8,128)S(1)}, s32[16,16]{1,0:T(8,128)S(1)}, u32[]{:S(2)}, u32[]{:S(2)}) collective-permute-start(s32[16,16]{1,0:T(8,128)S(1)} %add.42), channel_id=1, source_target_pairs={{0,32},{16,48},{32,0},{48,16},{64,96},{80,112},{96,64},{112,80},{1... | collective-permute-start | bytes 3080 | tf_op jit(solution)/shard_map/ppermute | solution.py:302
  20.2 4.0 %collective-permute-start.2 = (s32[16,16]{1,0:T(8,128)S(1)}, s32[16,16]{1,0:T(8,128)S(1)}, u32[]{:S(2)}, u32[]{:S(2)}) collective-permute-start(s32[16,16]{1,0:T(8,128)S(1)} %add.43), channel_id=1, source_target_pairs={{0,64},{16,80},{32,96},{48,112},{64,0},{80,16},{96,32},{112,48},{1... | collective-permute-start | bytes 3080 | tf_op jit(solution)/shard_map/ppermute | solution.py:302
  24.2 2.8 %collective-permute-start.3 = (s32[16,16]{1,0:T(8,128)S(1)}, s32[16,16]{1,0:T(8,128)S(1)}, u32[]{:S(2)}, u32[]{:S(2)}) collective-permute-start(s32[16,16]{1,0:T(8,128)S(1)} %add.44), channel_id=1, source_target_pairs={{0,128},{16,144},{32,160},{48,176},{64,192},{80,208},{96,224},{112... | collective-permute-start | bytes 3080 | tf_op jit(solution)/shard_map/ppermute | solution.py:302
  68.1 26.6 %all-to-all-start.1 = ((bf16[256,2,256]{2,1,0:T(2,128)(2,1)}), bf16[256,2,256]{2,1,0:T(2,128)(2,1)S(1)}, u32[]{:S(2)}, u32[]{:S(2)}) async-start(bf16[256,2,256]{2,1,0:T(2,128)(2,1)} %shard_map.93), calls=%async_computation.1 | async-start | bytes 524288 | tf_op jit(solution)/shard_map/all_to_all | solution.py:239
  84.1 27.6 %copy-start.1 = (bf16[256,1024]{1,0:T(8,128)(2,1)S(1)}, bf16[256,1024]{1,0:T(8,128)(2,1)}, u32[]{:S(2)}) copy-start(bf16[256,1024]{1,0:T(8,128)(2,1)} %proj_ref.3) | copy-start | bytes 1572868
  94.7 1.0 copy-start
  108.1 12.4 %all-to-all-start.3 = ((f32[16,1,2176]{2,1,0:T(1,128)}), f32[16,1,2176]{2,1,0:T(1,128)S(1)}, u32[]{:S(2)}, u32[]{:S(2)}) async-start(f32[16,1,2176]{2,1,0:T(1,128)} %shard_map.96), calls=%async_computation.3 | async-start | bytes 278528 | tf_op jit(solution)/shard_map/all_to_all | solution.py:239
  121.3 11.3 %all-to-all-start.4 = ((f32[16,1,2176]{2,1,0:T(1,128)}), f32[16,1,2176]{2,1,0:T(1,128)S(1)}, u32[]{:S(2)}, u32[]{:S(2)}) async-start(f32[16,1,2176]{2,1,0:T(1,128)} %shard_map.97), calls=%async_computation.4 | async-start | bytes 278528 | tf_op jit(solution)/shard_map/all_to_all | solution.py:239

commit v7 on v5

--- a/solution.py
+++ b/solution.py
@@ -34,7 +34,7 @@
     half = pw_turned_ref[...] * 0.5
     rows = []
     for trace in range(pair):
-        held = turned
+        held = turned.at[trace]
         held[0:RIM, :] = jnp.zeros((RIM, sources * local), F32)
         total = jnp.zeros((SUBLANES, filters), F32)
         for begin in range(0, length, BLOCK):
@@ -57,7 +57,7 @@
         in_specs=[whole] * 3,
         out_specs=whole,
         out_shape=jax.ShapeDtypeStruct((devices, pair, filters), BF16),
-        scratch_shapes=[pltpu.VMEM((length + RIM, metrics), F32)],
+        scratch_shapes=[pltpu.VMEM((pair, length + RIM, metrics), F32)],
         compiler_params=pltpu.CompilerParams(vmem_limit_bytes=8 << 20),
     )(traces, dw_turned, pw_turned)
 
@@ -105,7 +105,7 @@
 
 def middle_kernel(
     length, own_ref, pooled_ref, partner_ref, proj_ref, dw_ref, pw_turned_ref, terms_ref,
-    loss_ref, grad_a_ref, grad_v_ref, sums_ref, held_a, held_v,
+    loss_ref, grad_proj_ref, sums_ref, losses, held_a, held_v,
 ):
     filters, width = proj_ref.shape
     count = pooled_ref.shape[0]
@@ -130,7 +130,10 @@
     weights = jnp.exp(logits - LOGIT_SCALE)
     totals = jnp.sum(weights, 1, keepdims=True)
     positive = jnp.sum(jnp.where(matches, logits, 0.0), 1, keepdims=True)
-    loss_ref[...] = LOGIT_SCALE + jnp.log(totals) - positive
+    losses[...] = LOGIT_SCALE + jnp.log(totals) - positive
+    pairs = loss_ref.shape[1]
+    first = pl.multiple_of(own_ref[1] * pairs, SUBLANES)
+    loss_ref[...] = jnp.broadcast_to(losses[pl.ds(first, pairs), :], (pairs, LANES)).T[0:1, :]
     coeffs = (weights / totals - jnp.where(matches, 1.0, 0.0)).astype(BF16)
     unit_grad_a = factor * jnp.dot(coeffs, keys, preferred_element_type=F32)
     unit_grad_v = factor * lax.dot_general(
@@ -138,17 +141,34 @@
     )
     own = own_ref[0]
 
-    def pool_grad(unit, inverse, unit_grad, out_ref, held):
+    def pool_grad(unit, inverse, unit_grad, held):
         grad = inverse * (unit_grad - unit * jnp.mean(unit * unit_grad, 1, keepdims=True))
         grad = grad.astype(BF16)
-        out_ref[...] = grad
         held[...] = grad.astype(F32)
         row = jnp.broadcast_to(held[pl.ds(own, 1), :], (16, width)).astype(BF16)
         pool = lax.dot_general(row, proj, (((1,), (1,)), ((), ())), preferred_element_type=F32)
         return pool[0:1, :] * (0.5 / length)
 
-    pool_a = pool_grad(unit_a, inverse_a, unit_grad_a, grad_a_ref, held_a)
-    pool_v = pool_grad(unit_v, inverse_v, unit_grad_v, grad_v_ref, held_v)
+    pool_a = pool_grad(unit_a, inverse_a, unit_grad_a, held_a)
+    pool_v = pool_grad(unit_v, inverse_v, unit_grad_v, held_v)
+
+    proj_rows, proj_cols = grad_proj_ref.shape
+
+    def window(ref, begin, first, size):
+        lane = pl.multiple_of(begin + first // LANES * LANES, LANES)
+        block = ref[:, pl.ds(lane, LANES)].astype(F32)
+        return pltpu.roll(block, lax.rem(LANES - lax.rem(first, LANES), LANES), 1).astype(BF16)
+
+    def proj_part(begin, held):
+        return lax.dot_general(
+            window(pooled_ref, begin, own_ref[2] * proj_rows, proj_rows),
+            window(held, 0, own_ref[1] * proj_cols, proj_cols),
+            (((0,), (0,)), ((), ())),
+            preferred_element_type=F32,
+        )
+
+    grad_proj = proj_part(0, held_a) + proj_part(filters, held_v)
+    grad_proj_ref[...] = grad_proj[0:proj_rows, 0:proj_cols]
 
     pw_turned = pw_turned_ref[...].astype(F32)
     lanes = lax.broadcasted_iota(jnp.int32, (metrics, LANES), 1)
@@ -172,7 +192,7 @@
         sums_ref[part, 0:1, mix_rows * LANES :] = kernel[part : part + 1, :]
 
 
-def middle(own, pooled, partners, proj_weight, dw_weight, pw_turned, terms, parts, length):
+def middle(own, pooled, partners, proj_weight, dw_weight, pw_turned, terms, parts, others, length):
     filters, width = proj_weight.shape
     metrics = pw_turned.shape[0]
     count = pooled.shape[0]
@@ -181,14 +201,17 @@
     return pl.pallas_call(
         functools.partial(middle_kernel, length),
         in_specs=[pl.BlockSpec(memory_space=pltpu.SMEM)] + [whole] * 6,
-        out_specs=[whole] * 4,
+        out_specs=[whole] * 3,
         out_shape=[
-            jax.ShapeDtypeStruct((count, 1), F32),
-            jax.ShapeDtypeStruct((count, width), BF16),
-            jax.ShapeDtypeStruct((count, width), BF16),
+            jax.ShapeDtypeStruct((1, count // parts), F32),
+            jax.ShapeDtypeStruct((filters // others, width // parts), F32),
             jax.ShapeDtypeStruct((parts, 1, packed), F32),
         ],
-        scratch_shapes=[pltpu.VMEM((count, width), F32), pltpu.VMEM((count, width), F32)],
+        scratch_shapes=[
+            pltpu.VMEM((count, 1), F32),
+            pltpu.VMEM((count, width), F32),
+            pltpu.VMEM((count, width), F32),
+        ],
         compiler_params=pltpu.CompilerParams(vmem_limit_bytes=24 << 20),
     )(own, pooled, partners, proj_weight, dw_weight, pw_turned, terms)
 
@@ -265,28 +288,16 @@
     message = pool_pass(traces, dw_turned, pw_turned, dp_count * chan_count)
     pooled = swap(message, ("dp", "chan")).reshape(message.shape[0], -1)
     terms = terms_pass(traces, dw_turned, pw_turned)
-    own = (dp_index * chan_count + chan_index).astype(jnp.int32).reshape(1)
-    losses, grad_a, grad_v, sums = middle(
-        own, pooled, partners, proj_weight, dw_weight, pw_turned, terms, dp_count, length
+    own = jnp.stack([dp_index * chan_count + chan_index, dp_index, chan_index]).astype(jnp.int32)
+    loss, grad_proj, sums = middle(
+        own, pooled, partners, proj_weight, dw_weight, pw_turned, terms, dp_count, chan_count, length
     )
 
     shares = fold(swap(sums, "dp"), chan_count)
     shares = fold(swap(shares, "chan"), dp_count)
     grad_pw, grad_dw = unpack(chan_index, swap(shares, "dp"), filters, local_metrics)
 
-    cols = width // dp_count
-    rows = filters // chan_count
-
-    def proj_part(offset, grad):
-        features = lax.dynamic_slice_in_dim(pooled, offset + chan_index * rows, rows, 1)
-        part = lax.dynamic_slice_in_dim(grad, dp_index * cols, cols, 1)
-        return lax.dot_general(
-            features, part, (((0,), (0,)), ((), ())), preferred_element_type=F32
-        )
-
-    grad_proj = proj_part(0, grad_a) + proj_part(filters, grad_v)
-    loss = lax.dynamic_slice_in_dim(losses, dp_index * pairs, pairs, 0).reshape(pairs)
-    return (loss, grad_dw.T, grad_pw, grad_proj)
+    return (loss.reshape(pairs), grad_dw.T, grad_pw, grad_proj)
 
 
 def solution(mesh):

time: 134 us -> 133 us (level)
  blocking collectives: 9.37 us -> 32 us
  waiting for transfers between devices: 67.2 us -> 53.8 us
  starting transfers between devices: 36.9 us -> 28.3 us
    all_to_all x1 -> x3, blocking collectives: 9.37 us -> 32 us  [swap(): return lax.all_to_all(value, axis, 0, 0, tiled=True)]
    all_to_all x4 -> x2, waiting for transfers between devices: 61.5 us -> 48.1 us  [swap(): return lax.all_to_all(value, axis, 0, 0, tiled=True)]
    all_to_all x4 -> x2, starting transfers between devices: 31.4 us -> 22.8 us  [swap(): return lax.all_to_all(value, axis, 0, 0, tiled=True)]
  transfers between devices with their start and end apart: 8 -> 6, of which waited for: 8 -> 6; matrix products, arithmetic and copies ran while one was open for 2% -> 0% of each run, Pallas kernels for 4% -> 4%
where the time goes in v7:
time: 133 us; the launch traced here: 132 us
  waiting for transfers between devices  53.8 us (40%)
  blocking collectives  32 us (24%)
  starting transfers between devices  28.3 us (21%)
  Pallas kernels  12.8 us (10%)
  other arithmetic  3.15 us (2%)
  local copies, waits for them, and re-layouts  1.58 us (1%)
    all_to_all x2, waiting for transfers between devices, swap(): return lax.all_to_all(value, axis, 0, 0, tiled=True)  48.1 us
    all_to_all x3, blocking collectives, swap(): return lax.all_to_all(value, axis, 0, 0, tiled=True)  32 us
    all_to_all x2, starting transfers between devices, swap(): return lax.all_to_all(value, axis, 0, 0, tiled=True)  22.8 us
    ppermute x4, waiting for transfers between devices, body(): lax.ppermute(partners, 'dp', [(i, i ^ bit) for i in range(dp_count)])  5.68 us
    ppermute x4, starting transfers between devices, body(): lax.ppermute(partners, 'dp', [(i, i ^ bit) for i in range(dp_count)])  5.47 us
    pallas_call x1, Pallas kernels, terms_pass(): pl.pallas_call(terms_kernel, in_specs=[whole] * 3, out_specs=whole, out_s...  4.88 us
    pallas_call x1, Pallas kernels, middle(): pl.pallas_call(functools.partial(middle_kernel, length), in_specs=[pl.Blo...  3.68 us
    pallas_call x1, Pallas kernels, pool_pass(): pl.pallas_call(pool_kernel, in_specs=[whole] * 3, out_specs=whole, out_sh...  3.39 us
  transfers between devices with their start and end apart: 6, of which 6 were waited for; matrix products, arithmetic and copies ran while one was open for 0% of the time, Pallas kernels for 4%

profile of v7, /device:TPU:1, one launch (start us, length us, event | category | flops | bytes accessed | tf_op | source)
XLA Modules:
  0.0 132.3 jit_solution(14184234762355113057)
XLA Ops:
  0.6 3.1 %pad_maximum_fusion = bf16[16,2,8,4096]{3,2,1,0:T(8,128)(2,1)} fusion(bf16[16,1,8,4096]{3,2,1,0:T(8,128)(2,1)} %bitcast.20, bf16[16,1,8,4096]{3,2,1,0:T(8,128)(2,1)} %bitcast.21), kind=kLoop, calls=%fused_computation | loop fusion | flops 1048576 | bytes 4194304 | tf_op jit(solution)/shard_map/stack | solution.py:286
  3.7 0.0 copy-start.3
  3.7 0.0 copy-start.2
  3.7 0.0 copy-start.1
  3.7 11.9 %all-to-all-start = ((bf16[16,2,8,4096]{3,2,1,0:T(8,128)(2,1)}), bf16[16,2,8,4096]{3,2,1,0:T(8,128)(2,1)S(1)}, u32[]{:S(2)}, u32[]{:S(2)}) async-start(bf16[16,2,8,4096]{3,2,1,0:T(8,128)(2,1)} %pad_maximum_fusion), calls=%async_computation | async-start | bytes 4194304 | tf_op jit(solution)/shard_map/all_to_all | solution.py:220
  15.6 0.0 copy-done.3
  15.7 1.0 collective-permute-start
  16.7 0.8 collective-permute-done
  17.6 1.3 collective-permute-start.1
  18.8 1.3 collective-permute-done.1
  20.1 2.7 %collective-permute-start.2 = (s32[16,16]{1,0:T(8,128)S(1)}, s32[16,16]{1,0:T(8,128)S(1)}, u32[]{:S(2)}, u32[]{:S(2)}) collective-permute-start(s32[16,16]{1,0:T(8,128)S(1)} %add.22), channel_id=1, source_target_pairs={{0,64},{16,80},{32,96},{48,112},{64,0},{80,16},{96,32},{112,48},{1... | collective-permute-start | bytes 3080 | tf_op jit(solution)/shard_map/ppermute | solution.py:283
  22.9 1.3 collective-permute-done.2
  24.2 0.4 collective-permute-start.3
  24.5 0.0 copy-done.2
  24.6 0.1 copy.12
  24.7 2.3 %collective-permute-done.3 = s32[16,16]{1,0:T(8,128)S(1)} collective-permute-done((s32[16,16]{1,0:T(8,128)S(1)}, s32[16,16]{1,0:T(8,128)S(1)}, u32[]{:S(2)}, u32[]{:S(2)}) %collective-permute-start.3) | collective-permute-done | bytes 1056 | tf_op jit(solution)/shard_map/ppermute | solution.py:283
  27.0 0.1 reshape.18
  27.1 37.7 %all-to-all-done.x_ref = bf16[16,2,8,4096]{3,2,1,0:T(8,128)(2,1)S(1)} async-done(((bf16[16,2,8,4096]{3,2,1,0:T(8,128)(2,1)}), bf16[16,2,8,4096]{3,2,1,0:T(8,128)(2,1)S(1)}, u32[]{:S(2)}, u32[]{:S(2)}) %all-to-all-start) | async-done | bytes 2097184 | tf_op jit(solution)/shard_map/all_to_all | solution.py:220
  64.7 0.0 copy-done.1
  64.7 3.4 %shard_map.93 = bf16[256,2,256]{2,1,0:T(2,128)(2,1)} custom-call(bf16[16,2,8,4096]{3,2,1,0:T(8,128)(2,1)S(1)} %all-to-all-done.x_ref, f32[4,128]{1,0:T(4,128)S(1)} %bitcast.17, bf16[128,256]{1,0:T(8,128)(2,1)S(1)} %bitcast.13), custom_call_target="tpu_custom_call" | custom-call | tf_op jit(solution)/shard_map/pallas_call | solution.py:55
  68.1 10.9 %all-to-all-start.1 = ((bf16[256,2,256]{2,1,0:T(2,128)(2,1)}), bf16[256,2,256]{2,1,0:T(2,128)(2,1)S(1)}, u32[]{:S(2)}, u32[]{:S(2)}) async-start(bf16[256,2,256]{2,1,0:T(2,128)(2,1)} %shard_map.93), calls=%async_computation.1 | async-start | bytes 524288 | tf_op jit(solution)/shard_map/all_to_all | solution.py:220
  79.1 0.1 copy.14.dw_ref
  79.2 0.1 pad_add_fusion.own_ref
  79.2 4.9 %shard_map.94.terms_ref = f32[2,512,256]{2,1,0:T(8,128)S(1)} custom-call(bf16[16,2,8,4096]{3,2,1,0:T(8,128)(2,1)S(1)} %all-to-all-done.x_ref, f32[4,128]{1,0:T(4,128)S(1)} %bitcast.18, bf16[128,256]{1,0:T(8,128)(2,1)S(1)} %bitcast.14), custom_call_target="tpu_custom_call" | custom-call | tf_op jit(solution)/shard_map/pallas_call | solution.py:92
  84.1 0.1 copy.13.partner_ref
  84.3 10.4 %all-to-all-done.1 = bf16[256,2,256]{2,1,0:T(2,128)(2,1)S(1)} async-done(((bf16[256,2,256]{2,1,0:T(2,128)(2,1)}), bf16[256,2,256]{2,1,0:T(2,128)(2,1)S(1)}, u32[]{:S(2)}, u32[]{:S(2)}) %all-to-all-start.1) | async-done | bytes 262176 | tf_op jit(solution)/shard_map/all_to_all | solution.py:220
  94.7 0.0 copy-start
  94.7 1.0 copy-done
  95.8 3.7 %shard_map.95 = (f32[1,16]{1,0:T(1,128)}, f32[16,64]{1,0:T(8,128)}, f32[16,1,2176]{2,1,0:T(1,128)S(1)}) custom-call(s32[3]{0:T(128)S(1)} %pad_add_fusion.own_ref, bf16[256,512]{1,0:T(8,128)(2,1)S(1)} %bitcast.16, s32[256,1]{1,0:T(8,128)S(1)} %copy.13.partner_ref, bf16[256,1024]{1,0:T(8,128)(2,1)S(1)} %copy-done, f32[128,4]{1,0:T(8,128)S(1)} %copy.14.dw_ref, ...), custom_call_target="tpu_custom_call" | custom-call | tf_op jit(solution)/shard_map/pallas_call | solution.py:201
  99.4 9.3 %all_to_all.25.parts_ref = f32[16,1,2176]{2,1,0:T(1,128)S(1)} all-to-all(f32[16,1,2176]{2,1,0:T(1,128)S(1)} %get-tuple-element.14), channel_id=1, replica_groups=mesh['dp'=16,'chan'=16] {'dp'}, dimensions={0} | all-to-all | bytes 278528 | tf_op jit(solution)/shard_map/all_to_all | solution.py:220
  108.8 0.1 shard_map.96
  108.9 11.9 %all_to_all.26.parts_ref = f32[16,1,2176]{2,1,0:T(1,128)S(1)} all-to-all(f32[16,1,2176]{2,1,0:T(1,128)S(1)} %shard_map.96), channel_id=1, replica_groups=mesh['dp'=16,'chan'=16] {'chan'}, dimensions={0} | all-to-all | bytes 278528 | tf_op jit(solution)/shard_map/all_to_all | solution.py:220
  120.8 0.1 shard_map.97
  120.9 10.8 %all_to_all.27.shares_ref = f32[16,1,2176]{2,1,0:T(1,128)S(1)} all-to-all(f32[16,1,2176]{2,1,0:T(1,128)S(1)} %shard_map.97), channel_id=1, replica_groups=mesh['dp'=16,'chan'=16] {'dp'}, dimensions={0} | all-to-all | bytes 278528 | tf_op jit(solution)/shard_map/all_to_all | solution.py:220
  131.6 0.7 shard_map.98
  (8 shorter events, 0.1 us)
Async XLA Ops:
  3.7 11.9 %copy-start.3 = (s32[16]{0:T(128)S(1)}, s32[16]{0:T(128)}, u32[]{:S(2)}) copy-start(s32[16]{0:T(128)} %param.11) | copy-start | bytes 196
  3.7 20.9 %copy-start.2 = (bf16[256,128]{1,0:T(8,128)(2,1)S(1)}, bf16[256,128]{1,0:T(8,128)(2,1)}, u32[]{:S(2)}) copy-start(bf16[256,128]{1,0:T(8,128)(2,1)} %param.9) | copy-start | bytes 196612
  3.7 61.0 %copy-start.1 = (f32[128,4]{0,1:T(4,128)S(1)}, f32[128,4]{0,1:T(4,128)}, u32[]{:S(2)}) copy-start(f32[128,4]{0,1:T(4,128)} %param.8) | copy-start | bytes 6148
  3.7 61.0 %all-to-all-start = ((bf16[16,2,8,4096]{3,2,1,0:T(8,128)(2,1)}), bf16[16,2,8,4096]{3,2,1,0:T(8,128)(2,1)S(1)}, u32[]{:S(2)}, u32[]{:S(2)}) async-start(bf16[16,2,8,4096]{3,2,1,0:T(8,128)(2,1)} %pad_maximum_fusion), calls=%async_computation | async-start | bytes 4194304 | tf_op jit(solution)/shard_map/all_to_all | solution.py:220
  15.7 1.9 %collective-permute-start = (s32[16,16]{1,0:T(8,128)S(1)}, s32[16,16]{1,0:T(8,128)S(1)}, u32[]{:S(2)}, u32[]{:S(2)}) collective-permute-start(s32[16,16]{1,0:T(8,128)S(1)} %dynamic_update_slice.5), channel_id=1, source_target_pairs={{0,16},{16,0},{32,48},{48,32},{64,80},{80,64},{96,112},{112,96},{1... | collective-permute-start | bytes 3080 | tf_op jit(solution)/shard_map/ppermute | solution.py:283
  17.6 2.6 %collective-permute-start.1 = (s32[16,16]{1,0:T(8,128)S(1)}, s32[16,16]{1,0:T(8,128)S(1)}, u32[]{:S(2)}, u32[]{:S(2)}) collective-permute-start(s32[16,16]{1,0:T(8,128)S(1)} %add.21), channel_id=1, source_target_pairs={{0,32},{16,48},{32,0},{48,16},{64,96},{80,112},{96,64},{112,80},{1... | collective-permute-start | bytes 3080 | tf_op jit(solution)/shard_map/ppermute | solution.py:283
  20.1 4.0 %collective-permute-start.2 = (s32[16,16]{1,0:T(8,128)S(1)}, s32[16,16]{1,0:T(8,128)S(1)}, u32[]{:S(2)}, u32[]{:S(2)}) collective-permute-start(s32[16,16]{1,0:T(8,128)S(1)} %add.22), channel_id=1, source_target_pairs={{0,64},{16,80},{32,96},{48,112},{64,0},{80,16},{96,32},{112,48},{1... | collective-permute-start | bytes 3080 | tf_op jit(solution)/shard_map/ppermute | solution.py:283
  24.2 2.8 %collective-permute-start.3 = (s32[16,16]{1,0:T(8,128)S(1)}, s32[16,16]{1,0:T(8,128)S(1)}, u32[]{:S(2)}, u32[]{:S(2)}) collective-permute-start(s32[16,16]{1,0:T(8,128)S(1)} %add.23), channel_id=1, source_target_pairs={{0,128},{16,144},{32,160},{48,176},{64,192},{80,208},{96,224},{112... | collective-permute-start | bytes 3080 | tf_op jit(solution)/shard_map/ppermute | solution.py:283
  68.1 26.6 %all-to-all-start.1 = ((bf16[256,2,256]{2,1,0:T(2,128)(2,1)}), bf16[256,2,256]{2,1,0:T(2,128)(2,1)S(1)}, u32[]{:S(2)}, u32[]{:S(2)}) async-start(bf16[256,2,256]{2,1,0:T(2,128)(2,1)} %shard_map.93), calls=%async_computation.1 | async-start | bytes 524288 | tf_op jit(solution)/shard_map/all_to_all | solution.py:220
  94.7 1.0 copy-start

commit v8 on v7

--- a/solution.py
+++ b/solution.py
@@ -290,7 +290,8 @@
     terms = terms_pass(traces, dw_turned, pw_turned)
     own = jnp.stack([dp_index * chan_count + chan_index, dp_index, chan_index]).astype(jnp.int32)
     loss, grad_proj, sums = middle(
-        own, pooled, partners, proj_weight, dw_weight, pw_turned, terms, dp_count, chan_count, length
+        own, pooled, partners, pltpu.with_memory_space_constraint(proj_weight, pltpu.HBM), dw_weight,
+        pw_turned, terms, dp_count, chan_count, length,
     )
 
     shares = fold(swap(sums, "dp"), chan_count)

time: 133 us -> 132 us (level)
  no operation moved by 1% of the time
where the time goes in v8:
time: 132 us
  waiting for transfers between devices  53.8 us (41%)
  blocking collectives  32 us (24%)
  starting transfers between devices  28.3 us (21%)
  Pallas kernels  13.3 us (10%)
  other arithmetic  3.16 us (2%)
    all_to_all x2, waiting for transfers between devices, swap(): return lax.all_to_all(value, axis, 0, 0, tiled=True)  48.1 us
    all_to_all x3, blocking collectives, swap(): return lax.all_to_all(value, axis, 0, 0, tiled=True)  32 us
    all_to_all x2, starting transfers between devices, swap(): return lax.all_to_all(value, axis, 0, 0, tiled=True)  22.8 us
    ppermute x4, waiting for transfers between devices, body(): lax.ppermute(partners, 'dp', [(i, i ^ bit) for i in range(dp_count)])  5.68 us
    ppermute x4, starting transfers between devices, body(): lax.ppermute(partners, 'dp', [(i, i ^ bit) for i in range(dp_count)])  5.47 us
    pallas_call x1, Pallas kernels, terms_pass(): pl.pallas_call(terms_kernel, in_specs=[whole] * 3, out_specs=whole, out_s...  4.87 us
    pallas_call x1, Pallas kernels, middle(): pl.pallas_call(functools.partial(middle_kernel, length), in_specs=[pl.Blo...  4.19 us
    pallas_call x1, Pallas kernels, pool_pass(): pl.pallas_call(pool_kernel, in_specs=[whole] * 3, out_specs=whole, out_sh...  3.41 us
  transfers between devices with their start and end apart: 6, of which 6 were waited for; matrix products, arithmetic and copies ran while one was open for 0% of the time, Pallas kernels for 4%

profile of v8, /device:TPU:1, one launch (start us, length us, event | category | flops | bytes accessed | tf_op | source)
XLA Modules:
  0.0 131.8 jit_solution(8458527281124734519)
XLA Ops:
  0.6 3.1 %pad_maximum_fusion = bf16[16,2,8,4096]{3,2,1,0:T(8,128)(2,1)} fusion(bf16[16,1,8,4096]{3,2,1,0:T(8,128)(2,1)} %bitcast.20, bf16[16,1,8,4096]{3,2,1,0:T(8,128)(2,1)} %bitcast.21), kind=kLoop, calls=%fused_computation | loop fusion | flops 1048576 | bytes 4194304 | tf_op jit(solution)/shard_map/stack | solution.py:286
  3.7 0.0 copy-start.2
  3.7 0.0 copy-start.1
  3.7 0.0 copy-start
  3.7 11.9 %all-to-all-start = ((bf16[16,2,8,4096]{3,2,1,0:T(8,128)(2,1)}), bf16[16,2,8,4096]{3,2,1,0:T(8,128)(2,1)S(1)}, u32[]{:S(2)}, u32[]{:S(2)}) async-start(bf16[16,2,8,4096]{3,2,1,0:T(8,128)(2,1)} %pad_maximum_fusion), calls=%async_computation | async-start | bytes 4194304 | tf_op jit(solution)/shard_map/all_to_all | solution.py:220
  15.6 0.0 copy-done.2
  15.7 1.0 collective-permute-start
  16.7 0.8 collective-permute-done
  17.6 1.3 collective-permute-start.1
  18.9 1.3 collective-permute-done.1
  20.1 2.7 %collective-permute-start.2 = (s32[16,16]{1,0:T(8,128)S(1)}, s32[16,16]{1,0:T(8,128)S(1)}, u32[]{:S(2)}, u32[]{:S(2)}) collective-permute-start(s32[16,16]{1,0:T(8,128)S(1)} %add.22), channel_id=1, source_target_pairs={{0,64},{16,80},{32,96},{48,112},{64,0},{80,16},{96,32},{112,48},{1... | collective-permute-start | bytes 3080 | tf_op jit(solution)/shard_map/ppermute | solution.py:283
  22.9 1.3 collective-permute-done.2
  24.2 0.4 collective-permute-start.3
  24.6 0.0 copy-done.1
  24.6 0.1 copy.12
  24.7 2.3 %collective-permute-done.3 = s32[16,16]{1,0:T(8,128)S(1)} collective-permute-done((s32[16,16]{1,0:T(8,128)S(1)}, s32[16,16]{1,0:T(8,128)S(1)}, u32[]{:S(2)}, u32[]{:S(2)}) %collective-permute-start.3) | collective-permute-done | bytes 1056 | tf_op jit(solution)/shard_map/ppermute | solution.py:283
  27.0 0.1 reshape.18
  27.1 37.7 %all-to-all-done.x_ref = bf16[16,2,8,4096]{3,2,1,0:T(8,128)(2,1)S(1)} async-done(((bf16[16,2,8,4096]{3,2,1,0:T(8,128)(2,1)}), bf16[16,2,8,4096]{3,2,1,0:T(8,128)(2,1)S(1)}, u32[]{:S(2)}, u32[]{:S(2)}) %all-to-all-start) | async-done | bytes 2097184 | tf_op jit(solution)/shard_map/all_to_all | solution.py:220
  64.7 0.0 copy-done
  64.7 3.4 %shard_map.93 = bf16[256,2,256]{2,1,0:T(2,128)(2,1)} custom-call(bf16[16,2,8,4096]{3,2,1,0:T(8,128)(2,1)S(1)} %all-to-all-done.x_ref, f32[4,128]{1,0:T(4,128)S(1)} %bitcast.17, bf16[128,256]{1,0:T(8,128)(2,1)S(1)} %bitcast.13), custom_call_target="tpu_custom_call" | custom-call | tf_op jit(solution)/shard_map/pallas_call | solution.py:55
  68.1 10.9 %all-to-all-start.1 = ((bf16[256,2,256]{2,1,0:T(2,128)(2,1)}), bf16[256,2,256]{2,1,0:T(2,128)(2,1)S(1)}, u32[]{:S(2)}, u32[]{:S(2)}) async-start(bf16[256,2,256]{2,1,0:T(2,128)(2,1)} %shard_map.93), calls=%async_computation.1 | async-start | bytes 524288 | tf_op jit(solution)/shard_map/all_to_all | solution.py:220
  79.1 0.1 copy.14.dw_ref
  79.2 0.1 pad_add_fusion.own_ref
  79.3 4.9 %shard_map.94.terms_ref = f32[2,512,256]{2,1,0:T(8,128)S(1)} custom-call(bf16[16,2,8,4096]{3,2,1,0:T(8,128)(2,1)S(1)} %all-to-all-done.x_ref, f32[4,128]{1,0:T(4,128)S(1)} %bitcast.18, bf16[128,256]{1,0:T(8,128)(2,1)S(1)} %bitcast.14), custom_call_target="tpu_custom_call" | custom-call | tf_op jit(solution)/shard_map/pallas_call | solution.py:92
  84.1 0.1 copy.13.partner_ref
  84.3 10.4 %all-to-all-done.1 = bf16[256,2,256]{2,1,0:T(2,128)(2,1)S(1)} async-done(((bf16[256,2,256]{2,1,0:T(2,128)(2,1)}), bf16[256,2,256]{2,1,0:T(2,128)(2,1)S(1)}, u32[]{:S(2)}, u32[]{:S(2)}) %all-to-all-start.1) | async-done | bytes 262176 | tf_op jit(solution)/shard_map/all_to_all | solution.py:220
  94.7 4.2 %shard_map.95 = (f32[1,16]{1,0:T(1,128)}, f32[16,64]{1,0:T(8,128)}, f32[16,1,2176]{2,1,0:T(1,128)S(1)}) custom-call(s32[3]{0:T(128)S(1)} %pad_add_fusion.own_ref, bf16[256,512]{1,0:T(8,128)(2,1)S(1)} %bitcast.16, s32[256,1]{1,0:T(8,128)S(1)} %copy.13.partner_ref, bf16[256,1024]{1,0:T(8,128)(2,1)} %proj_ref.1, f32[128,4]{1,0:T(8,128)S(1)} %copy.14.dw_ref, ...), custom_call_target="tpu_custom_call" | custom-call | tf_op jit(solution)/shard_map/pallas_call | solution.py:201
  98.9 9.4 %all_to_all.25.parts_ref = f32[16,1,2176]{2,1,0:T(1,128)S(1)} all-to-all(f32[16,1,2176]{2,1,0:T(1,128)S(1)} %get-tuple-element.14), channel_id=1, replica_groups=mesh['dp'=16,'chan'=16] {'dp'}, dimensions={0} | all-to-all | bytes 278528 | tf_op jit(solution)/shard_map/all_to_all | solution.py:220
  108.3 0.1 shard_map.96
  108.4 11.9 %all_to_all.26.parts_ref = f32[16,1,2176]{2,1,0:T(1,128)S(1)} all-to-all(f32[16,1,2176]{2,1,0:T(1,128)S(1)} %shard_map.96), channel_id=1, replica_groups=mesh['dp'=16,'chan'=16] {'chan'}, dimensions={0} | all-to-all | bytes 278528 | tf_op jit(solution)/shard_map/all_to_all | solution.py:220
  120.2 0.1 shard_map.97
  120.3 10.8 %all_to_all.27.shares_ref = f32[16,1,2176]{2,1,0:T(1,128)S(1)} all-to-all(f32[16,1,2176]{2,1,0:T(1,128)S(1)} %shard_map.97), channel_id=1, replica_groups=mesh['dp'=16,'chan'=16] {'dp'}, dimensions={0} | all-to-all | bytes 278528 | tf_op jit(solution)/shard_map/all_to_all | solution.py:220
  131.1 0.7 shard_map.98
  (8 shorter events, 0.1 us)
Async XLA Ops:
  3.7 11.9 %copy-start.2 = (s32[16]{0:T(128)S(1)}, s32[16]{0:T(128)}, u32[]{:S(2)}) copy-start(s32[16]{0:T(128)} %param.11) | copy-start | bytes 196
  3.7 20.9 %copy-start.1 = (bf16[256,128]{1,0:T(8,128)(2,1)S(1)}, bf16[256,128]{1,0:T(8,128)(2,1)}, u32[]{:S(2)}) copy-start(bf16[256,128]{1,0:T(8,128)(2,1)} %param.9) | copy-start | bytes 196612
  3.7 61.0 %copy-start = (f32[128,4]{0,1:T(4,128)S(1)}, f32[128,4]{0,1:T(4,128)}, u32[]{:S(2)}) copy-start(f32[128,4]{0,1:T(4,128)} %param.8) | copy-start | bytes 6148
  3.7 61.0 %all-to-all-start = ((bf16[16,2,8,4096]{3,2,1,0:T(8,128)(2,1)}), bf16[16,2,8,4096]{3,2,1,0:T(8,128)(2,1)S(1)}, u32[]{:S(2)}, u32[]{:S(2)}) async-start(bf16[16,2,8,4096]{3,2,1,0:T(8,128)(2,1)} %pad_maximum_fusion), calls=%async_computation | async-start | bytes 4194304 | tf_op jit(solution)/shard_map/all_to_all | solution.py:220
  15.7 1.9 %collective-permute-start = (s32[16,16]{1,0:T(8,128)S(1)}, s32[16,16]{1,0:T(8,128)S(1)}, u32[]{:S(2)}, u32[]{:S(2)}) collective-permute-start(s32[16,16]{1,0:T(8,128)S(1)} %dynamic_update_slice.5), channel_id=1, source_target_pairs={{0,16},{16,0},{32,48},{48,32},{64,80},{80,64},{96,112},{112,96},{1... | collective-permute-start | bytes 3080 | tf_op jit(solution)/shard_map/ppermute | solution.py:283
  17.6 2.6 %collective-permute-start.1 = (s32[16,16]{1,0:T(8,128)S(1)}, s32[16,16]{1,0:T(8,128)S(1)}, u32[]{:S(2)}, u32[]{:S(2)}) collective-permute-start(s32[16,16]{1,0:T(8,128)S(1)} %add.21), channel_id=1, source_target_pairs={{0,32},{16,48},{32,0},{48,16},{64,96},{80,112},{96,64},{112,80},{1... | collective-permute-start | bytes 3080 | tf_op jit(solution)/shard_map/ppermute | solution.py:283
  20.1 4.0 %collective-permute-start.2 = (s32[16,16]{1,0:T(8,128)S(1)}, s32[16,16]{1,0:T(8,128)S(1)}, u32[]{:S(2)}, u32[]{:S(2)}) collective-permute-start(s32[16,16]{1,0:T(8,128)S(1)} %add.22), channel_id=1, source_target_pairs={{0,64},{16,80},{32,96},{48,112},{64,0},{80,16},{96,32},{112,48},{1... | collective-permute-start | bytes 3080 | tf_op jit(solution)/shard_map/ppermute | solution.py:283
  24.2 2.8 %collective-permute-start.3 = (s32[16,16]{1,0:T(8,128)S(1)}, s32[16,16]{1,0:T(8,128)S(1)}, u32[]{:S(2)}, u32[]{:S(2)}) collective-permute-start(s32[16,16]{1,0:T(8,128)S(1)} %add.23), channel_id=1, source_target_pairs={{0,128},{16,144},{32,160},{48,176},{64,192},{80,208},{96,224},{112... | collective-permute-start | bytes 3080 | tf_op jit(solution)/shard_map/ppermute | solution.py:283
  68.1 26.6 %all-to-all-start.1 = ((bf16[256,2,256]{2,1,0:T(2,128)(2,1)}), bf16[256,2,256]{2,1,0:T(2,128)(2,1)S(1)}, u32[]{:S(2)}, u32[]{:S(2)}) async-start(bf16[256,2,256]{2,1,0:T(2,128)(2,1)} %shard_map.93), calls=%async_computation.1 | async-start | bytes 524288 | tf_op jit(solution)/shard_map/all_to_all | solution.py:220
